TPU v7x, 32 devices: a whole 2x2x4 slice. The times are simulated.
32 devices in a mesh: fsdp: 8 (over z, core), tp: 4 (over y, x).
Axes of the slice: x: 2, y: 2, z: 4, core: 2. Of those that a mesh axis runs over, the one named last changes fastest.
Arguments:
- layer_input: bfloat16 [8192, 2048], P(('fsdp', 'tp')), may hold values from -6 to 6
- cotangent: bfloat16 [8192, 2048], P(('fsdp', 'tp')), may hold values from -6 to 6
- segment_ids: int32 [8192], P('fsdp'), may hold values from 0 to 12, as said below
- path_positions: int32 [8192], P('fsdp'), may hold values from 0 to 383, as said below
- ancestor_masks: int32 [8, 13, 13], P('fsdp'), may hold values from 0 to 1, as said below
- attn_gain: bfloat16 [2048], P('fsdp'), may hold values from 0.5 to 1.5
- query_weight: bfloat16 [2048, 2048], P('fsdp', 'tp'), may hold values from -0.125 to 0.125
- key_weight: bfloat16 [2048, 512], P('fsdp', 'tp'), may hold values from -0.125 to 0.125
- value_weight: bfloat16 [2048, 512], P('fsdp', 'tp'), may hold values from -0.125 to 0.125
- out_weight: bfloat16 [2048, 2048], P('tp', 'fsdp'), may hold values from -1.5 to 1.5
- mlp_gain: bfloat16 [2048], P('fsdp'), may hold values from 0.5 to 1.5
- gate_weight: bfloat16 [2048, 8192], P('fsdp', 'tp'), may hold values from -0.125 to 0.125
- up_weight: bfloat16 [2048, 8192], P('fsdp', 'tp'), may hold values from -0.125 to 0.125
- down_weight: bfloat16 [8192, 2048], P('tp', 'fsdp'), may hold values from -0.0625 to 0.0625
Outputs:
- output: bfloat16 [8192, 2048], P(('fsdp', 'tp'))
- input_grad: float32 [8192, 2048], P(('fsdp', 'tp'))
- attn_gain_grad: float32 [2048], P('fsdp')
- query_grad: float32 [2048, 2048], P('fsdp', 'tp')
- key_grad: float32 [2048, 512], P('fsdp', 'tp')
- value_grad: float32 [2048, 512], P('fsdp', 'tp')
- out_grad: float32 [2048, 2048], P('tp', 'fsdp')
- mlp_gain_grad: float32 [2048], P('fsdp')
- gate_grad: float32 [2048, 8192], P('fsdp', 'tp')
- up_grad: float32 [2048, 8192], P('fsdp', 'tp')
- down_grad: float32 [8192, 2048], P('tp', 'fsdp')
Inputs may be any that keep to these rules, and one draw needn't show every extreme that they name: `segment_ids`: in each tree the trunk, segment 0, fills the first 256 rows; segments 1 to 4 are branches and the rest leaves, each filling one aligned run of 64 rows, in any order. `path_positions`: trunk rows count from 0; a branch's rows from 256, a leaf's from (5) * 64. `ancestor_masks`: the trunk is the parent of every branch, each branch the parent of two leaves; a segment counts as its own ancestor.
All inputs are finite; a program needn't handle non-finite values.
Results may differ from a plain program's by a relative error of at most 0.019.
Values may be sent and summed in bfloat16 or wider, within the bound.
A program may use at most 320 MiB of HBM per device.

v0:
```python
import math

import jax
import jax.numpy as jnp
import numpy as np
from jax import lax
from jax.sharding import PartitionSpec as P

HD = 64
SEGS = 13


EPSILON = 1e-05


def inverse_freq(head_size):
    base_freq = 1.0 / 500000.0 ** (np.arange(0, head_size, 2) / head_size)
    wavelen = 2.0 * math.pi / base_freq
    smooth = (8192.0 / wavelen - 1.0) / 3.0
    blended = (1.0 - smooth) * base_freq / 32.0 + smooth * base_freq
    scaled = np.where(
        wavelen > 8192.0, base_freq / 32.0, np.where(wavelen < 2048.0, base_freq, blended)
    )
    return scaled.astype(np.float32)


def rope_tables(positions, head_size):
    freqs = jnp.asarray(inverse_freq(head_size))
    angles = positions.astype(jnp.float32)[:, None] * freqs[None, :]
    angles = jnp.concatenate([angles, angles], axis=-1)
    return (jnp.cos(angles), jnp.sin(angles))


def rotate_half(values):
    half_size = values.shape[-1] // 2
    return jnp.concatenate([-values[..., half_size:], values[..., :half_size]], axis=-1)


def apply_rope(values, cosine_table, sine_table):
    return values * cosine_table[:, None, :] + rotate_half(values) * sine_table[:, None, :]


def rope_back(gradient, cosine_table, sine_table):
    return gradient * cosine_table[:, None, :] - rotate_half(gradient * sine_table[:, None, :])


def rms_scale(row_values):
    return lax.rsqrt(jnp.mean(row_values * row_values, axis=-1, keepdims=True) + EPSILON)


def norm_back(row_values, row_scale, gain_values, grad_out):
    scaled_grad = grad_out * gain_values
    gain_part = jnp.sum(grad_out * row_values * row_scale, axis=0)
    rows_grad = row_scale * scaled_grad - row_values * row_scale**3 * jnp.mean(
        scaled_grad * row_values, axis=-1, keepdims=True
    )
    return (rows_grad, gain_part)


def contract_rows(left, right):
    return lax.dot_general(
        left, right, (((0,), (0,)), ((), ())), preferred_element_type=jnp.float32
    )


def times_transposed(left, right):
    return lax.dot_general(
        left, right, (((1,), (1,)), ((), ())), preferred_element_type=jnp.float32
    )


def gather_rows(pieces):
    return lax.all_gather(pieces, "tp", axis=0, tiled=True)


def scatter_rows(partial_sums):
    return lax.psum_scatter(partial_sums, "tp", scatter_dimension=0, tiled=True)


def body(
    layer_input,
    cotangent,
    segment_ids,
    path_positions,
    ancestor_masks,
    attn_gain,
    query_weight,
    key_weight,
    value_weight,
    out_weight,
    mlp_gain,
    gate_weight,
    up_weight,
    down_weight,
):
    tree_len = segment_ids.shape[0]
    local_heads = query_weight.shape[1] // HD
    local_groups = key_weight.shape[1] // HD
    group_size = local_heads // local_groups
    score_scale = HD ** (-0.5)
    block_rows = min(512, tree_len)
    cosine_table, sine_table = rope_tables(path_positions, HD)
    segment_hot = (segment_ids[:, None] == jnp.arange(SEGS)[None, :]).astype(jnp.float32)
    ancestor_table = ancestor_masks[0].astype(jnp.float32)
    token_index = jnp.arange(tree_len)

    def allowed_block(row_start):
        hot_rows = segment_hot[row_start : row_start + block_rows]
        reach_rows = jnp.dot(hot_rows, ancestor_table, precision=lax.Precision.HIGHEST)
        reach = times_transposed(reach_rows, segment_hot)
        same_segment = times_transposed(hot_rows, segment_hot)
        causal = token_index[None, :] <= (row_start + jnp.arange(block_rows))[:, None]
        return (reach > 0.5) & ((same_segment < 0.5) | causal)

    query_full, key_full, value_full, gain_first = (
        lax.all_gather(query_weight, "fsdp", axis=0, tiled=True),
        lax.all_gather(key_weight, "fsdp", axis=0, tiled=True),
        lax.all_gather(value_weight, "fsdp", axis=0, tiled=True),
        lax.all_gather(attn_gain, "fsdp", axis=0, tiled=True),
    )
    input_rows = layer_input.astype(jnp.float32)
    first_scale = rms_scale(input_rows)
    first_gain = gain_first.astype(jnp.float32)
    first_normed = gather_rows((input_rows * first_scale * first_gain).astype(jnp.bfloat16))
    query_pre = jnp.dot(first_normed, query_full, preferred_element_type=jnp.float32)
    queries = apply_rope(
        query_pre.reshape(tree_len, local_heads, HD), cosine_table, sine_table
    ).astype(jnp.bfloat16)
    key_pre = jnp.dot(first_normed, key_full, preferred_element_type=jnp.float32)
    key_rows = apply_rope(
        key_pre.reshape(tree_len, local_groups, HD), cosine_table, sine_table
    ).astype(jnp.bfloat16)
    value_rows = (
        jnp.dot(first_normed, value_full, preferred_element_type=jnp.float32)
        .astype(jnp.bfloat16)
        .reshape(tree_len, local_groups, HD)
    )
    query_groups = queries.reshape(tree_len, local_groups, group_size, HD)
    attended_blocks = []
    lse_blocks = []
    for row_start in range(0, tree_len, block_rows):
        allowed = allowed_block(row_start)
        query_block = query_groups[row_start : row_start + block_rows]
        raw_scores = (
            jnp.einsum("qkgd,skd->kgqs", query_block, key_rows, preferred_element_type=jnp.float32)
            * score_scale
        )
        masked = jnp.where(allowed[None, None], raw_scores, -1e30)
        row_max = jnp.max(masked, axis=-1, keepdims=True)
        exponent = jnp.exp(masked - row_max)
        row_total = jnp.sum(exponent, axis=-1, keepdims=True)
        probs_low = (exponent / row_total).astype(jnp.bfloat16)
        mixture = jnp.einsum(
            "kgqs,skd->qkgd", probs_low, value_rows, preferred_element_type=jnp.float32
        )
        attended_blocks.append(mixture.astype(jnp.bfloat16).reshape(block_rows, local_heads * HD))
        lse_blocks.append(row_max + jnp.log(row_total))
    attended = jnp.concatenate(attended_blocks, axis=0)
    out_full = lax.all_gather(out_weight, "fsdp", axis=1, tiled=True)
    residual = input_rows + scatter_rows(
        jnp.dot(attended, out_full, preferred_element_type=jnp.float32)
    )
    gate_full, up_full, gain_second = (
        lax.all_gather(gate_weight, "fsdp", axis=0, tiled=True),
        lax.all_gather(up_weight, "fsdp", axis=0, tiled=True),
        lax.all_gather(mlp_gain, "fsdp", axis=0, tiled=True),
    )
    down_full = lax.all_gather(down_weight, "fsdp", axis=1, tiled=True)
    second_scale = rms_scale(residual)
    second_gain = gain_second.astype(jnp.float32)
    second_normed = gather_rows((residual * second_scale * second_gain).astype(jnp.bfloat16))
    gate_proj = jnp.dot(second_normed, gate_full, preferred_element_type=jnp.float32)
    up_proj = jnp.dot(second_normed, up_full, preferred_element_type=jnp.float32)
    sigmoid_gate = jax.nn.sigmoid(gate_proj)
    hidden = (gate_proj * sigmoid_gate * up_proj).astype(jnp.bfloat16)
    output_rows = residual + scatter_rows(
        jnp.dot(hidden, down_full, preferred_element_type=jnp.float32)
    )
    output = output_rows.astype(jnp.bfloat16)
    gate_used, up_used, down_used = (gate_full, up_full, down_full)
    cot_rows = cotangent.astype(jnp.float32)
    mlp_back = gather_rows(cotangent)
    hidden_back = times_transposed(mlp_back, down_used)
    down_grad = contract_rows(hidden, mlp_back)
    gate_back = (
        hidden_back * up_proj * sigmoid_gate * (1.0 + gate_proj * (1.0 - sigmoid_gate))
    ).astype(jnp.bfloat16)
    up_back = (hidden_back * gate_proj * sigmoid_gate).astype(jnp.bfloat16)
    gate_grad = contract_rows(second_normed, gate_back)
    up_grad = contract_rows(second_normed, up_back)
    second_back = scatter_rows(
        times_transposed(gate_back, gate_used) + times_transposed(up_back, up_used)
    )
    residual_back, mlp_gain_part = norm_back(residual, second_scale, second_gain, second_back)
    residual_back = residual_back + cot_rows
    branch_back = gather_rows(residual_back.astype(jnp.bfloat16))
    attended_back = times_transposed(branch_back, out_full).astype(jnp.bfloat16)
    out_grad = contract_rows(attended, branch_back)
    key_accum = jnp.zeros((tree_len, local_groups, HD), jnp.float32)
    value_accum = jnp.zeros((tree_len, local_groups, HD), jnp.float32)
    query_blocks = []
    for block_index, row_start in enumerate(range(0, tree_len, block_rows)):
        allowed = allowed_block(row_start)
        query_block = query_groups[row_start : row_start + block_rows]
        raw_scores = (
            jnp.einsum("qkgd,skd->kgqs", query_block, key_rows, preferred_element_type=jnp.float32)
            * score_scale
        )
        masked = jnp.where(allowed[None, None], raw_scores, -1e30)
        prob_block = jnp.exp(masked - lse_blocks[block_index])
        probs_low = prob_block.astype(jnp.bfloat16)
        grad_block = attended_back[row_start : row_start + block_rows].reshape(
            block_rows, local_groups, group_size, HD
        )
        prob_back = jnp.einsum(
            "qkgd,skd->kgqs", grad_block, value_rows, preferred_element_type=jnp.float32
        )
        row_delta = jnp.sum(prob_block * prob_back, axis=-1, keepdims=True)
        score_back = (prob_block * (prob_back - row_delta)).astype(jnp.bfloat16)
        query_blocks.append(
            jnp.einsum("kgqs,skd->qkgd", score_back, key_rows, preferred_element_type=jnp.float32)
            * score_scale
        )
        key_accum = (
            key_accum
            + jnp.einsum(
                "kgqs,qkgd->skd", score_back, query_block, preferred_element_type=jnp.float32
            )
            * score_scale
        )
        value_accum = value_accum + jnp.einsum(
            "kgqs,qkgd->skd", probs_low, grad_block, preferred_element_type=jnp.float32
        )
    query_accum = jnp.concatenate(query_blocks, axis=0).reshape(tree_len, local_heads, HD)
    query_back = (
        rope_back(query_accum, cosine_table, sine_table)
        .astype(jnp.bfloat16)
        .reshape(tree_len, local_heads * HD)
    )
    key_back = (
        rope_back(key_accum, cosine_table, sine_table)
        .astype(jnp.bfloat16)
        .reshape(tree_len, local_groups * HD)
    )
    value_back = value_accum.astype(jnp.bfloat16).reshape(tree_len, local_groups * HD)
    query_grad = contract_rows(first_normed, query_back)
    key_grad = contract_rows(first_normed, key_back)
    value_grad = contract_rows(first_normed, value_back)
    first_back = scatter_rows(
        times_transposed(query_back, query_full)
        + times_transposed(key_back, key_full)
        + times_transposed(value_back, value_full)
    )
    input_grad, attn_gain_part = norm_back(input_rows, first_scale, first_gain, first_back)
    input_grad = input_grad + residual_back
    attn_gain_sum, query_sum, key_sum, value_sum, mlp_gain_sum, gate_sum, up_sum = (
        lax.psum_scatter(
            attn_gain_part.astype(jnp.bfloat16), "fsdp", scatter_dimension=0, tiled=True
        ).astype(jnp.float32),
        lax.psum_scatter(
            query_grad.astype(jnp.bfloat16), "fsdp", scatter_dimension=0, tiled=True
        ).astype(jnp.float32),
        lax.psum_scatter(
            key_grad.astype(jnp.bfloat16), "fsdp", scatter_dimension=0, tiled=True
        ).astype(jnp.float32),
        lax.psum_scatter(
            value_grad.astype(jnp.bfloat16), "fsdp", scatter_dimension=0, tiled=True
        ).astype(jnp.float32),
        lax.psum_scatter(
            mlp_gain_part.astype(jnp.bfloat16), "fsdp", scatter_dimension=0, tiled=True
        ).astype(jnp.float32),
        lax.psum_scatter(
            gate_grad.astype(jnp.bfloat16), "fsdp", scatter_dimension=0, tiled=True
        ).astype(jnp.float32),
        lax.psum_scatter(
            up_grad.astype(jnp.bfloat16), "fsdp", scatter_dimension=0, tiled=True
        ).astype(jnp.float32),
    )
    out_sum, down_sum = (
        lax.psum_scatter(
            out_grad.astype(jnp.bfloat16), "fsdp", scatter_dimension=1, tiled=True
        ).astype(jnp.float32),
        lax.psum_scatter(
            down_grad.astype(jnp.bfloat16), "fsdp", scatter_dimension=1, tiled=True
        ).astype(jnp.float32),
    )
    attn_gain_total, mlp_gain_total = lax.psum((attn_gain_sum, mlp_gain_sum), "tp")
    return (
        output,
        input_grad,
        attn_gain_total,
        query_sum,
        key_sum,
        value_sum,
        out_sum,
        mlp_gain_total,
        gate_sum,
        up_sum,
        down_sum,
    )


def solution(mesh):
    return jax.shard_map(
        body,
        mesh=mesh,
        in_specs=(
            P(("fsdp", "tp"), None),
            P(("fsdp", "tp"), None),
            P("fsdp"),
            P("fsdp"),
            P("fsdp", None, None),
            P("fsdp"),
            P("fsdp", "tp"),
            P("fsdp", "tp"),
            P("fsdp", "tp"),
            P("tp", "fsdp"),
            P("fsdp"),
            P("fsdp", "tp"),
            P("fsdp", "tp"),
            P("tp", "fsdp"),
        ),
        out_specs=(
            P(("fsdp", "tp"), None),
            P(("fsdp", "tp"), None),
            P("fsdp"),
            P("fsdp", "tp"),
            P("fsdp", "tp"),
            P("fsdp", "tp"),
            P("tp", "fsdp"),
            P("fsdp"),
            P("fsdp", "tp"),
            P("fsdp", "tp"),
            P("tp", "fsdp"),
        ),
        check_vma=False,
    )
```

profile of v0, /device:TPU:0, one launch (start us, length us, event | category | flops | bytes accessed | tf_op | source)
XLA Modules:
  0.0 1434.2 jit_solution(2800710086688930849)
XLA Ops:
  10.0 13.4 all-gather
  31.4 15.0 %all_gather.42 = bf16[2048,128]{1,0:T(8,128)(2,1)S(1)} all-gather(bf16[256,128]{1,0:T(8,128)(2,1)S(1)} %copy-done.37), channel_id=1, replica_groups=mesh['fsdp'=8,'tp'=4] {'fsdp'}, dimensions={0}, use_global_device_ids=true | all-gather | bytes 589824 | tf_op jit(solution)/shard_map/all_gather | solution.py:117
  46.4 15.0 %all_gather.41 = bf16[2048,128]{1,0:T(8,128)(2,1)S(1)} all-gather(bf16[256,128]{1,0:T(8,128)(2,1)S(1)} %copy-done.38), channel_id=1, replica_groups=mesh['fsdp'=8,'tp'=4] {'fsdp'}, dimensions={0}, use_global_device_ids=true | all-gather | bytes 589824 | tf_op jit(solution)/shard_map/all_gather | solution.py:118
  68.4 9.3 all-gather.12.cloned.1.call-done
  81.5 27.0 %all-gather.14.cloned.1.call-done = bf16[2048,512]{1,0:T(8,128)(2,1)} async-done(((bf16[256,512]{1,0:T(8,128)(2,1)}), bf16[2048,512]{1,0:T(8,128)(2,1)}) %all-gather.14.cloned.1.call-update) | async-done | bytes 2097168 | tf_op jit(solution)/shard_map/all_gather | solution.py:116
  108.4 5.2 fusion.83
  116.6 7.3 fusion.80
  123.9 8.3 fusion.7
  133.8 8.1 fusion.36
  142.0 7.3 fusion.81
  149.2 8.1 fusion.6
  157.9 7.4 fusion.37
  165.4 7.5 fusion.52
  173.5 10.3 all-gather.1
  183.9 75.0 %reduce-scatter.12.cloned.1.call-done = f32[256,2048]{1,0:T(8,128)} async-done(((f32[1024,2048]{1,0:T(8,128)}), f32[256,2048]{1,0:T(8,128)}) %reduce-scatter.12.cloned.1.call-update) | async-done | bytes 2097168 | tf_op jit(solution)/shard_map/reduce_scatter | solution.py:77
  264.4 78.1 %all-gather.22.cloned.1.call-done = bf16[2048,2048]{1,0:T(8,128)(2,1)} async-done(((bf16[256,2048]{1,0:T(8,128)(2,1)}), bf16[2048,2048]{1,0:T(8,128)(2,1)}) %all-gather.22.cloned.1.call-update) | async-done | bytes 8388624 | tf_op jit(solution)/shard_map/all_gather | solution.py:165
  342.5 53.7 %all-gather.18.cloned.1.call-done = bf16[1024,2048]{1,0:T(8,128)(2,1)} async-done(((bf16[256,2048]{1,0:T(8,128)(2,1)}), bf16[1024,2048]{1,0:T(8,128)(2,1)}) %all-gather.18.cloned.1.call-update) | async-done | bytes 4194320 | tf_op jit(solution)/shard_map/all_gather | solution.py:73
  396.2 14.7 %fusion.85 = f32[1024,2048]{1,0:T(8,128)} fusion(bf16[1024,2048]{1,0:T(8,128)(2,1)} %all-gather.18.cloned.1.call-done, bf16[2048,2048]{1,0:T(8,128)(2,1)} %all-gather.22.cloned.1.call-done), kind=kOutput, calls=%fused_computation.150 | convolution fusion | flops 8589934592 | bytes 20971520 | tf_op jit(solution)/shard_map/dot_general | solution.py:173
  410.9 69.1 %all-gather.20.cloned.1.call-done = bf16[2048,2048]{1,0:T(8,128)(2,1)} async-done(((bf16[256,2048]{1,0:T(8,128)(2,1)}), bf16[2048,2048]{1,0:T(8,128)(2,1)}) %all-gather.20.cloned.1.call-update) | async-done | bytes 8388624 | tf_op jit(solution)/shard_map/all_gather | solution.py:164
  480.0 14.4 %fusion.84 = f32[1024,2048]{1,0:T(8,128)} fusion(bf16[1024,2048]{1,0:T(8,128)(2,1)} %all-gather.18.cloned.1.call-done, bf16[2048,2048]{1,0:T(8,128)(2,1)} %all-gather.20.cloned.1.call-done), kind=kOutput, calls=%fused_computation.149 | convolution fusion | flops 8589934592 | bytes 20971520 | tf_op jit(solution)/shard_map/dot_general | solution.py:172
  494.4 38.8 %all-gather.26.cloned.1.call-done = bf16[1024,2048]{1,0:T(8,128)(2,1)} async-done(((bf16[256,2048]{1,0:T(8,128)(2,1)}), bf16[1024,2048]{1,0:T(8,128)(2,1)}) %all-gather.26.cloned.1.call-update) | async-done | bytes 4194320 | tf_op jit(solution)/shard_map/all_gather | solution.py:73
  533.2 84.2 %all-gather.24.cloned.1.call-done = bf16[2048,2048]{1,0:T(8,128)(2,1)} async-done(((bf16[2048,256]{1,0:T(8,128)(2,1)}), bf16[2048,2048]{1,0:T(8,128)(2,1)}) %all-gather.24.cloned.1.call-update) | async-done | bytes 8388624 | tf_op jit(solution)/shard_map/all_gather | solution.py:168
  617.5 21.8 %multiply_convert_fusion = (bf16[1024,2048]{1,0:T(8,128)(2,1)}, bf16[1024,2048]{1,0:T(8,128)(2,1)}, bf16[1024,2048]{1,0:T(8,128)(2,1)}) fusion(f32[1024,2048]{1,0:T(8,128)} %fusion.84, f32[1024,2048]{1,0:T(8,128)} %fusion.85, bf16[1024,2048]{1,0:T(8,128)(2,1)} %all-gather.26.cloned.1.call-done, bf16[2048,2048]{1,0:T(8,128)(2,1)} %all-gather.24.cloned.1.call-done), kind=kOutput, calls=%fused_computation.26 | convolution fusion | flops 8623489024 | bytes 41943040 | tf_op jit(solution)/shard_map/dot_general | solution.py:67
  639.3 12.9 fusion.87
  652.2 13.5 convolution_add_fusion
  665.8 14.5 %fusion.86 = f32[1024,2048]{1,0:T(8,128)} fusion(bf16[1024,2048]{1,0:T(8,128)(2,1)} %get-tuple-element.25, bf16[2048,2048]{1,0:T(8,128)(2,1)} %all-gather.24.cloned.1.call-done), kind=kOutput, calls=%fused_computation.151 | convolution fusion | flops 8589934592 | bytes 20971520 | tf_op jit(solution)/shard_map/dot_general | solution.py:177
  680.4 70.1 %reduce-scatter.16.cloned.1.call-done = f32[256,2048]{1,0:T(8,128)} async-done(((f32[1024,2048]{1,0:T(8,128)}), f32[256,2048]{1,0:T(8,128)}) %reduce-scatter.16.cloned.1.call-update) | async-done | bytes 2097168 | tf_op jit(solution)/shard_map/reduce_scatter | solution.py:77
  753.2 86.8 %reduce-scatter.14.cloned.1.call-done = f32[256,2048]{1,0:T(8,128)} async-done(((f32[1024,2048]{1,0:T(8,128)}), f32[256,2048]{1,0:T(8,128)}) %reduce-scatter.14.cloned.1.call-update) | async-done | bytes 2097168 | tf_op jit(solution)/shard_map/reduce_scatter | solution.py:77
  845.1 14.5 %convolution_convert_fusion = bf16[2048,2048]{1,0:T(8,128)(2,1)} fusion(bf16[1024,2048]{1,0:T(8,128)(2,1)} %get-tuple-element.25, bf16[1024,2048]{1,0:T(8,128)(2,1)} %all-gather.26.cloned.1.call-done), kind=kOutput, calls=%fused_computation.33 | convolution fusion | flops 8594128896 | bytes 16777216 | tf_op jit(solution)/shard_map/dot_general | solution.py:61
  859.6 14.1 convolution_convert_fusion.1
  873.8 14.3 convolution_convert_fusion.2
  888.9 9.0 all-gather.28.cloned.1.call-done
  903.5 10.8 fusion.38
  922.4 15.1 %fusion = (f32[2,4,512]{2,1,0:T(4,128)S(1)}, f32[2,1024,512,4]{2,1,3,0:T(8,128)}) fusion(f32[2,4,512,1024]{2,3,1,0:T(8,128)} %get-tuple-element.48, f32[2,4,512]{2,1,0:T(4,128)S(1)} %bitcast.189, bf16[1024,2,64,1]{0,2,3,1:T(8,128)(2,1)} %bitcast.179, bf16[512,2,4,64]{0,3,2,1:T(8,128)(2,1)} %bitcast.170), kind=kOutput, calls=%fused_computation.2 | convolution fusion | flops 549449728 | bytes 34373632 | tf_op jit(solution)/shard_map/qkgd,skd->kgqs/dot_general | solution.py:215
  937.6 12.3 fusion.2
  955.9 7.6 fusion.3
  963.5 12.4 fusion.5
  983.5 6.0 convolution_convert_fusion.3
  994.5 5.7 fusion.35
  1021.6 58.6 %reduce-scatter.30.cloned.1.call-done = bf16[256,2048]{1,0:T(8,128)(2,1)} async-done(((bf16[2048,2048]{1,0:T(8,128)(2,1)}), bf16[256,2048]{1,0:T(8,128)(2,1)}) %reduce-scatter.30.cloned.1.call-update) | async-done | bytes 1048592 | tf_op jit(solution)/shard_map/reduce_scatter | solution.py:275
  1083.0 87.4 %reduce-scatter.28.cloned.1.call-done = bf16[256,2048]{1,0:T(8,128)(2,1)} async-done(((bf16[2048,2048]{1,0:T(8,128)(2,1)}), bf16[256,2048]{1,0:T(8,128)(2,1)}) %reduce-scatter.28.cloned.1.call-update) | async-done | bytes 1048592 | tf_op jit(solution)/shard_map/reduce_scatter | solution.py:272
  1173.2 28.7 %reduce-scatter.24.cloned.1.call-done = bf16[256,128]{1,0:T(8,128)(2,1)} async-done(((bf16[2048,128]{1,0:T(8,128)(2,1)}), bf16[256,128]{1,0:T(8,128)(2,1)}) %reduce-scatter.24.cloned.1.call-update) | async-done | bytes 65552 | tf_op jit(solution)/shard_map/reduce_scatter | solution.py:266
  1203.4 30.3 %reduce-scatter.22.cloned.1.call-done = bf16[256,128]{1,0:T(8,128)(2,1)} async-done(((bf16[2048,128]{1,0:T(8,128)(2,1)}), bf16[256,128]{1,0:T(8,128)(2,1)}) %reduce-scatter.22.cloned.1.call-update) | async-done | bytes 65552 | tf_op jit(solution)/shard_map/reduce_scatter | solution.py:263
  1235.3 34.8 %reduce-scatter.26.cloned.1.call-done = bf16[512,256]{1,0:T(8,128)(2,1)} async-done(((bf16[512,2048]{1,0:T(8,128)(2,1)}), bf16[512,256]{1,0:T(8,128)(2,1)}) %reduce-scatter.26.cloned.1.call-update) | async-done | bytes 262160 | tf_op jit(solution)/shard_map/reduce_scatter | solution.py:280
  1271.9 35.1 %reduce-scatter.20.cloned.1.call-done = bf16[256,512]{1,0:T(8,128)(2,1)} async-done(((bf16[2048,512]{1,0:T(8,128)(2,1)}), bf16[256,512]{1,0:T(8,128)(2,1)}) %reduce-scatter.20.cloned.1.call-update) | async-done | bytes 262160 | tf_op jit(solution)/shard_map/reduce_scatter | solution.py:260
  1308.8 86.5 %reduce-scatter.18.cloned.1.call-done = f32[256,2048]{1,0:T(8,128)} async-done(((f32[1024,2048]{1,0:T(8,128)}), f32[256,2048]{1,0:T(8,128)}) %reduce-scatter.18.cloned.1.call-update) | async-done | bytes 2097168 | tf_op jit(solution)/shard_map/reduce_scatter | solution.py:77
  1397.6 16.6 %all-reduce.3 = (bf16[2048]{0:T(1024)(128)(2,1)S(1)}, bf16[2048]{0:T(1024)(128)(2,1)S(1)}) all-reduce(bf16[2048]{0:T(1024)(128)(2,1)S(1)} %get-tuple-element.13, bf16[2048]{0:T(1024)(128)(2,1)S(1)} %copy-done.46), channel_id=6, replica_groups=mesh['fsdp'=8,'tp'=4] {'fsdp'}, use_global_device_ids=true, to_apply=%region_15.16.clone | all-reduce | flops 4096 | bytes 16384
  1414.2 9.4 all-reduce.2
  (247 shorter events, 111.9 us)
Async XLA Ops:
  7.2 21.0 %copy-start.47 = (s32[1,13,13]{2,0,1:T(1,128)S(1)}, s32[1,13,13]{2,0,1:T(1,128)}, u32[]{:S(2)}) copy-start(s32[1,13,13]{2,0,1:T(1,128)} %param.19) | copy-start | bytes 2032
  7.2 21.0 %copy-start.43 = (s32[1024]{0:T(1024)S(1)}, s32[1024]{0:T(1024)}, u32[]{:S(2)}) copy-start(s32[1024]{0:T(1024)} %param.17) | copy-start | bytes 12292
  7.2 70.5 %all-gather.12.cloned.1.call-start = ((), (), s32[]{:S(2)}) async-start(), calls=%async_computation.11 | async-start | bytes 5242880 | tf_op jit(solution)/shard_map/all_gather | solution.py:73
  10.0 21.4 %copy-start.44 = (f32[256]{0:T(256)}, f32[256]{0:T(256)S(1)}, u32[]{:S(2)}) copy-start(f32[256]{0:T(256)S(1)} %get-tuple-element.44) | copy-start | bytes 3076
  24.1 22.3 %copy-start.38 = (bf16[256,128]{1,0:T(8,128)(2,1)S(1)}, bf16[256,128]{1,0:T(8,128)(2,1)}, u32[]{:S(2)}) copy-start(bf16[256,128]{1,0:T(8,128)(2,1)} %param.23) | copy-start | bytes 196612
  26.6 34.7 %copy-start.50 = (f32[32]{0:T(128)S(1)}, f32[32]{0:T(128)}, u32[]{:S(2)}) copy-start(f32[32]{0:T(128)} %constant.26.clone) | copy-start | bytes 388
  26.6 81.8 %all-gather.14.cloned.1.call-start = ((), (), s32[]{:S(2)}) async-start(), calls=%async_computation.12 | async-start | bytes 2359296 | tf_op jit(solution)/shard_map/all_gather | solution.py:116
  27.4 138.0 %all-gather.16.cloned.1.call-start = ((), (), s32[]{:S(2)}) async-start(), calls=%async_computation.13 | async-start | bytes 2359296 | tf_op jit(solution)/shard_map/all_gather | solution.py:159
  28.1 230.8 %reduce-scatter.12.cloned.1.call-start = ((), (), s32[]{:S(2)}) async-start(), calls=%async_computation.14 | async-start | bytes 10485760 | tf_op jit(solution)/shard_map/reduce_scatter | solution.py:77
  46.4 31.4 %copy-start.15 = (bf16[2048,128]{1,0:T(8,128)(2,1)}, bf16[2048,128]{1,0:T(8,128)(2,1)S(1)}, u32[]{:S(2)}) copy-start(bf16[2048,128]{1,0:T(8,128)(2,1)S(1)} %all_gather.42) | copy-start | bytes 1572868
  61.3 70.9 %copy-start.13 = (bf16[2048,128]{1,0:T(8,128)(2,1)}, bf16[2048,128]{1,0:T(8,128)(2,1)S(1)}, u32[]{:S(2)}) copy-start(bf16[2048,128]{1,0:T(8,128)(2,1)S(1)} %all_gather.41) | copy-start | bytes 1572868
  63.4 50.4 %copy-start.24 = (f32[1024,64]{0,1:T(8,128)}, f32[1024,64]{0,1:T(8,128)S(1)}, u32[]{:S(2)}) copy-start(f32[1024,64]{0,1:T(8,128)S(1)} %get-tuple-element.42) | copy-start | bytes 786436
  63.4 51.9 %copy-start.22 = (f32[1024,64]{0,1:T(8,128)}, f32[1024,64]{0,1:T(8,128)S(1)}, u32[]{:S(2)}) copy-start(f32[1024,64]{0,1:T(8,128)S(1)} %get-tuple-element.41) | copy-start | bytes 786436
  116.6 25.4 %copy-start.9 = (bf16[1024,2,64,1]{0,2,3,1:T(8,128)(2,1)}, bf16[1024,2,64,1]{0,2,3,1:T(8,128)(2,1)S(1)}, u32[]{:S(2)}) copy-start(bf16[1024,2,64,1]{0,2,3,1:T(8,128)(2,1)S(1)} %fusion.58) | copy-start | bytes 786436
  133.8 23.5 %copy-start.26 = (bf16[1024,128]{0,1:T(8,128)(2,1)}, bf16[1024,128]{0,1:T(8,128)(2,1)S(1)}, u32[]{:S(2)}) copy-start(bf16[1024,128]{0,1:T(8,128)(2,1)S(1)} %convolution_convert_fusion.8) | copy-start | bytes 786436
  141.9 23.4 %copy-start.54 = (bf16[2,64,4,512]{3,1,2,0:T(8,128)(2,1)}, bf16[2,64,4,512]{3,1,2,0:T(8,128)(2,1)S(1)}, u32[]{:S(2)}) copy-start(bf16[2,64,4,512]{3,1,2,0:T(8,128)(2,1)S(1)} %fusion.36) | copy-start | bytes 1572868
  172.8 86.1 %copy-start.2 = (bf16[256,2048]{1,0:T(8,128)(2,1)S(1)}, bf16[256,2048]{1,0:T(8,128)(2,1)}, u32[]{:S(2)}) copy-start(bf16[256,2048]{1,0:T(8,128)(2,1)} %param.15) | copy-start | bytes 3145732
  172.9 169.7 %all-gather.22.cloned.1.call-start = ((), (), s32[]{:S(2)}) async-start(), calls=%async_computation.17 | async-start | bytes 9437184 | tf_op jit(solution)/shard_map/all_gather | solution.py:165
  173.4 222.8 %all-gather.18.cloned.1.call-start = ((), (), s32[]{:S(2)}) async-start(), calls=%async_computation.15 | async-start | bytes 5242880 | tf_op jit(solution)/shard_map/all_gather | solution.py:73
  262.1 217.9 %all-gather.20.cloned.1.call-start = ((), (), s32[]{:S(2)}) async-start(), calls=%async_computation.16 | async-start | bytes 9437184 | tf_op jit(solution)/shard_map/all_gather | solution.py:164
  262.9 270.4 %all-gather.26.cloned.1.call-start = ((), (), s32[]{:S(2)}) async-start(), calls=%async_computation.20 | async-start | bytes 5242880 | tf_op jit(solution)/shard_map/all_gather | solution.py:73
  263.6 353.9 %all-gather.24.cloned.1.call-start = ((), (), s32[]{:S(2)}) async-start(), calls=%async_computation.18 | async-start | bytes 9437184 | tf_op jit(solution)/shard_map/all_gather | solution.py:168
  264.3 486.2 %reduce-scatter.16.cloned.1.call-start = ((), (), s32[]{:S(2)}) async-start(), calls=%async_computation.21 | async-start | bytes 10485760 | tf_op jit(solution)/shard_map/reduce_scatter | solution.py:77
  639.3 12.9 copy-start.59
  665.8 174.3 %reduce-scatter.14.cloned.1.call-start = ((), (), s32[]{:S(2)}) async-start(), calls=%async_computation.19 | async-start | bytes 10485760 | tf_op jit(solution)/shard_map/reduce_scatter | solution.py:77
  680.3 159.7 %copy-start.21 = (bf16[256,2048]{1,0:T(8,128)(2,1)S(1)}, bf16[256,2048]{1,0:T(8,128)(2,1)}, u32[]{:S(2)}) copy-start(bf16[256,2048]{1,0:T(8,128)(2,1)} %param.16) | copy-start | bytes 3145732
  680.3 217.6 %all-gather.28.cloned.1.call-start = ((), (), s32[]{:S(2)}) async-start(), calls=%async_computation.22 | async-start | bytes 5242880 | tf_op jit(solution)/shard_map/all_gather | solution.py:73
  845.0 173.8 %reduce-scatter.32.cloned.1.call-start = ((), (), s32[]{:S(2)}) async-start(), calls=%async_computation.30 | async-start | bytes 9437184 | tf_op jit(solution)/shard_map/reduce_scatter | solution.py:283
  859.6 220.6 %reduce-scatter.30.cloned.1.call-start = ((), (), s32[]{:S(2)}) async-start(), calls=%async_computation.29 | async-start | bytes 9437184 | tf_op jit(solution)/shard_map/reduce_scatter | solution.py:275
  873.8 296.6 %reduce-scatter.28.cloned.1.call-start = ((), (), s32[]{:S(2)}) async-start(), calls=%async_computation.28 | async-start | bytes 9437184 | tf_op jit(solution)/shard_map/reduce_scatter | solution.py:272
  888.1 313.8 %reduce-scatter.24.cloned.1.call-start = ((), (), s32[]{:S(2)}) async-start(), calls=%async_computation.26 | async-start | bytes 589824 | tf_op jit(solution)/shard_map/reduce_scatter | solution.py:266
  897.9 16.4 %slice-start.4 = ((s8[16777216]{0:T(1024)(128)(4,1)}), s8[4194304]{0:T(1024)(128)(4,1)S(1)}, s32[]{:S(2)}) async-start(s8[16777216]{0:T(1024)(128)(4,1)} %bitcast.163), calls=%async_computation.35 | async-start | bytes 8388608
  897.9 16.4 %slice-start.5 = ((s8[16777216]{0:T(1024)(128)(4,1)}), s8[4194304]{0:T(1024)(128)(4,1)S(1)}, s32[]{:S(2)}) async-start(s8[16777216]{0:T(1024)(128)(4,1)} %bitcast.163), calls=%async_computation.36 | async-start | bytes 8388608
  922.4 33.4 %slice-start = ((s8[16777216]{0:T(1024)(128)(4,1)}), s8[4194304]{0:T(1024)(128)(4,1)S(1)}, s32[]{:S(2)}) async-start(s8[16777216]{0:T(1024)(128)(4,1)} %bitcast.161), calls=%async_computation.31 | async-start | bytes 8388608
  922.4 33.4 %slice-start.1 = ((s8[16777216]{0:T(1024)(128)(4,1)}), s8[4194304]{0:T(1024)(128)(4,1)S(1)}, s32[]{:S(2)}) async-start(s8[16777216]{0:T(1024)(128)(4,1)} %bitcast.161), calls=%async_computation.32 | async-start | bytes 8388608
  937.5 15.6 %copy-start.18 = (bf16[512,8,64]{0,2,1:T(8,128)(2,1)S(1)}, bf16[512,8,64]{0,2,1:T(8,128)(2,1)}, u32[]{:S(2)}) copy-start(bf16[512,8,64]{0,2,1:T(8,128)(2,1)} %copy-done.17) | copy-start | bytes 1572868
  937.5 18.3 %slice-start.2 = ((s8[16777216]{0:T(1024)(128)(4,1)}), s8[4194304]{0:T(1024)(128)(4,1)S(1)}, s32[]{:S(2)}) async-start(s8[16777216]{0:T(1024)(128)(4,1)} %bitcast.161), calls=%async_computation.33 | async-start | bytes 8388608
  937.6 18.3 %slice-start.3 = ((s8[16777216]{0:T(1024)(128)(4,1)}), s8[4194304]{0:T(1024)(128)(4,1)S(1)}, s32[]{:S(2)}) async-start(s8[16777216]{0:T(1024)(128)(4,1)} %bitcast.161), calls=%async_computation.34 | async-start | bytes 8388608
  963.5 270.3 %reduce-scatter.22.cloned.1.call-start = ((), (), s32[]{:S(2)}) async-start(), calls=%async_computation.25 | async-start | bytes 589824 | tf_op jit(solution)/shard_map/reduce_scatter | solution.py:263
  983.4 286.7 %reduce-scatter.26.cloned.1.call-start = ((), (), s32[]{:S(2)}) async-start(), calls=%async_computation.27 | async-start | bytes 2359296 | tf_op jit(solution)/shard_map/reduce_scatter | solution.py:280
  989.5 317.5 %reduce-scatter.20.cloned.1.call-start = ((), (), s32[]{:S(2)}) async-start(), calls=%async_computation.24 | async-start | bytes 2359296 | tf_op jit(solution)/shard_map/reduce_scatter | solution.py:260
  1008.0 387.3 %reduce-scatter.18.cloned.1.call-start = ((), (), s32[]{:S(2)}) async-start(), calls=%async_computation.23 | async-start | bytes 10485760 | tf_op jit(solution)/shard_map/reduce_scatter | solution.py:77
  1021.6 373.7 %copy-start.3 = (bf16[256,2048]{1,0:T(8,128)(2,1)S(1)}, bf16[256,2048]{1,0:T(8,128)(2,1)}, u32[]{:S(2)}) copy-start(bf16[256,2048]{1,0:T(8,128)(2,1)} %param.15) | copy-start | bytes 3145732
  1021.6 373.7 %copy-start.36 = (f32[8,1,256]{2,1,0:T(1,128)S(1)}, f32[8,1,256]{2,1,0:T(1,128)}, u32[]{:S(2)}) copy-start(f32[8,1,256]{2,1,0:T(1,128)} %copy-done.35) | copy-start | bytes 24580
  1021.6 373.7 %copy-start.45 = (f32[256]{0:T(256)S(1)}, f32[256]{0:T(256)}, u32[]{:S(2)}) copy-start(f32[256]{0:T(256)} %copy-done.44) | copy-start | bytes 3076
  1083.0 314.6 %copy-start.46 = (bf16[2048]{0:T(1024)(128)(2,1)S(1)}, bf16[2048]{0:T(1024)(128)(2,1)}, u32[]{:S(2)}) copy-start(bf16[2048]{0:T(1024)(128)(2,1)} %get-tuple-element.11) | copy-start | bytes 12292
  1083.0 340.7 %copy-start.48 = (f32[256]{0:T(256)S(1)}, f32[256]{0:T(256)}, u32[]{:S(2)}) copy-start(f32[256]{0:T(256)} %get-tuple-element.43) | copy-start | bytes 3076
  1395.3 28.4 %copy-start.8 = (f32[256,2048]{1,0:T(8,128)S(1)}, f32[256,2048]{1,0:T(8,128)}, u32[]{:S(2)}) copy-start(f32[256,2048]{1,0:T(8,128)} %reduce-scatter.18.cloned.1.call-done) | copy-start | bytes 6291460
  (40 other events, 203.2 us)
Sparse Core Ops, SparseCore 0:
  26.7 50.9 all-gather.11
  79.3 29.0 all-gather.13
  110.0 30.3 all-gather.15
  173.0 85.8 reduce-scatter.11
  260.4 82.0 all-gather.21
  344.9 51.2 all-gather.17
  397.9 82.0 all-gather.19
  482.0 51.2 all-gather.25
  534.9 82.4 all-gather.23
  665.9 84.5 reduce-scatter.15
  753.6 86.3 reduce-scatter.13
  845.2 52.6 all-gather.27
  900.3 89.5 reduce-scatter.31
  992.2 87.9 reduce-scatter.29
  1082.4 87.9 reduce-scatter.27
  1172.6 29.2 reduce-scatter.23
  1204.6 29.1 reduce-scatter.21
  1236.0 34.0 reduce-scatter.25
  1272.5 34.4 reduce-scatter.19
  1310.2 85.0 reduce-scatter.17
where the time goes:
time: 1440 us; the launch traced here: 1430 us
  waiting for transfers between devices  967 us (67%)
  matrix products  271 us (19%)
  other arithmetic  83.3 us (6%)
  blocking collectives  79.7 us (6%)
  between operations  16 us (1%)
  local copies, waits for them, and re-layouts  15.7 us (1%)
    reduce_scatter x4, waiting for transfers between devices, scatter_rows(): return lax.psum_scatter(partial_sums, 'tp', scatter_dimension=0, tiled=True)  318 us
    all_gather x4, waiting for transfers between devices, gather_rows(): return lax.all_gather(pieces, 'tp', axis=0, tiled=True)  111 us
    reduce_scatter x1, waiting for transfers between devices, body(): lax.psum_scatter(gate_grad.astype(jnp.bfloat16), 'fsdp', scatter_dimensio...  87.4 us
    all_gather x1, waiting for transfers between devices, body(): down_full = lax.all_gather(down_weight, 'fsdp', axis=1, tiled=True)  84.2 us
    all_gather x1, waiting for transfers between devices, body(): lax.all_gather(up_weight, 'fsdp', axis=0, tiled=True)  78.1 us
    all_gather x1, waiting for transfers between devices, body(): lax.all_gather(gate_weight, 'fsdp', axis=0, tiled=True)  69.1 us
    dot_general x11, matrix products, times_transposed(): lax.dot_general(left, right, (((1,), (1,)), ((), ())), preferred_element_...  66.9 us
    reduce_scatter x1, waiting for transfers between devices, body(): lax.psum_scatter(up_grad.astype(jnp.bfloat16), 'fsdp', scatter_dimension=...  58.6 us
  transfers between devices with their start and end apart: 20, of which 18 were waited for; matrix products, arithmetic and copies ran while one was open for 20% of the time, Pallas kernels for 0%

commit v1 on v0

v1 whole, which is shorter than its diff:
```python
import functools
import math

import jax
import jax.numpy as jnp
import numpy as np
from jax import lax
from jax.experimental import pallas as pl
from jax.experimental.pallas import tpu as pltpu
from jax.sharding import PartitionSpec as P

HD = 64
SEGS = 13
SEG = 64
TRUNK = 256
BRANCHES = 4
EPSILON = 1e-05
PARTS = (3, 3, 2)
HOPS = 1
NEG = -1e30
BF = jnp.bfloat16
F32 = jnp.float32


def inverse_freq(head_size):
    base_freq = 1.0 / 500000.0 ** (np.arange(0, head_size, 2) / head_size)
    wavelen = 2.0 * math.pi / base_freq
    smooth = (8192.0 / wavelen - 1.0) / 3.0
    blended = (1.0 - smooth) * base_freq / 32.0 + smooth * base_freq
    scaled = np.where(
        wavelen > 8192.0, base_freq / 32.0, np.where(wavelen < 2048.0, base_freq, blended)
    )
    return scaled.astype(np.float32)


def dot_nn(left, right):
    return lax.dot_general(
        left, right, (((1,), (0,)), ((), ())), preferred_element_type=F32
    )


def dot_nt(left, right):
    return lax.dot_general(
        left, right, (((1,), (1,)), ((), ())), preferred_element_type=F32
    )


def dot_tn(left, right):
    return lax.dot_general(
        left, right, (((0,), (0,)), ((), ())), preferred_element_type=F32
    )


def rope_lanes(values, cosine, signed_sine, low_half):
    rolled = jnp.where(low_half, pltpu.roll(values, 96, 1), pltpu.roll(values, 32, 1))
    return values * cosine + rolled * signed_sine


def rope_lanes_back(grads, cosine, signed_sine, low_half):
    scaled = grads * signed_sine
    rolled = jnp.where(low_half, pltpu.roll(scaled, 96, 1), pltpu.roll(scaled, 32, 1))
    return grads * cosine + rolled


def low_half_mask(rows):
    lane = lax.broadcasted_iota(jnp.int32, (rows, 128), 1)
    return lax.rem(lane, HD) < HD // 2


def parent_block(mask_ref, seg_ref, segment, block_count):
    parent = jnp.int32(0)
    for branch in range(1, BRANCHES + 1):
        parent = parent + branch * mask_ref[segment * SEGS + branch]
    parent = jnp.where(segment > BRANCHES, parent, segment)
    found = jnp.int32(0)
    for block in range(block_count):
        found = found + block * (seg_ref[block] == parent).astype(jnp.int32)
    return found


def block_mask(has_parent, members):
    shape = (members * SEG, 2 * SEG)
    row = lax.rem(lax.broadcasted_iota(jnp.int32, shape, 0), SEG)
    col = lax.broadcasted_iota(jnp.int32, shape, 1)
    return ((col < SEG) & has_parent) | ((col >= SEG) & (col - SEG <= row))


def trunk_mask(index, members):
    shape = (members * SEG, TRUNK)
    row = lax.rem(lax.broadcasted_iota(jnp.int32, shape, 0), SEG) + index * SEG
    col = lax.broadcasted_iota(jnp.int32, shape, 1)
    return col <= row


def softmax_rows(scores):
    row_max = jnp.max(scores, axis=-1, keepdims=True)
    exponent = jnp.exp(scores - row_max)
    return exponent / jnp.sum(exponent, axis=-1, keepdims=True)


def attn_fwd_kernel(
    heads, groups, mask_ref, seg_ref, base_ref, pre_ref, cos_ref, sin_ref,
    att_ref, q_ref, k_ref, v_ref,
):
    rows = pre_ref.shape[0]
    blocks = rows // SEG
    members = heads // groups
    score_scale = HD ** (-0.5)
    low_half = low_half_mask(rows)
    cosine = cos_ref[...]
    sine = sin_ref[...]
    q_width = heads * HD
    kv_width = groups * HD

    def put_heads(dest, first, wide, count):
        for half in range(count):
            head = first + half
            part = wide[:, half * HD : (half + 1) * HD].reshape(blocks, SEG, HD)
            group, member = head // members, head % members
            dest[group, :, member * SEG : (member + 1) * SEG, :] = part

    for pair in range(q_width // 128):
        lanes = pre_ref[:, pair * 128 : (pair + 1) * 128]
        put_heads(q_ref, 2 * pair, rope_lanes(lanes, cosine, sine, low_half).astype(BF), 2)
    if kv_width % 128 == 0:
        for pair in range(kv_width // 128):
            at = q_width + pair * 128
            wide = rope_lanes(pre_ref[:, at : at + 128], cosine, sine, low_half).astype(BF)
            at = q_width + kv_width + pair * 128
            plain = pre_ref[:, at : at + 128].astype(BF)
            for half in range(2):
                k_ref[2 * pair + half] = wide[:, half * HD : (half + 1) * HD]
                v_ref[2 * pair + half] = plain[:, half * HD : (half + 1) * HD]
    else:
        both = pre_ref[:, q_width : q_width + 128]
        k_ref[0] = rope_lanes(both, cosine, sine, low_half).astype(BF)[:, :HD]
        v_ref[0] = both.astype(BF)[:, HD:]

    base = base_ref[0]
    trunk_block = base // SEG
    trunk_rows = pl.ds(pl.multiple_of(base, TRUNK), TRUNK)

    def store(group, block, mixed):
        at = pl.ds(pl.multiple_of(block * SEG, SEG), SEG)
        for member in range(members):
            head = group * members + member
            att_ref[at, head * HD : (head + 1) * HD] = mixed[
                member * SEG : (member + 1) * SEG
            ].astype(BF)

    for group in range(groups):
        def one_block(block, carry):
            inside = block - trunk_block
            is_trunk = (inside >= 0) & (inside < TRUNK // SEG)

            @pl.when(is_trunk)
            def _():
                queries = q_ref[group, block]
                scores = dot_nt(queries, k_ref[group, trunk_rows, :]) * score_scale
                scores = jnp.where(trunk_mask(inside, members), scores, NEG)
                probs = softmax_rows(scores).astype(BF)
                store(group, block, dot_nn(probs, v_ref[group, trunk_rows, :]))

            @pl.when(jnp.logical_not(is_trunk))
            def _():
                segment = seg_ref[block]
                parent = parent_block(mask_ref, seg_ref, segment, blocks)
                up = pl.ds(pl.multiple_of(parent * SEG, SEG), SEG)
                own = pl.ds(pl.multiple_of(block * SEG, SEG), SEG)
                queries = q_ref[group, block]
                keys = jnp.concatenate(
                    [k_ref[group, trunk_rows, :], k_ref[group, up, :], k_ref[group, own, :]], axis=0
                )
                vals = jnp.concatenate(
                    [v_ref[group, trunk_rows, :], v_ref[group, up, :], v_ref[group, own, :]], axis=0
                )
                scores = dot_nt(queries, keys) * score_scale
                tail = jnp.where(
                    block_mask(segment > BRANCHES, members), scores[:, TRUNK:], NEG
                )
                scores = jnp.concatenate([scores[:, :TRUNK], tail], axis=1)
                probs = softmax_rows(scores).astype(BF)
                store(group, block, dot_nn(probs, vals))

            return carry

        lax.fori_loop(0, blocks, one_block, 0)


def attn_bwd_kernel(
    heads, groups, mask_ref, seg_ref, base_ref, q_ref, k_ref, v_ref, grad_ref, cos_ref, sin_ref,
    out_ref, g_ref, dq_ref, dk_ref, dv_ref,
):
    rows = grad_ref.shape[0]
    blocks = rows // SEG
    members = heads // groups
    score_scale = HD ** (-0.5)
    low_half = low_half_mask(rows)
    cosine = cos_ref[...]
    sine = sin_ref[...]
    q_width = heads * HD
    kv_width = groups * HD
    for head in range(heads):
        part = grad_ref[:, head * HD : (head + 1) * HD].reshape(blocks, SEG, HD)
        group, member = head // members, head % members
        g_ref[group, :, member * SEG : (member + 1) * SEG, :] = part
    dk_ref[...] = jnp.zeros_like(dk_ref)
    dv_ref[...] = jnp.zeros_like(dv_ref)
    base = base_ref[0]
    trunk_block = base // SEG
    trunk_rows = pl.ds(pl.multiple_of(base, TRUNK), TRUNK)

    def store(group, block, d_query):
        at = pl.ds(pl.multiple_of(block * SEG, SEG), SEG)
        for member in range(members):
            head = group * members + member
            dq_ref[at, head * HD : (head + 1) * HD] = d_query[member * SEG : (member + 1) * SEG]

    for group in range(groups):
        lanes = slice(group * HD, (group + 1) * HD)

        def grads(queries, out_grads, keys, vals, scores):
            probs = softmax_rows(scores)
            prob_back = dot_nt(out_grads, vals)
            delta = jnp.sum(probs * prob_back, axis=-1, keepdims=True)
            score_back = (probs * (prob_back - delta)).astype(BF)
            d_query = dot_nn(score_back, keys) * score_scale
            d_key = dot_tn(score_back, queries) * score_scale
            d_val = dot_tn(probs.astype(BF), out_grads)
            return d_query, d_key, d_val

        def one_block(block, carry):
            inside = block - trunk_block
            is_trunk = (inside >= 0) & (inside < TRUNK // SEG)

            @pl.when(is_trunk)
            def _():
                queries = q_ref[group, block]
                keys = k_ref[group, trunk_rows, :]
                scores = dot_nt(queries, keys) * score_scale
                scores = jnp.where(trunk_mask(inside, members), scores, NEG)
                d_query, d_key, d_val = grads(
                    queries, g_ref[group, block], keys, v_ref[group, trunk_rows, :], scores
                )
                store(group, block, d_query)
                dk_ref[trunk_rows, lanes] += d_key
                dv_ref[trunk_rows, lanes] += d_val

            @pl.when(jnp.logical_not(is_trunk))
            def _():
                segment = seg_ref[block]
                parent = parent_block(mask_ref, seg_ref, segment, blocks)
                up = pl.ds(pl.multiple_of(parent * SEG, SEG), SEG)
                own = pl.ds(pl.multiple_of(block * SEG, SEG), SEG)
                queries = q_ref[group, block]
                keys = jnp.concatenate(
                    [k_ref[group, trunk_rows, :], k_ref[group, up, :], k_ref[group, own, :]], axis=0
                )
                vals = jnp.concatenate(
                    [v_ref[group, trunk_rows, :], v_ref[group, up, :], v_ref[group, own, :]], axis=0
                )
                scores = dot_nt(queries, keys) * score_scale
                tail = jnp.where(
                    block_mask(segment > BRANCHES, members), scores[:, TRUNK:], NEG
                )
                scores = jnp.concatenate([scores[:, :TRUNK], tail], axis=1)
                d_query, d_key, d_val = grads(queries, g_ref[group, block], keys, vals, scores)
                store(group, block, d_query)
                for ref, val in ((dk_ref, d_key), (dv_ref, d_val)):
                    ref[trunk_rows, lanes] += val[:TRUNK]
                    ref[up, lanes] += val[TRUNK : TRUNK + SEG]
                    ref[own, lanes] += val[TRUNK + SEG :]

            return carry

        lax.fori_loop(0, blocks, one_block, 0)
    for pair in range(q_width // 128):
        at = slice(pair * 128, (pair + 1) * 128)
        out_ref[:, at] = rope_lanes_back(dq_ref[:, at], cosine, sine, low_half).astype(BF)
    if kv_width % 128 == 0:
        for pair in range(kv_width // 128):
            at = slice(pair * 128, (pair + 1) * 128)
            turned = rope_lanes_back(dk_ref[:, at], cosine, sine, low_half)
            out_ref[:, q_width + pair * 128 : q_width + (pair + 1) * 128] = turned.astype(BF)
            first = q_width + kv_width + pair * 128
            out_ref[:, first : first + 128] = dv_ref[:, at].astype(BF)
    else:
        wide = jnp.concatenate([dk_ref[...], dv_ref[...]], axis=1)
        turned = rope_lanes_back(wide, cosine, sine, low_half)
        lane = lax.broadcasted_iota(jnp.int32, (rows, 128), 1)
        out_ref[:, q_width : q_width + 128] = jnp.where(lane < HD, turned, wide).astype(BF)


SMEM = pl.BlockSpec(memory_space=pltpu.SMEM)
VMEM = pl.BlockSpec(memory_space=pltpu.VMEM)


def attention_forward(heads, groups, masks, segs, base, pre, cosine, sine):
    rows = pre.shape[0]
    members = heads // groups
    blocks = rows // SEG
    return pl.pallas_call(
        functools.partial(attn_fwd_kernel, heads, groups),
        name="attn_fwd",
        out_shape=(
            jax.ShapeDtypeStruct((rows, heads * HD), BF),
            jax.ShapeDtypeStruct((groups, blocks, members * SEG, HD), BF),
            jax.ShapeDtypeStruct((groups, rows, HD), BF),
            jax.ShapeDtypeStruct((groups, rows, HD), BF),
        ),
        in_specs=[SMEM, SMEM, SMEM, VMEM, VMEM, VMEM],
        out_specs=(VMEM, VMEM, VMEM, VMEM),
        compiler_params=pltpu.CompilerParams(vmem_limit_bytes=40 << 20),
        cost_estimate=pl.CostEstimate(
            flops=8_000_000_000, bytes_accessed=8_000_000, transcendentals=3_000_000
        ),
    )(masks, segs, base, pre, cosine, sine)


def attention_backward(heads, groups, masks, segs, base, queries, keys, vals, grads, cosine, sine):
    rows = grads.shape[0]
    members = heads // groups
    blocks = rows // SEG
    return pl.pallas_call(
        functools.partial(attn_bwd_kernel, heads, groups),
        name="attn_bwd",
        out_shape=jax.ShapeDtypeStruct((rows, (heads + 2 * groups) * HD), BF),
        in_specs=[SMEM, SMEM, SMEM, VMEM, VMEM, VMEM, VMEM, VMEM, VMEM],
        out_specs=VMEM,
        scratch_shapes=[
            pltpu.VMEM((groups, blocks, members * SEG, HD), BF),
            pltpu.VMEM((rows, heads * HD), F32),
            pltpu.VMEM((rows, groups * HD), F32),
            pltpu.VMEM((rows, groups * HD), F32),
        ],
        compiler_params=pltpu.CompilerParams(vmem_limit_bytes=40 << 20),
        cost_estimate=pl.CostEstimate(
            flops=20_000_000_000, bytes_accessed=8_000_000, transcendentals=3_000_000
        ),
    )(masks, segs, base, queries, keys, vals, grads, cosine, sine)


def chunk_kernel(steps, slabs, halves, added, last, order_ref, *refs):
    rows_ref, cot_ref, full_ref, rows_turned_ref, cot_turned_ref = refs[:5]
    refs = refs[5:]
    if added:
        (back_in_ref, out_in_ref), refs = refs[:2], refs[2:]
    grad_refs, refs = refs[:halves], refs[halves:]
    back_ref, out_ref, pair_ref, hidden_ref = refs
    step = pl.program_id(0)
    chunk = hidden_ref.shape[1]
    tile = chunk // steps
    height = rows_turned_ref.shape[0]

    for at in range(steps):

        @pl.when(step == at)
        def _():
            cut = slice(at * tile, (at + 1) * tile)
            gate = dot_nn(rows_ref[...], full_ref[:, cut])
            up = dot_nn(rows_ref[...], full_ref[:, chunk + at * tile : chunk + (at + 1) * tile])
            back = dot_nn(
                cot_ref[...], full_ref[:, 2 * chunk + at * tile : 2 * chunk + (at + 1) * tile]
            )
            sigmoid = 1.0 / (1.0 + jnp.exp(-gate))
            silu = gate * sigmoid
            hidden_ref[:, cut] = (silu * up).astype(BF)
            pair_ref[:, cut] = (back * up * sigmoid * (1.0 + gate * (1.0 - sigmoid))).astype(BF)
            pair_ref[:, chunk + at * tile : chunk + (at + 1) * tile] = (back * silu).astype(BF)

    def write(grad_ref):
        grad = jnp.concatenate(
            [
                dot_nn(rows_turned_ref[...], pair_ref[...]).astype(BF),
                dot_nn(cot_turned_ref[...], hidden_ref[...]).astype(BF),
            ],
            axis=1,
        )
        grad_ref[...] = grad.reshape(grad_ref.shape)

    @pl.when(step >= steps)
    def _():
        slab = pl.ds(pl.multiple_of(order_ref[step - steps] * height, height), height)
        back = dot_nt(pair_ref[...], full_ref[slab, : 2 * chunk])
        out = dot_nt(hidden_ref[...], full_ref[slab, 2 * chunk :])
        back = back_in_ref[...] + back if added else back
        out = out_in_ref[...] + out if added else out
        back_ref[...] = back.astype(back_ref.dtype)
        out_ref[...] = out.astype(out_ref.dtype)
        if halves == 1:
            write(grad_refs[0])

    if halves == 2:

        @pl.when((step >= steps) & (step < steps + slabs // 2))
        def _():
            write(grad_refs[0])

        @pl.when(step >= steps + slabs // 2)
        def _():
            write(grad_refs[1])


def chunk_pass(order, halves, rows, cot, full, rows_turned, cot_turned, sums, last):
    count, depth = rows.shape
    width = full.shape[1]
    chunk = width // 3
    slabs = order.shape[0]
    height = depth // slabs
    steps = max(1, chunk // 256)
    added = sums is not None
    whole = pl.BlockSpec(memory_space=pltpu.VMEM)

    def place(i):
        return jnp.maximum(i - steps, 0)

    turned = pl.BlockSpec((height, count), lambda i, order: (order[place(i)], 0))
    column = pl.BlockSpec((count, height), lambda i, order: (0, order[place(i)]))
    if halves == 2:
        half = slabs // 2
        grad_shapes = [jax.ShapeDtypeStruct((half, height, width), BF)] * 2
        grad_specs = [
            pl.BlockSpec(
                (1, height, width), lambda i, order: (jnp.minimum(place(i), half - 1), 0, 0)
            ),
            pl.BlockSpec(
                (1, height, width), lambda i, order: (jnp.maximum(place(i) - half, 0), 0, 0)
            ),
        ]
    else:
        grad_shapes = [jax.ShapeDtypeStruct((depth, width), BF)]
        grad_specs = [pl.BlockSpec((height, width), lambda i, order: (order[place(i)], 0))]
    total = jax.ShapeDtypeStruct((count, depth), BF if last else F32)
    return pl.pallas_call(
        functools.partial(chunk_kernel, steps, slabs, halves, added, last),
        name="chunk_pass",
        out_shape=(*grad_shapes, total, total),
        grid_spec=pltpu.PrefetchScalarGridSpec(
            num_scalar_prefetch=1,
            grid=(steps + slabs,),
            in_specs=[whole, whole, whole, turned, turned] + [column] * (2 if added else 0),
            out_specs=(*grad_specs, column, column),
            scratch_shapes=[
                pltpu.VMEM((count, 2 * chunk), BF),
                pltpu.VMEM((count, chunk), BF),
            ],
        ),
        input_output_aliases={6: halves, 7: halves + 1} if added and not last else {},
        compiler_params=pltpu.CompilerParams(vmem_limit_bytes=56 << 20),
        cost_estimate=pl.CostEstimate(
            flops=6 * count * depth * width,
            bytes_accessed=8 * count * depth + 4 * depth * width + 16 * count * depth,
            transcendentals=count * chunk,
        ),
    )(order, rows, cot, full, rows_turned, cot_turned, *(sums if added else ()))


def pair_kernel(left_ref, first_ref, other_ref, second_ref, out_ref):
    width = first_ref.shape[1]
    out_ref[:, :width] = dot_tn(left_ref[...], first_ref[...]).astype(BF)
    out_ref[:, width:] = dot_tn(other_ref[...], second_ref[...]).astype(BF)


def pair_grads(left, first, other, second):
    count, depth = left.shape
    width = first.shape[1] + second.shape[1]
    height = 256
    whole = pl.BlockSpec(memory_space=pltpu.VMEM)
    column = pl.BlockSpec((count, height), lambda i: (0, i))
    return pl.pallas_call(
        pair_kernel,
        name="pair_grads",
        out_shape=jax.ShapeDtypeStruct((depth, width), BF),
        grid=(depth // height,),
        in_specs=[column, whole, column, whole],
        out_specs=pl.BlockSpec((height, width), lambda i: (i, 0)),
        compiler_params=pltpu.CompilerParams(vmem_limit_bytes=32 << 20),
        cost_estimate=pl.CostEstimate(
            flops=2 * count * depth * width,
            bytes_accessed=4 * count * depth + 2 * depth * width,
            transcendentals=0,
        ),
    )(left, first, other, second)


def on_z(pairs):
    return [(2 * a + core, 2 * b + core) for a, b in pairs for core in range(2)]


UP = [on_z([(z, z + 1) for z in range(count)]) for count in (1, 2, 3)]
DOWN = [on_z([(3 - z, 2 - z) for z in range(count)]) for count in (1, 2, 3)]
CORES = [(i, i ^ 1) for i in range(8)]
X_SWAP = [(i, i ^ 1) for i in range(4)]
Y_SWAP = [(i, i ^ 2) for i in range(4)]


def by_fsdp(value, pairs):
    return lax.ppermute(value, "fsdp", pairs)


def by_tp(value, pairs):
    return lax.ppermute(value, "tp", pairs)


def after(value, *earlier):
    return lax.optimization_barrier((value, *earlier))[0]


class Line:
    by_hops = True
    slabs = 8

    def __init__(self):
        place = lax.axis_index("fsdp")
        z, core = place // 2, place % 2
        self.rank = lax.axis_index("tp")
        self.order = jnp.stack(
            [((z + 4 - slot) % 4) * 2 + (core ^ other) for other in (1, 0) for slot in range(4)]
        ).astype(jnp.int32)

    def row_order(self, values):
        count = values.shape[0] // 4
        return jnp.concatenate(
            [lax.dynamic_slice_in_dim(values, (self.rank ^ p) * count, count, 0) for p in range(4)]
        )

    def trunk_base(self):
        return self.rank * TRUNK

    def sum_slabs(self, away, own):
        sums = own.astype(F32) + by_fsdp(away, CORES).astype(F32)
        low = sums.astype(BF)
        up = by_fsdp(low[1], UP[0])
        down = by_fsdp(low[3], DOWN[0])
        middle = (sums[2] + up.astype(F32) + down.astype(F32)).astype(BF)
        marks = [low, middle]
        up = by_fsdp(middle, UP[1])
        down = by_fsdp(middle, DOWN[1])
        up = (sums[3] + up.astype(F32)).astype(BF)
        down = (sums[1] + down.astype(F32)).astype(BF)
        marks.append(up)
        marks.append(down)
        up = by_fsdp(up, UP[2])
        down = by_fsdp(down, DOWN[2])
        return sums[0] + up.astype(F32) + down.astype(F32), marks

    def gather_rows(self, rows):
        half = rows.shape[0] // 2
        beside = by_tp(rows, X_SWAP)
        above = by_tp(rows, Y_SWAP)
        return jnp.concatenate(
            [rows, beside, above, by_tp(beside[:half], Y_SWAP), by_tp(above[half:], X_SWAP)]
        )

    def scatter_rows(self, partial):
        count = partial.shape[0] // 4
        half = count // 2
        own = partial[:count].astype(F32)
        beside = partial[count : 2 * count]
        above = partial[2 * count : 3 * count]
        far = partial[3 * count :].astype(BF)
        first = by_tp(far[:half], X_SWAP).astype(F32)
        second = by_tp(far[half:], Y_SWAP).astype(F32)
        above = jnp.concatenate([above[:half] + first, above[half:].astype(F32)]).astype(BF)
        beside = jnp.concatenate([beside[:half].astype(F32), beside[half:] + second]).astype(BF)
        return own + by_tp(beside, X_SWAP).astype(F32) + by_tp(above, Y_SWAP).astype(F32)


class Plain:
    by_hops = False
    slabs = 8

    def row_order(self, values):
        return values

    def trunk_base(self):
        return jnp.int32(0)

    def gather_rows(self, rows):
        return lax.all_gather(rows, "tp", axis=0, tiled=True)

    def scatter_rows(self, partial):
        return lax.psum_scatter(partial.astype(F32), "tp", scatter_dimension=0, tiled=True)


def gather_slabs(shard):
    return lax.all_gather(shard, "fsdp", axis=0, tiled=True)


def scatter_slabs(grads):
    return lax.psum_scatter(grads, "fsdp", scatter_dimension=0, tiled=True).astype(F32)


def rms_scale(row_values):
    return lax.rsqrt(jnp.mean(row_values * row_values, axis=-1, keepdims=True) + EPSILON)


def norm_back(row_values, row_scale, gain_values, grad_out):
    scaled_grad = grad_out * gain_values
    return row_scale * scaled_grad - row_values * row_scale**3 * jnp.mean(
        scaled_grad * row_values, axis=-1, keepdims=True
    )


def body(
    make_links,
    layer_input,
    cotangent,
    segment_ids,
    path_positions,
    ancestor_masks,
    attn_gain,
    query_weight,
    key_weight,
    value_weight,
    out_weight,
    mlp_gain,
    gate_weight,
    up_weight,
    down_weight,
):
    links = make_links()
    heads = query_weight.shape[1] // HD
    groups = key_weight.shape[1] // HD
    q_width, kv_width = heads * HD, groups * HD
    qkv_width = q_width + 2 * kv_width
    units = gate_weight.shape[1]
    edges = [units * sum(PARTS[:i]) // sum(PARTS) for i in range(len(PARTS) + 1)]

    gain_rows = gather_slabs(jnp.stack([attn_gain, mlp_gain], axis=1)).astype(F32)
    first_gain, second_gain = gain_rows[:, 0][None, :], gain_rows[:, 1][None, :]
    own_qkv = jnp.concatenate([query_weight, key_weight, value_weight], axis=1)
    attn_full = gather_slabs(jnp.concatenate([own_qkv, out_weight.T], axis=1))
    qkv_full, out_full = attn_full[:, :qkv_width], attn_full[:, qkv_width:]
    own_down = down_weight.T
    mlp_full = []
    for first, last in zip(edges[:-1], edges[1:]):
        cut = slice(first, last)
        mlp_full.append(
            gather_slabs(
                jnp.concatenate([gate_weight[:, cut], up_weight[:, cut], own_down[:, cut]], axis=1)
            )
        )

    positions = links.row_order(path_positions)
    angles = positions.astype(F32)[:, None] * jnp.asarray(inverse_freq(HD))[None, :]
    cosine, sine = jnp.cos(angles), jnp.sin(angles)
    cosine = jnp.concatenate([cosine] * 4, axis=1)
    sine = jnp.concatenate([-sine, sine] * 2, axis=1)
    segs = links.row_order(segment_ids)[::SEG]
    masks = ancestor_masks.reshape(SEGS * SEGS)
    base = jnp.reshape(links.trunk_base(), (1,)).astype(jnp.int32)

    inputs = layer_input.astype(F32)
    first_scale = rms_scale(inputs)
    first_normed = links.gather_rows((inputs * first_scale * first_gain).astype(BF))

    qkv_pre = dot_nn(first_normed, qkv_full)
    cot_all = links.gather_rows(after(cotangent, qkv_pre))
    attended, queries, keys, vals = attention_forward(
        heads, groups, masks, segs, base, qkv_pre, cosine, sine
    )
    residual = inputs + links.scatter_rows(dot_nt(attended, out_full))
    second_scale = rms_scale(residual)
    cot_turned = cot_all.T
    second_rows = (residual * second_scale * second_gain).astype(BF)
    second_normed = links.gather_rows(after(second_rows, cot_turned))

    second_turned = second_normed.T
    sums = None
    mlp_sums = []
    later = []
    for index, full in enumerate(mlp_full):
        halves = 2 if index < HOPS and links.by_hops else 1
        if later:
            full = after(full, later.pop(0))
        *grads, back_sum, out_sum = chunk_pass(
            links.order if halves == 2 else jnp.arange(links.slabs, dtype=jnp.int32),
            halves,
            second_normed,
            cot_all,
            full,
            second_turned,
            cot_turned,
            sums,
            index == len(mlp_full) - 1,
        )
        sums = (back_sum, out_sum)
        if halves == 2:
            part, later = links.sum_slabs(*grads)
        else:
            part = scatter_slabs(grads[0])
        mlp_sums.append(part)
    if later:
        back_sum = after(back_sum, *later)
    second_back = links.scatter_rows(back_sum)
    cot_float = cotangent.astype(F32)
    residual_back = cot_float + norm_back(residual, second_scale, second_gain, second_back)
    branch_back = links.gather_rows(residual_back.astype(BF))
    attended_back = dot_nn(branch_back, out_full).astype(BF)
    output = (residual + links.scatter_rows(out_sum)).astype(BF)
    qkv_back = attention_backward(
        heads, groups, masks, segs, base, queries, keys, vals, attended_back, cosine, sine
    )
    first_back = links.scatter_rows(dot_nt(qkv_back, qkv_full))
    attn_grads = pair_grads(first_normed, after(qkv_back, *mlp_sums), branch_back, attended)
    attn_sum = scatter_slabs(attn_grads)
    qkv_sum = attn_sum[:, :qkv_width]
    input_grad = residual_back + norm_back(inputs, first_scale, first_gain, first_back)

    thirds = [
        [part[:, at * part.shape[1] // 3 : (at + 1) * part.shape[1] // 3] for part in mlp_sums]
        for at in range(3)
    ]
    gate_sum, up_sum = jnp.concatenate(thirds[0], axis=1), jnp.concatenate(thirds[1], axis=1)
    down_sum = jnp.concatenate(thirds[2], axis=1).T
    attn_part = jnp.sum(own_qkv.astype(F32) * qkv_sum, axis=1)
    mlp_part = jnp.sum(
        gate_weight.astype(F32) * gate_sum + up_weight.astype(F32) * up_sum, axis=1
    )
    attn_total, mlp_total = lax.psum((attn_part, mlp_part), "tp")
    return (
        output,
        input_grad,
        attn_total / attn_gain.astype(F32),
        qkv_sum[:, :q_width],
        qkv_sum[:, q_width : q_width + kv_width],
        qkv_sum[:, q_width + kv_width :],
        attn_sum[:, qkv_width:].T,
        mlp_total / mlp_gain.astype(F32),
        gate_sum,
        up_sum,
        down_sum,
    )


def solution(mesh):
    fits = mesh.shape["fsdp"] == 8 and mesh.shape["tp"] == 4
    return jax.shard_map(
        functools.partial(body, Line if fits else Plain),
        mesh=mesh,
        in_specs=(
            P(("fsdp", "tp"), None),
            P(("fsdp", "tp"), None),
            P("fsdp"),
            P("fsdp"),
            P("fsdp", None, None),
            P("fsdp"),
            P("fsdp", "tp"),
            P("fsdp", "tp"),
            P("fsdp", "tp"),
            P("tp", "fsdp"),
            P("fsdp"),
            P("fsdp", "tp"),
            P("fsdp", "tp"),
            P("tp", "fsdp"),
        ),
        out_specs=(
            P(("fsdp", "tp"), None),
            P(("fsdp", "tp"), None),
            P("fsdp"),
            P("fsdp", "tp"),
            P("fsdp", "tp"),
            P("fsdp", "tp"),
            P("tp", "fsdp"),
            P("fsdp"),
            P("fsdp", "tp"),
            P("fsdp", "tp"),
            P("tp", "fsdp"),
        ),
        check_vma=False,
    )
```

time: 1440 us -> 700 us (0.49)
  waiting for transfers between devices: 967 us -> 266 us
  matrix products: 271 us -> 26.1 us
  Pallas kernels: 0 us -> 182 us
  local copies, waits for them, and re-layouts: 15.7 us -> 73.2 us
  starting transfers between devices: 0.98 us -> 58 us
  blocking collectives: 79.7 us -> 23.4 us
  other arithmetic: 83.3 us -> 49.6 us
    reduce_scatter x11 -> x3, waiting for transfers between devices: 593 us -> 24.5 us  [scatter_slabs(): lax.psum_scatter(grads, 'fsdp', scatter_dimension=0, tiled=True).astype(F32)]
    all_gather x9 -> x4, waiting for transfers between devices: 369 us -> 0.03 us  [gather_slabs(): return lax.all_gather(shard, 'fsdp', axis=0, tiled=True)]
    dot_general x39 -> x4, matrix products: 271 us -> 26.1 us  [the longest x2 13.7 us: dot_nt(): lax.dot_general(left, right, (((1,), (1,)), ((), ())), preferred_element_...]
    ppermute x0 -> x39, waiting for transfers between devices: none -> 241 us  [the longest x32 191 us: by_tp(): return lax.ppermute(value, 'tp', pairs)]
    pallas_call x0 -> x6, Pallas kernels: none -> 182 us  [the longest x3 120 us: chunk_pass(): pl.pallas_call(functools.partial(chunk_kernel, steps, slabs, halves, adde...]
    ppermute x0 -> x39, starting transfers between devices: none -> 57.7 us  [the longest x32 39.3 us: by_tp(): return lax.ppermute(value, 'tp', pairs)]
    all_gather x4 -> x1, blocking collectives: 53.7 us -> 13.6 us  [gather_slabs(): return lax.all_gather(shard, 'fsdp', axis=0, tiled=True)]
    convert_element_type x21 -> x6, other arithmetic: 51 us -> 15.7 us  [the longest x1 8.61 us: sum_slabs(): low = sums.astype(BF)]
  transfers between devices with their start and end apart: 20 -> 46, of which waited for: 18 -> 26; matrix products, arithmetic and copies ran while one was open for 20% -> 18% of each run, Pallas kernels for 0% -> 20%
where the time goes in v1:
time: 700 us; the launch traced here: 693 us
  waiting for transfers between devices  266 us (38%)
  Pallas kernels  182 us (26%)
  local copies, waits for them, and re-layouts  73.2 us (10%)
  starting transfers between devices  58 us (8%)
  other arithmetic  49.6 us (7%)
  matrix products  26.1 us (4%)
  blocking collectives  23.4 us (3%)
  between operations  15.4 us (2%)
    ppermute x32, waiting for transfers between devices, by_tp(): return lax.ppermute(value, 'tp', pairs)  191 us
    pallas_call x3, Pallas kernels, chunk_pass(): pl.pallas_call(functools.partial(chunk_kernel, steps, slabs, halves, adde...  120 us
    ppermute x7, waiting for transfers between devices, by_fsdp(): return lax.ppermute(value, 'fsdp', pairs)  49.5 us
    ppermute x32, starting transfers between devices, by_tp(): return lax.ppermute(value, 'tp', pairs)  39.3 us
    unnamed x122, local copies, waits for them, and re-layouts  35.9 us
    pallas_call x1, Pallas kernels, attention_backward(): pl.pallas_call(functools.partial(attn_bwd_kernel, heads, groups), name='a...  29.3 us
    reduce_scatter x3, waiting for transfers between devices, scatter_slabs(): lax.psum_scatter(grads, 'fsdp', scatter_dimension=0, tiled=True).astype(F32)  24.5 us
    pallas_call x1, Pallas kernels, attention_forward(): pl.pallas_call(functools.partial(attn_fwd_kernel, heads, groups), name='a...  23.8 us
  transfers between devices with their start and end apart: 46, of which 26 were waited for; matrix products, arithmetic and copies ran while one was open for 18% of the time, Pallas kernels for 20%

profile of v1, /device:TPU:0, one launch (start us, length us, event | category | flops | bytes accessed | tf_op | source)
XLA Modules:
  0.0 693.5 jit_solution(2957305113305997165)
XLA Ops:
  18.2 13.6 %all_gather.15 = bf16[2048,2]{0,1:T(2,128)(2,1)S(1)} all-gather(bf16[256,2]{0,1:T(2,128)(2,1)S(1)} %pad_maximum_fusion.16), channel_id=1, replica_groups=mesh['fsdp'=8,'tp'=4] {'fsdp'}, dimensions={0}, use_global_device_ids=true | all-gather | bytes 9216 | tf_op jit(solution)/shard_map/all_gather | solution.py:587
  40.4 19.6 %collective-permute-done = bf16[256,2048]{1,0:T(8,128)(2,1)S(1)} collective-permute-done((bf16[256,2048]{1,0:T(8,128)(2,1)}, bf16[256,2048]{1,0:T(8,128)(2,1)S(1)}, u32[]{:S(2)}, u32[]{:S(2)}) %collective-permute-start) | collective-permute-done | bytes 1048608 | tf_op jit(solution)/shard_map/ppermute | solution.py:502
  66.3 2.3 constant_dynamic-update-slice_fusion.2
  68.6 6.0 collective-permute-done.2
  77.7 6.9 fusion.2.pre_ref
  84.7 23.8 %attn_fwd.1 = (bf16[1024,512]{1,0:T(8,128)(2,1)S(1)}, bf16[2,16,256,64]{3,2,1,0:T(8,128)(2,1)S(1)}, bf16[2,1024,64]{2,1,0:T(8,128)(2,1)S(1)}, bf16[2,1024,64]{2,1,0:T(8,128)(2,1)S(1)}) custom-call(s32[169]{0:T(256)S(1)} %reshape.96.mask_ref, s32[16]{0:T(128)S(1)} %slice.255.seg_ref, s32[1]{0:T(128)} %bitcast.base_ref, f32[1024,768]{1,0:T(8,128)S(1)} %fusion.2.pre_ref, ...), custom_call_target="tpu_custom_call" | custom-call | flops 8000000000 | bytes 8000000 | tf_op jit(solution)/shard_map/attn_fwd/pallas_call | solution.py:302
  108.5 8.3 %fusion.52 = (bf16[1024,2048]{1,0:T(8,128)(2,1)S(1)}, f32[1024,2048]{1,0:T(8,128)}) fusion(bf16[1024,512]{1,0:T(8,128)(2,1)S(1)} %get-tuple-element.31.second_ref, bf16[2048,1280]{0,1:T(8,128)(2,1)} %all-gather.5.cloned.1.call-done), kind=kOutput, calls=%fused_computation.130 | convolution fusion | flops 2149580800 | bytes 15728640 | tf_op jit(solution)/shard_map/dot_general | solution.py:43
  120.7 2.3 copy.64
  124.5 8.9 %collective-permute-done.4 = bf16[128,2048]{1,0:T(8,128)(2,1)} collective-permute-done((bf16[128,2048]{1,0:T(8,128)(2,1)}, bf16[128,2048]{1,0:T(8,128)(2,1)}, u32[]{:S(2)}, u32[]{:S(2)}) %collective-permute-start.4) | collective-permute-done | bytes 524320 | tf_op jit(solution)/shard_map/ppermute | solution.py:502
  139.6 17.2 %collective-permute-done.8 = bf16[256,2048]{0,1:T(8,128)(2,1)S(1)} collective-permute-done((bf16[256,2048]{0,1:T(8,128)(2,1)}, bf16[256,2048]{0,1:T(8,128)(2,1)S(1)}, u32[]{:S(2)}, u32[]{:S(2)}) %collective-permute-start.8) | collective-permute-done | bytes 1048608 | tf_op jit(solution)/shard_map/ppermute | solution.py:502
  159.8 19.5 %collective-permute-done.5 = bf16[256,2048]{1,0:T(8,128)(2,1)S(1)} collective-permute-done((bf16[256,2048]{1,0:T(8,128)(2,1)S(1)}, bf16[256,2048]{1,0:T(8,128)(2,1)S(1)}, u32[]{:S(2)}, u32[]{:S(2)}) %collective-permute-start.5) | collective-permute-done | bytes 1048608 | tf_op jit(solution)/shard_map/ppermute | solution.py:502
  179.2 2.3 multiply_reduce_fusion.1
  181.6 4.8 collective-permute-done.10
  192.8 17.4 %collective-permute-done.12 = bf16[256,2048]{1,0:T(8,128)(2,1)} collective-permute-done((bf16[256,2048]{1,0:T(8,128)(2,1)S(1)}, bf16[256,2048]{1,0:T(8,128)(2,1)}, u32[]{:S(2)}, u32[]{:S(2)}) %collective-permute-start.12) | collective-permute-done | bytes 1048608 | tf_op jit(solution)/shard_map/ppermute | solution.py:502
  213.9 6.5 copy.70.refs_1_
  223.1 2.3 constant_dynamic-update-slice_fusion.13
  225.4 2.3 constant_dynamic-update-slice_fusion.12
  232.2 6.4 copy.67.refs_3_
  238.6 44.3 %chunk_pass.3 = (bf16[4,256,2304]{2,1,0:T(8,128)(2,1)}, bf16[4,256,2304]{2,1,0:T(8,128)(2,1)}, f32[1024,2048]{1,0:T(8,128)}, f32[1024,2048]{1,0:T(8,128)}) custom-call(s32[8]{0:T(128)} %stack.47.order_ref, bf16[1024,2048]{1,0:T(8,128)(2,1)} %constant_dynamic-update-slice_fusion.10.refs_0_, bf16[1024,2048]{1,0:T(8,128)(2,1)} %copy.70.refs_1_, ...), custom_call_target="tpu_custom_call" | custom-call | flops 28991029248 | bytes 69206016 | tf_op jit(solution)/shard_map/chunk_pass/pallas_call | solution.py:434
  283.0 8.7 %collective-permute-done.16 = bf16[4,256,2304]{2,1,0:T(8,128)(2,1)S(1)} collective-permute-done((bf16[4,256,2304]{2,1,0:T(8,128)(2,1)}, bf16[4,256,2304]{2,1,0:T(8,128)(2,1)S(1)}, u32[]{:S(2)}, u32[]{:S(2)}) %collective-permute-start.16) | collective-permute-done | bytes 4718624 | tf_op jit(solution)/shard_map/ppermute | solution.py:498
  291.6 2.2 copy-done.20
  293.8 8.6 %fusion.36 = (bf16[4,256,2304]{2,1,0:T(8,128)(2,1)S(1)}, f32[4,256,2304]{2,1,0:T(8,128)}) fusion(bf16[4,256,2304]{2,1,0:T(8,128)(2,1)} %copy-done.20, bf16[4,256,2304]{2,1,0:T(8,128)(2,1)} %get-tuple-element.34), kind=kLoop, calls=%fused_computation.115 | loop fusion | flops 9437184 | bytes 23592960 | tf_op jit(solution)/shard_map/convert_element_type | solution.py:532
  307.6 43.2 %chunk_pass.4 = (bf16[2048,2304]{1,0:T(8,128)(2,1)}, f32[1024,2048]{1,0:T(8,128)}, f32[1024,2048]{1,0:T(8,128)}) custom-call(s32[8]{0:T(128)} %iota.7.order_ref, bf16[1024,2048]{1,0:T(8,128)(2,1)} %constant_dynamic-update-slice_fusion.10.refs_0_, bf16[1024,2048]{1,0:T(8,128)(2,1)} %copy.70.refs_1_, ...), custom_call_target="tpu_custom_call", output_to_operand_aliasing={{1}: (6, {}), {2}: (7, {})} | custom-call | flops 28991029248 | bytes 69206016 | tf_op jit(solution)/shard_map/chunk_pass/pallas_call | solution.py:434
  351.8 2.7 fusion.12
  355.1 32.9 %chunk_pass.5 = (bf16[2048,1536]{1,0:T(8,128)(2,1)}, bf16[1024,2048]{1,0:T(8,128)(2,1)}, bf16[1024,2048]{1,0:T(8,128)(2,1)}) custom-call(s32[8]{0:T(128)} %iota.6.order_ref, bf16[1024,2048]{1,0:T(8,128)(2,1)} %constant_dynamic-update-slice_fusion.10.refs_0_, bf16[1024,2048]{1,0:T(8,128)(2,1)} %copy.70.refs_1_, ...), custom_call_target="tpu_custom_call" | custom-call | flops 19327352832 | bytes 62914560 | tf_op jit(solution)/shard_map/chunk_pass/pallas_call | solution.py:434
  395.1 40.8 %collective-permute-done.23 = bf16[256,2304]{1,0:T(8,128)(2,1)S(1)} collective-permute-done((bf16[256,2304]{1,0:T(8,128)(2,1)S(1)}, bf16[256,2304]{1,0:T(8,128)(2,1)S(1)}, u32[]{:S(2)}, u32[]{:S(2)}) %collective-permute-start.23) | collective-permute-done | bytes 1179680 | tf_op jit(solution)/shard_map/ppermute | solution.py:498
  435.9 2.9 fusion.7
  443.9 10.1 %collective-permute-done.25 = bf16[128,2048]{1,0:T(8,128)(2,1)S(1)} collective-permute-done((bf16[128,2048]{1,0:T(8,128)(2,1)S(1)}, bf16[128,2048]{1,0:T(8,128)(2,1)S(1)}, u32[]{:S(2)}, u32[]{:S(2)}) %collective-permute-start.25) | collective-permute-done | bytes 524320 | tf_op jit(solution)/shard_map/ppermute | solution.py:502
  457.9 11.9 %collective-permute-start.37 = (bf16[256,2304]{1,0:T(8,128)(2,1)S(1)}, bf16[256,2304]{1,0:T(8,128)(2,1)S(1)}, u32[]{:S(2)}, u32[]{:S(2)}) collective-permute-start(bf16[256,2304]{1,0:T(8,128)(2,1)S(1)} %get-tuple-element.97), channel_id=1, source_target_pairs={{0,8},{4,12},{8,16},{12,20},{16,24},{20,28},{1,9},{5,13},{9,17},{1... | collective-permute-start | bytes 3538952 | tf_op jit(solution)/shard_map/ppermute | solution.py:498
  469.8 6.9 collective-permute-done.20
  477.9 18.6 %collective-permute-done.26 = bf16[256,2048]{1,0:T(8,128)(2,1)S(1)} collective-permute-done((bf16[256,2048]{1,0:T(8,128)(2,1)S(1)}, bf16[256,2048]{1,0:T(8,128)(2,1)S(1)}, u32[]{:S(2)}, u32[]{:S(2)}) %collective-permute-start.26) | collective-permute-done | bytes 1048608 | tf_op jit(solution)/shard_map/ppermute | solution.py:502
  498.7 2.3 constant_dynamic-update-slice_fusion.19
  503.8 19.8 %collective-permute-done.29 = bf16[256,2048]{1,0:T(8,128)(2,1)S(1)} collective-permute-done((bf16[256,2048]{1,0:T(8,128)(2,1)S(1)}, bf16[256,2048]{1,0:T(8,128)(2,1)S(1)}, u32[]{:S(2)}, u32[]{:S(2)}) %collective-permute-start.29) | collective-permute-done | bytes 1048608 | tf_op jit(solution)/shard_map/ppermute | solution.py:502
  525.2 3.4 fusion.5
  530.1 5.7 collective-permute-done.31
  535.8 3.2 collective-permute-done.32
  539.0 5.5 fusion.27.grad_ref
  544.6 29.3 %attn_bwd.1.first_ref = bf16[1024,768]{1,0:T(8,128)(2,1)S(1)} custom-call(s32[169]{0:T(256)S(1)} %reshape.96.mask_ref, s32[16]{0:T(128)S(1)} %slice.255.seg_ref, s32[1]{0:T(128)} %bitcast.base_ref, bf16[2,16,256,64]{3,2,1,0:T(8,128)(2,1)S(1)} %copy-done.10, bf16[2,1024,64]{2,1,0:T(8,128)(2,1)S(1)} %get-tuple-element.46.k_ref, ...), custom_call_target="tpu_custom_call" | custom-call | flops 20000000000 | bytes 8000000 | tf_op jit(solution)/shard_map/attn_bwd/pallas_call | solution.py:324
  575.1 22.2 %reduce-scatter.4.cloned.1.call-done = bf16[256,2304]{1,0:T(8,128)(2,1)} async-done(((bf16[2048,2304]{1,0:T(8,128)(2,1)}), bf16[256,2304]{1,0:T(8,128)(2,1)}) %reduce-scatter.4.cloned.1.call-update) | async-done | bytes 1179664 | tf_op jit(solution)/shard_map/reduce_scatter | solution.py:591
  603.1 8.4 %pair_grads.1 = bf16[2048,1280]{1,0:T(8,128)(2,1)S(1)} custom-call(bf16[1024,2048]{1,0:T(8,128)(2,1)S(1)} %copy-done.3, bf16[1024,768]{1,0:T(8,128)(2,1)S(1)} %copy-done.7, bf16[1024,2048]{1,0:T(8,128)(2,1)S(1)} %copy-done.5, bf16[1024,512]{1,0:T(8,128)(2,1)S(1)} %copy-done.2), custom_call_target="tpu_custom_call" | custom-call | flops 5368709120 | bytes 13631488 | tf_op jit(solution)/shard_map/pair_grads/pallas_call | solution.py:470
  611.5 2.4 copy-done
  615.3 5.3 fusion.53
  622.7 9.4 %collective-permute-done.33 = bf16[128,2048]{1,0:T(8,128)(2,1)S(1)} collective-permute-done((bf16[128,2048]{1,0:T(8,128)(2,1)S(1)}, bf16[128,2048]{1,0:T(8,128)(2,1)S(1)}, u32[]{:S(2)}, u32[]{:S(2)}) %collective-permute-start.33) | collective-permute-done | bytes 524320 | tf_op jit(solution)/shard_map/ppermute | solution.py:502
  637.7 18.3 %collective-permute-done.34 = bf16[256,2048]{1,0:T(8,128)(2,1)S(1)} collective-permute-done((bf16[256,2048]{1,0:T(8,128)(2,1)S(1)}, bf16[256,2048]{1,0:T(8,128)(2,1)S(1)}, u32[]{:S(2)}, u32[]{:S(2)}) %collective-permute-start.34) | collective-permute-done | bytes 1048608 | tf_op jit(solution)/shard_map/ppermute | solution.py:502
  656.8 2.2 fusion.18
  664.0 5.1 add_reduce_fusion
  669.1 2.2 reduce-scatter.8.cloned.1.call-done
  672.8 9.9 %all-reduce = (f32[256]{0:T(256)S(1)}, f32[256]{0:T(256)S(1)}) all-reduce(f32[256]{0:T(256)S(1)} %fusion.34, f32[256]{0:T(256)S(1)} %get-tuple-element.86), channel_id=1, replica_groups=mesh['fsdp'=8,'tp'=4] {'tp'}, use_global_device_ids=true, to_apply=%region_8.9 | all-reduce | flops 512 | bytes 4096 | tf_op jit(solution)/shard_map/psum | solution.py:721
  (272 shorter events, 119.4 us)
Async XLA Ops:
  7.2 70.6 %all-gather.5.cloned.1.call-start = ((), (), s32[]{:S(2)}) async-start(), calls=%async_computation.3 | async-start | bytes 5898240 | tf_op jit(solution)/shard_map/all_gather | solution.py:587
  12.1 226.5 %all-gather.9.cloned.1.call-start = ((), (), s32[]{:S(2)}) async-start(), calls=%async_computation.5 | async-start | bytes 10616832 | tf_op jit(solution)/shard_map/all_gather | solution.py:587
  16.6 290.5 %all-gather.11.cloned.1.call-start = ((), (), s32[]{:S(2)}) async-start(), calls=%async_computation.6 | async-start | bytes 10616832 | tf_op jit(solution)/shard_map/all_gather | solution.py:587
  18.1 336.5 %all-gather.7.cloned.1.call-start = ((), (), s32[]{:S(2)}) async-start(), calls=%async_computation.4 | async-start | bytes 7077888 | tf_op jit(solution)/shard_map/all_gather | solution.py:587
  34.4 25.6 %collective-permute-start = (bf16[256,2048]{1,0:T(8,128)(2,1)}, bf16[256,2048]{1,0:T(8,128)(2,1)S(1)}, u32[]{:S(2)}, u32[]{:S(2)}) collective-permute-start(bf16[256,2048]{1,0:T(8,128)(2,1)} %get-tuple-element.95), channel_id=1, source_target_pairs={{0,1},{1,0},{2,3},{3,2},{4,5},{5,4},{6,7},{7,6},{8,9},{9,8},{10,11... | collective-permute-start | bytes 3145736 | tf_op jit(solution)/shard_map/ppermute | solution.py:502
  35.9 26.7 %collective-permute-start.1 = (bf16[256,2048]{1,0:T(8,128)(2,1)}, bf16[256,2048]{1,0:T(8,128)(2,1)}, u32[]{:S(2)}, u32[]{:S(2)}) collective-permute-start(bf16[256,2048]{1,0:T(8,128)(2,1)} %get-tuple-element.95), channel_id=1, source_target_pairs={{0,2},{1,3},{2,0},{3,1},{4,6},{5,7},{6,4},{7,5},{8,10},{9,11},{10,... | collective-permute-start | bytes 3145736 | tf_op jit(solution)/shard_map/ppermute | solution.py:502
  60.8 13.8 %collective-permute-start.2 = (bf16[128,2048]{1,0:T(8,128)(2,1)}, bf16[128,2048]{1,0:T(8,128)(2,1)}, u32[]{:S(2)}, u32[]{:S(2)}) collective-permute-start(bf16[128,2048]{1,0:T(8,128)(2,1)} %slice.326), channel_id=1, source_target_pairs={{0,2},{1,3},{2,0},{3,1},{4,6},{5,7},{6,4},{7,5},{8,10},{9,11},{10,... | collective-permute-start | bytes 1572872 | tf_op jit(solution)/shard_map/ppermute | solution.py:502
  63.7 13.2 %collective-permute-start.3 = (bf16[128,2048]{1,0:T(8,128)(2,1)S(1)}, bf16[128,2048]{1,0:T(8,128)(2,1)S(1)}, u32[]{:S(2)}, u32[]{:S(2)}) collective-permute-start(bf16[128,2048]{1,0:T(8,128)(2,1)S(1)} %slice.327), channel_id=1, source_target_pairs={{0,1},{1,0},{2,3},{3,2},{4,5},{5,4},{6,7},{7,6},{8,9},{9,8},{10,11... | collective-permute-start | bytes 1572872 | tf_op jit(solution)/shard_map/ppermute | solution.py:502
  118.2 15.2 %collective-permute-start.4 = (bf16[128,2048]{1,0:T(8,128)(2,1)}, bf16[128,2048]{1,0:T(8,128)(2,1)}, u32[]{:S(2)}, u32[]{:S(2)}) collective-permute-start(bf16[128,2048]{1,0:T(8,128)(2,1)} %get-tuple-element.125), channel_id=1, source_target_pairs={{0,2},{1,3},{2,0},{3,1},{4,6},{5,7},{6,4},{7,5},{8,10},{9,11},{10,... | collective-permute-start | bytes 1572872 | tf_op jit(solution)/shard_map/ppermute | solution.py:502
  119.2 15.2 %collective-permute-start.6 = (bf16[128,2048]{1,0:T(8,128)(2,1)}, bf16[128,2048]{1,0:T(8,128)(2,1)}, u32[]{:S(2)}, u32[]{:S(2)}) collective-permute-start(bf16[128,2048]{1,0:T(8,128)(2,1)} %get-tuple-element.124), channel_id=1, source_target_pairs={{0,1},{1,0},{2,3},{3,2},{4,5},{5,4},{6,7},{7,6},{8,9},{9,8},{10,11... | collective-permute-start | bytes 1572872 | tf_op jit(solution)/shard_map/ppermute | solution.py:502
  123.0 33.8 %collective-permute-start.8 = (bf16[256,2048]{0,1:T(8,128)(2,1)}, bf16[256,2048]{0,1:T(8,128)(2,1)S(1)}, u32[]{:S(2)}, u32[]{:S(2)}) collective-permute-start(bf16[256,2048]{0,1:T(8,128)(2,1)} %copy.64), channel_id=1, source_target_pairs={{0,1},{1,0},{2,3},{3,2},{4,5},{5,4},{6,7},{7,6},{8,9},{9,8},{10,11... | collective-permute-start | bytes 3145736 | tf_op jit(solution)/shard_map/ppermute | solution.py:502
  123.5 34.4 %collective-permute-start.9 = (bf16[256,2048]{0,1:T(8,128)(2,1)}, bf16[256,2048]{0,1:T(8,128)(2,1)S(1)}, u32[]{:S(2)}, u32[]{:S(2)}) collective-permute-start(bf16[256,2048]{0,1:T(8,128)(2,1)} %copy.64), channel_id=1, source_target_pairs={{0,2},{1,3},{2,0},{3,1},{4,6},{5,7},{6,4},{7,5},{8,10},{9,11},{10,... | collective-permute-start | bytes 3145736 | tf_op jit(solution)/shard_map/ppermute | solution.py:502
  136.7 42.5 %collective-permute-start.5 = (bf16[256,2048]{1,0:T(8,128)(2,1)S(1)}, bf16[256,2048]{1,0:T(8,128)(2,1)S(1)}, u32[]{:S(2)}, u32[]{:S(2)}) collective-permute-start(bf16[256,2048]{1,0:T(8,128)(2,1)S(1)} %pad_maximum_fusion.4), channel_id=1, source_target_pairs={{0,1},{1,0},{2,3},{3,2},{4,5},{5,4},{6,7},{7,6},{8,9},{9,8},{10,11... | collective-permute-start | bytes 3145736 | tf_op jit(solution)/shard_map/ppermute | solution.py:502
  138.4 40.9 %collective-permute-start.7 = (bf16[256,2048]{1,0:T(8,128)(2,1)S(1)}, bf16[256,2048]{1,0:T(8,128)(2,1)S(1)}, u32[]{:S(2)}, u32[]{:S(2)}) collective-permute-start(bf16[256,2048]{1,0:T(8,128)(2,1)S(1)} %pad_maximum_fusion.5), channel_id=1, source_target_pairs={{0,2},{1,3},{2,0},{3,1},{4,6},{5,7},{6,4},{7,5},{8,10},{9,11},{10,... | collective-permute-start | bytes 3145736 | tf_op jit(solution)/shard_map/ppermute | solution.py:502
  156.8 29.6 %collective-permute-start.10 = (bf16[128,2048]{0,1:T(8,128)(2,1)S(1)}, bf16[128,2048]{0,1:T(8,128)(2,1)S(1)}, u32[]{:S(2)}, u32[]{:S(2)}) collective-permute-start(bf16[128,2048]{0,1:T(8,128)(2,1)S(1)} %slice.338), channel_id=1, source_target_pairs={{0,2},{1,3},{2,0},{3,1},{4,6},{5,7},{6,4},{7,5},{8,10},{9,11},{10,... | collective-permute-start | bytes 1572872 | tf_op jit(solution)/shard_map/ppermute | solution.py:502
  157.9 29.4 %collective-permute-start.11 = (bf16[128,2048]{0,1:T(8,128)(2,1)S(1)}, bf16[128,2048]{0,1:T(8,128)(2,1)S(1)}, u32[]{:S(2)}, u32[]{:S(2)}) collective-permute-start(bf16[128,2048]{0,1:T(8,128)(2,1)S(1)} %slice.339), channel_id=1, source_target_pairs={{0,1},{1,0},{2,3},{3,2},{4,5},{5,4},{6,7},{7,6},{8,9},{9,8},{10,11... | collective-permute-start | bytes 1572872 | tf_op jit(solution)/shard_map/ppermute | solution.py:502
  187.8 22.3 %collective-permute-start.12 = (bf16[256,2048]{1,0:T(8,128)(2,1)S(1)}, bf16[256,2048]{1,0:T(8,128)(2,1)}, u32[]{:S(2)}, u32[]{:S(2)}) collective-permute-start(bf16[256,2048]{1,0:T(8,128)(2,1)S(1)} %multiply_convert_fusion), channel_id=1, source_target_pairs={{0,1},{1,0},{2,3},{3,2},{4,5},{5,4},{6,7},{7,6},{8,9},{9,8},{10,11... | collective-permute-start | bytes 3145736 | tf_op jit(solution)/shard_map/ppermute | solution.py:502
  189.4 31.0 %collective-permute-start.13 = (bf16[256,2048]{1,0:T(8,128)(2,1)S(1)}, bf16[256,2048]{1,0:T(8,128)(2,1)}, u32[]{:S(2)}, u32[]{:S(2)}) collective-permute-start(bf16[256,2048]{1,0:T(8,128)(2,1)S(1)} %multiply_convert_fusion), channel_id=1, source_target_pairs={{0,2},{1,3},{2,0},{3,1},{4,6},{5,7},{6,4},{7,5},{8,10},{9,11},{10,... | collective-permute-start | bytes 3145736 | tf_op jit(solution)/shard_map/ppermute | solution.py:502
  192.0 383.0 %reduce-scatter.6.cloned.1.call-start = ((), (), s32[]{:S(2)}) async-start(), calls=%async_computation.8 | async-start | bytes 7077888 | tf_op jit(solution)/shard_map/reduce_scatter | solution.py:591
  212.1 15.6 %collective-permute-start.14 = (bf16[128,2048]{1,0:T(8,128)(2,1)}, bf16[128,2048]{1,0:T(8,128)(2,1)}, u32[]{:S(2)}, u32[]{:S(2)}) collective-permute-start(bf16[128,2048]{1,0:T(8,128)(2,1)} %slice.340), channel_id=1, source_target_pairs={{0,2},{1,3},{2,0},{3,1},{4,6},{5,7},{6,4},{7,5},{8,10},{9,11},{10,... | collective-permute-start | bytes 1572872 | tf_op jit(solution)/shard_map/ppermute | solution.py:502
  221.5 9.9 %collective-permute-start.15 = (bf16[128,2048]{1,0:T(8,128)(2,1)S(1)}, bf16[128,2048]{1,0:T(8,128)(2,1)S(1)}, u32[]{:S(2)}, u32[]{:S(2)}) collective-permute-start(bf16[128,2048]{1,0:T(8,128)(2,1)S(1)} %slice.341), channel_id=1, source_target_pairs={{0,1},{1,0},{2,3},{3,2},{4,5},{5,4},{6,7},{7,6},{8,9},{9,8},{10,11... | collective-permute-start | bytes 1572872 | tf_op jit(solution)/shard_map/ppermute | solution.py:502
  282.9 8.7 %collective-permute-start.16 = (bf16[4,256,2304]{2,1,0:T(8,128)(2,1)}, bf16[4,256,2304]{2,1,0:T(8,128)(2,1)S(1)}, u32[]{:S(2)}, u32[]{:S(2)}) collective-permute-start(bf16[4,256,2304]{2,1,0:T(8,128)(2,1)} %get-tuple-element.35), channel_id=1, source_target_pairs={{0,4},{4,0},{8,12},{12,8},{16,20},{20,16},{24,28},{28,24},{1,5},{5... | collective-permute-start | bytes 14155784 | tf_op jit(solution)/shard_map/ppermute | solution.py:498
  304.0 46.8 %collective-permute-start.17 = (bf16[256,2304]{1,0:T(8,128)(2,1)}, bf16[256,2304]{1,0:T(8,128)(2,1)S(1)}, u32[]{:S(2)}, u32[]{:S(2)}) collective-permute-start(bf16[256,2304]{1,0:T(8,128)(2,1)} %get-tuple-element.104), channel_id=1, source_target_pairs={{0,8},{4,12},{1,9},{5,13},{2,10},{6,14},{3,11},{7,15}} | collective-permute-start | bytes 3538952 | tf_op jit(solution)/shard_map/ppermute | solution.py:498
  305.4 45.4 %collective-permute-start.18 = (bf16[256,2304]{1,0:T(8,128)(2,1)}, bf16[256,2304]{1,0:T(8,128)(2,1)}, u32[]{:S(2)}, u32[]{:S(2)}) collective-permute-start(bf16[256,2304]{1,0:T(8,128)(2,1)} %get-tuple-element.105), channel_id=1, source_target_pairs={{24,16},{28,20},{25,17},{29,21},{26,18},{30,22},{27,19},{31,23}} | collective-permute-start | bytes 3538952 | tf_op jit(solution)/shard_map/ppermute | solution.py:498
  388.0 209.4 %reduce-scatter.4.cloned.1.call-start = ((), (), s32[]{:S(2)}) async-start(), calls=%async_computation.7 | async-start | bytes 10616832 | tf_op jit(solution)/shard_map/reduce_scatter | solution.py:591
  388.5 282.8 %reduce-scatter.8.cloned.1.call-start = ((), (), s32[]{:S(2)}) async-start(), calls=%async_computation.9 | async-start | bytes 5898240 | tf_op jit(solution)/shard_map/reduce_scatter | solution.py:591
  388.6 47.3 %collective-permute-start.23 = (bf16[256,2304]{1,0:T(8,128)(2,1)S(1)}, bf16[256,2304]{1,0:T(8,128)(2,1)S(1)}, u32[]{:S(2)}, u32[]{:S(2)}) collective-permute-start(bf16[256,2304]{1,0:T(8,128)(2,1)S(1)} %fusion.12), channel_id=1, source_target_pairs={{0,8},{4,12},{8,16},{12,20},{1,9},{5,13},{9,17},{13,21},{2,10},{6,... | collective-permute-start | bytes 3538952 | tf_op jit(solution)/shard_map/ppermute | solution.py:498
  390.0 45.9 %collective-permute-start.24 = (bf16[256,2304]{1,0:T(8,128)(2,1)S(1)}, bf16[256,2304]{1,0:T(8,128)(2,1)S(1)}, u32[]{:S(2)}, u32[]{:S(2)}) collective-permute-start(bf16[256,2304]{1,0:T(8,128)(2,1)S(1)} %fusion.12), channel_id=1, source_target_pairs={{24,16},{28,20},{16,8},{20,12},{25,17},{29,21},{17,9},{21,13},{26,... | collective-permute-start | bytes 3538952 | tf_op jit(solution)/shard_map/ppermute | solution.py:498
  392.5 48.5 %collective-permute-start.19 = (bf16[128,2048]{1,0:T(8,128)(2,1)S(1)}, bf16[128,2048]{1,0:T(8,128)(2,1)S(1)}, u32[]{:S(2)}, u32[]{:S(2)}) collective-permute-start(bf16[128,2048]{1,0:T(8,128)(2,1)S(1)} %get-tuple-element.119), channel_id=1, source_target_pairs={{0,2},{1,3},{2,0},{3,1},{4,6},{5,7},{6,4},{7,5},{8,10},{9,11},{10,... | collective-permute-start | bytes 1572872 | tf_op jit(solution)/shard_map/ppermute | solution.py:502
  393.6 45.2 %copy-start.18 = (bf16[1024,2048]{1,0:T(8,128)(2,1)S(1)}, bf16[1024,2048]{1,0:T(8,128)(2,1)}, u32[]{:S(2)}) copy-start(bf16[1024,2048]{1,0:T(8,128)(2,1)} %get-tuple-element.44) | copy-start | bytes 12582916
  393.6 47.4 %collective-permute-start.21 = (bf16[128,2048]{1,0:T(8,128)(2,1)S(1)}, bf16[128,2048]{1,0:T(8,128)(2,1)S(1)}, u32[]{:S(2)}, u32[]{:S(2)}) collective-permute-start(bf16[128,2048]{1,0:T(8,128)(2,1)S(1)} %get-tuple-element.118), channel_id=1, source_target_pairs={{0,1},{1,0},{2,3},{3,2},{4,5},{5,4},{6,7},{7,6},{8,9},{9,8},{10,11... | collective-permute-start | bytes 1572872 | tf_op jit(solution)/shard_map/ppermute | solution.py:502
  439.0 14.9 %collective-permute-start.25 = (bf16[128,2048]{1,0:T(8,128)(2,1)S(1)}, bf16[128,2048]{1,0:T(8,128)(2,1)S(1)}, u32[]{:S(2)}, u32[]{:S(2)}) collective-permute-start(bf16[128,2048]{1,0:T(8,128)(2,1)S(1)} %get-tuple-element.113), channel_id=1, source_target_pairs={{0,2},{1,3},{2,0},{3,1},{4,6},{5,7},{6,4},{7,5},{8,10},{9,11},{10,... | collective-permute-start | bytes 1572872 | tf_op jit(solution)/shard_map/ppermute | solution.py:502
  439.3 14.9 %collective-permute-start.27 = (bf16[128,2048]{1,0:T(8,128)(2,1)S(1)}, bf16[128,2048]{1,0:T(8,128)(2,1)S(1)}, u32[]{:S(2)}, u32[]{:S(2)}) collective-permute-start(bf16[128,2048]{1,0:T(8,128)(2,1)S(1)} %get-tuple-element.112), channel_id=1, source_target_pairs={{0,1},{1,0},{2,3},{3,2},{4,5},{5,4},{6,7},{7,6},{8,9},{9,8},{10,11... | collective-permute-start | bytes 1572872 | tf_op jit(solution)/shard_map/ppermute | solution.py:502
  441.5 35.1 %collective-permute-start.20 = (bf16[256,2048]{1,0:T(8,128)(2,1)S(1)}, bf16[256,2048]{1,0:T(8,128)(2,1)S(1)}, u32[]{:S(2)}, u32[]{:S(2)}) collective-permute-start(bf16[256,2048]{1,0:T(8,128)(2,1)S(1)} %pad_maximum_fusion.6), channel_id=1, source_target_pairs={{0,1},{1,0},{2,3},{3,2},{4,5},{5,4},{6,7},{7,6},{8,9},{9,8},{10,11... | collective-permute-start | bytes 3145736 | tf_op jit(solution)/shard_map/ppermute | solution.py:502
  442.8 35.1 %collective-permute-start.22 = (bf16[256,2048]{1,0:T(8,128)(2,1)S(1)}, bf16[256,2048]{1,0:T(8,128)(2,1)S(1)}, u32[]{:S(2)}, u32[]{:S(2)}) collective-permute-start(bf16[256,2048]{1,0:T(8,128)(2,1)S(1)} %pad_maximum_fusion.7), channel_id=1, source_target_pairs={{0,2},{1,3},{2,0},{3,1},{4,6},{5,7},{6,4},{7,5},{8,10},{9,11},{10,... | collective-permute-start | bytes 3145736 | tf_op jit(solution)/shard_map/ppermute | solution.py:502
  454.6 41.9 %collective-permute-start.26 = (bf16[256,2048]{1,0:T(8,128)(2,1)S(1)}, bf16[256,2048]{1,0:T(8,128)(2,1)S(1)}, u32[]{:S(2)}, u32[]{:S(2)}) collective-permute-start(bf16[256,2048]{1,0:T(8,128)(2,1)S(1)} %pad_maximum_fusion.8), channel_id=1, source_target_pairs={{0,1},{1,0},{2,3},{3,2},{4,5},{5,4},{6,7},{7,6},{8,9},{9,8},{10,11... | collective-permute-start | bytes 3145736 | tf_op jit(solution)/shard_map/ppermute | solution.py:502
  456.5 40.0 %collective-permute-start.28 = (bf16[256,2048]{1,0:T(8,128)(2,1)S(1)}, bf16[256,2048]{1,0:T(8,128)(2,1)S(1)}, u32[]{:S(2)}, u32[]{:S(2)}) collective-permute-start(bf16[256,2048]{1,0:T(8,128)(2,1)S(1)} %pad_maximum_fusion.9), channel_id=1, source_target_pairs={{0,2},{1,3},{2,0},{3,1},{4,6},{5,7},{6,4},{7,5},{8,10},{9,11},{10,... | collective-permute-start | bytes 3145736 | tf_op jit(solution)/shard_map/ppermute | solution.py:502
  457.9 67.4 %collective-permute-start.37 = (bf16[256,2304]{1,0:T(8,128)(2,1)S(1)}, bf16[256,2304]{1,0:T(8,128)(2,1)S(1)}, u32[]{:S(2)}, u32[]{:S(2)}) collective-permute-start(bf16[256,2304]{1,0:T(8,128)(2,1)S(1)} %get-tuple-element.97), channel_id=1, source_target_pairs={{0,8},{4,12},{8,16},{12,20},{16,24},{20,28},{1,9},{5,13},{9,17},{1... | collective-permute-start | bytes 3538952 | tf_op jit(solution)/shard_map/ppermute | solution.py:498
  476.6 48.6 %collective-permute-start.38 = (bf16[256,2304]{1,0:T(8,128)(2,1)S(1)}, bf16[256,2304]{1,0:T(8,128)(2,1)S(1)}, u32[]{:S(2)}, u32[]{:S(2)}) collective-permute-start(bf16[256,2304]{1,0:T(8,128)(2,1)S(1)} %get-tuple-element.96), channel_id=1, source_target_pairs={{24,16},{28,20},{16,8},{20,12},{8,0},{12,4},{25,17},{29,21},{17,9}... | collective-permute-start | bytes 3538952 | tf_op jit(solution)/shard_map/ppermute | solution.py:498
  501.0 22.6 %collective-permute-start.29 = (bf16[256,2048]{1,0:T(8,128)(2,1)S(1)}, bf16[256,2048]{1,0:T(8,128)(2,1)S(1)}, u32[]{:S(2)}, u32[]{:S(2)}) collective-permute-start(bf16[256,2048]{1,0:T(8,128)(2,1)S(1)} %get-tuple-element.90), channel_id=1, source_target_pairs={{0,1},{1,0},{2,3},{3,2},{4,5},{5,4},{6,7},{7,6},{8,9},{9,8},{10,11... | collective-permute-start | bytes 3145736 | tf_op jit(solution)/shard_map/ppermute | solution.py:502
  502.3 26.4 %collective-permute-start.30 = (bf16[256,2048]{1,0:T(8,128)(2,1)S(1)}, bf16[256,2048]{1,0:T(8,128)(2,1)S(1)}, u32[]{:S(2)}, u32[]{:S(2)}) collective-permute-start(bf16[256,2048]{1,0:T(8,128)(2,1)S(1)} %get-tuple-element.90), channel_id=1, source_target_pairs={{0,2},{1,3},{2,0},{3,1},{4,6},{5,7},{6,4},{7,5},{8,10},{9,11},{10,... | collective-permute-start | bytes 3145736 | tf_op jit(solution)/shard_map/ppermute | solution.py:502
  523.7 12.0 %collective-permute-start.31 = (bf16[128,2048]{1,0:T(8,128)(2,1)S(1)}, bf16[128,2048]{1,0:T(8,128)(2,1)S(1)}, u32[]{:S(2)}, u32[]{:S(2)}) collective-permute-start(bf16[128,2048]{1,0:T(8,128)(2,1)S(1)} %slice.350), channel_id=1, source_target_pairs={{0,2},{1,3},{2,0},{3,1},{4,6},{5,7},{6,4},{7,5},{8,10},{9,11},{10,... | collective-permute-start | bytes 1572872 | tf_op jit(solution)/shard_map/ppermute | solution.py:502
  528.7 10.3 %collective-permute-start.32 = (bf16[128,2048]{1,0:T(8,128)(2,1)S(1)}, bf16[128,2048]{1,0:T(8,128)(2,1)S(1)}, u32[]{:S(2)}, u32[]{:S(2)}) collective-permute-start(bf16[128,2048]{1,0:T(8,128)(2,1)S(1)} %slice.351), channel_id=1, source_target_pairs={{0,1},{1,0},{2,3},{3,2},{4,5},{5,4},{6,7},{7,6},{8,9},{9,8},{10,11... | collective-permute-start | bytes 1572872 | tf_op jit(solution)/shard_map/ppermute | solution.py:502
  544.6 52.7 %copy-start.2 = (bf16[1024,512]{1,0:T(8,128)(2,1)S(1)}, bf16[1024,512]{1,0:T(8,128)(2,1)}, u32[]{:S(2)}) copy-start(bf16[1024,512]{1,0:T(8,128)(2,1)} %copy-done.1) | copy-start | bytes 3145732
  620.8 11.4 %collective-permute-start.33 = (bf16[128,2048]{1,0:T(8,128)(2,1)S(1)}, bf16[128,2048]{1,0:T(8,128)(2,1)S(1)}, u32[]{:S(2)}, u32[]{:S(2)}) collective-permute-start(bf16[128,2048]{1,0:T(8,128)(2,1)S(1)} %get-tuple-element.109), channel_id=1, source_target_pairs={{0,2},{1,3},{2,0},{3,1},{4,6},{5,7},{6,4},{7,5},{8,10},{9,11},{10,... | collective-permute-start | bytes 1572872 | tf_op jit(solution)/shard_map/ppermute | solution.py:502
  622.5 11.5 %collective-permute-start.35 = (bf16[128,2048]{1,0:T(8,128)(2,1)S(1)}, bf16[128,2048]{1,0:T(8,128)(2,1)S(1)}, u32[]{:S(2)}, u32[]{:S(2)}) collective-permute-start(bf16[128,2048]{1,0:T(8,128)(2,1)S(1)} %get-tuple-element.108), channel_id=1, source_target_pairs={{0,1},{1,0},{2,3},{3,2},{4,5},{5,4},{6,7},{7,6},{8,9},{9,8},{10,11... | collective-permute-start | bytes 1572872 | tf_op jit(solution)/shard_map/ppermute | solution.py:502
  634.4 21.6 %collective-permute-start.34 = (bf16[256,2048]{1,0:T(8,128)(2,1)S(1)}, bf16[256,2048]{1,0:T(8,128)(2,1)S(1)}, u32[]{:S(2)}, u32[]{:S(2)}) collective-permute-start(bf16[256,2048]{1,0:T(8,128)(2,1)S(1)} %pad_maximum_fusion.10), channel_id=1, source_target_pairs={{0,1},{1,0},{2,3},{3,2},{4,5},{5,4},{6,7},{7,6},{8,9},{9,8},{10,11... | collective-permute-start | bytes 3145736 | tf_op jit(solution)/shard_map/ppermute | solution.py:502
  634.7 21.3 %collective-permute-start.36 = (bf16[256,2048]{1,0:T(8,128)(2,1)S(1)}, bf16[256,2048]{1,0:T(8,128)(2,1)S(1)}, u32[]{:S(2)}, u32[]{:S(2)}) collective-permute-start(bf16[256,2048]{1,0:T(8,128)(2,1)S(1)} %pad_maximum_fusion.11), channel_id=1, source_target_pairs={{0,2},{1,3},{2,0},{3,1},{4,6},{5,7},{6,4},{7,5},{8,10},{9,11},{10,... | collective-permute-start | bytes 3145736 | tf_op jit(solution)/shard_map/ppermute | solution.py:502
  (51 other events, 401.2 us)
Sparse Core Ops, SparseCore 0:
  12.2 59.2 all-gather.4
  73.7 88.9 all-gather.8
  164.8 89.1 all-gather.10
  256.1 66.0 all-gather.6
  388.1 99.3 reduce-scatter.5
  489.7 107.5 reduce-scatter.3
  614.0 57.2 reduce-scatter.7

commit v2 on v1

--- a/solution.py
+++ b/solution.py
@@ -16,7 +16,7 @@
 BRANCHES = 4
 EPSILON = 1e-05
 PARTS = (3, 3, 2)
-HOPS = 1
+EARLY = 1
 NEG = -1e30
 BF = jnp.bfloat16
 F32 = jnp.float32
@@ -291,6 +291,7 @@
         out_ref[:, q_width : q_width + 128] = jnp.where(lane < HD, turned, wide).astype(BF)
 
 
+LIGHT = pl.CostEstimate(flops=1000, bytes_accessed=1000, transcendentals=0)
 SMEM = pl.BlockSpec(memory_space=pltpu.SMEM)
 VMEM = pl.BlockSpec(memory_space=pltpu.VMEM)
 
@@ -311,9 +312,7 @@
         in_specs=[SMEM, SMEM, SMEM, VMEM, VMEM, VMEM],
         out_specs=(VMEM, VMEM, VMEM, VMEM),
         compiler_params=pltpu.CompilerParams(vmem_limit_bytes=40 << 20),
-        cost_estimate=pl.CostEstimate(
-            flops=8_000_000_000, bytes_accessed=8_000_000, transcendentals=3_000_000
-        ),
+        cost_estimate=LIGHT,
     )(masks, segs, base, pre, cosine, sine)
 
 
@@ -334,23 +333,215 @@
             pltpu.VMEM((rows, groups * HD), F32),
         ],
         compiler_params=pltpu.CompilerParams(vmem_limit_bytes=40 << 20),
-        cost_estimate=pl.CostEstimate(
-            flops=20_000_000_000, bytes_accessed=8_000_000, transcendentals=3_000_000
-        ),
+        cost_estimate=LIGHT,
     )(masks, segs, base, queries, keys, vals, grads, cosine, sine)
 
 
-def chunk_kernel(steps, slabs, halves, added, last, order_ref, *refs):
-    rows_ref, cot_ref, full_ref, rows_turned_ref, cot_turned_ref = refs[:5]
-    refs = refs[5:]
-    if added:
-        (back_in_ref, out_in_ref), refs = refs[:2], refs[2:]
-    grad_refs, refs = refs[:halves], refs[halves:]
-    back_ref, out_ref, pair_ref, hidden_ref = refs
+MESH = pl.DeviceIdType.MESH
+
+
+def swap_peers():
+    rank = lax.axis_index("tp")
+    place = lax.axis_index("fsdp")
+    return [(place, rank + 1 - 2 * (rank % 2)), (place, (rank + 2) % 4)]
+
+
+def greet(peers):
+    barrier = pltpu.get_barrier_semaphore()
+    for peer in peers:
+        pl.semaphore_signal(barrier, inc=1, device_id=peer, device_id_type=MESH)
+    pl.semaphore_wait(barrier, len(peers))
+
+
+def send(source, target, send_sem, recv_sem, peer):
+    copy = pltpu.make_async_remote_copy(
+        src_ref=source,
+        dst_ref=target,
+        send_sem=send_sem,
+        recv_sem=recv_sem,
+        device_id=peer,
+        device_id_type=MESH,
+    )
+    copy.start()
+    return copy
+
+
+def line_peers():
+    place = lax.axis_index("fsdp")
+    rank = lax.axis_index("tp")
+    z, core = place // 2, place % 2
+    up, down = (z + 1) % 4, (z + 3) % 4
+    return z, core, [(2 * z + 1 - core, rank), (2 * up + core, rank), (2 * down + core, rank)]
+
+
+def far_copies(far_ref, far_recv, send_sem, recv_sem, z, peers):
+    heading = z // 2
+    place = lax.axis_index("fsdp")
+    target = (place + 2 - 4 * heading, lax.axis_index("tp"))
+    return pltpu.make_async_remote_copy(
+        src_ref=far_ref,
+        dst_ref=far_recv.at[heading],
+        send_sem=send_sem,
+        recv_sem=recv_sem.at[heading],
+        device_id=target,
+        device_id_type=MESH,
+    )
+
+
+def far_add(pair_ref, far_recv, recv_sem, z, peers):
+    @pl.when((z == 1) | (z == 2))
+    def _():
+        for heading in range(2):
+            pltpu.make_async_remote_copy(
+                src_ref=far_recv.at[heading],
+                dst_ref=far_recv.at[heading],
+                send_sem=recv_sem.at[heading],
+                recv_sem=recv_sem.at[heading],
+                device_id=peers[0],
+                device_id_type=MESH,
+            ).wait_recv()
+        pair_ref[0] = (pair_ref[0].astype(F32) + far_recv[1].astype(F32)).astype(BF)
+        pair_ref[1] = (pair_ref[1].astype(F32) + far_recv[0].astype(F32)).astype(BF)
+
+
+def near_copies(pair_ref, near_recv, send_sem, recv_sem, peers):
+    return [
+        pltpu.make_async_remote_copy(
+            src_ref=pair_ref.at[at],
+            dst_ref=near_recv.at[at],
+            send_sem=send_sem.at[at],
+            recv_sem=recv_sem.at[at],
+            device_id=peers[2 - at],
+            device_id_type=MESH,
+        )
+        for at in range(2)
+    ]
+
+
+class Hops:
+    def __init__(self, slabs_ref, total_ref, pair_ref, slab_ref, far_recv, near_recv, sends, recvs, loads):
+        self.z, _, self.line = line_peers()
+        self.total_ref, self.pair_ref, self.slab_ref = total_ref, pair_ref, slab_ref
+        self.far_recv, self.near_recv, self.recvs = far_recv, near_recv, recvs
+        self.far = far_copies(
+            slabs_ref.at[0], far_recv, sends.at[0, 0], recvs.at[0], self.z, self.line
+        )
+        self.loads = [
+            pltpu.make_async_copy(slabs_ref.at[1 + at], pair_ref.at[at], loads.at[at])
+            for at in range(2)
+        ] + [pltpu.make_async_copy(slabs_ref.at[3], slab_ref, loads.at[2])]
+        self.near = near_copies(pair_ref, near_recv, sends.at[1], recvs.at[1], self.line)
+
+    def begin(self):
+        self.far.start()
+        for load in self.loads:
+            load.start()
+
+    def onward(self):
+        for load in self.loads:
+            load.wait()
+        self.far.wait_send()
+        far_add(self.pair_ref, self.far_recv, self.recvs.at[0], self.z, self.line)
+        for copy in self.near:
+            copy.start()
+
+    def finish(self):
+        for copy in self.near:
+            copy.wait()
+        self.total_ref[...] = (
+            self.slab_ref[...].astype(F32)
+            + self.near_recv[0].astype(F32)
+            + self.near_recv[1].astype(F32)
+        )
+
+
+def hop_scratch(height, width):
+    return [
+        pltpu.VMEM((2, height, width), BF),
+        pltpu.VMEM((height, width), BF),
+        pltpu.VMEM((2, height, width), BF),
+        pltpu.VMEM((2, height, width), BF),
+        pltpu.SemaphoreType.DMA((2, 2)),
+        pltpu.SemaphoreType.DMA((2, 2)),
+        pltpu.SemaphoreType.DMA((3,)),
+    ]
+
+
+SLOTS = (2, 1, 3, 0)
+
+
+def chunk_kernel(cfg, *refs):
+    steps, slabs, first, last, cores, job, owners = cfg
+    refs = list(refs)
+    take = lambda count: [refs.pop(0) for _ in range(count)]
+    rows_ref, cot_ref, full_ref = take(3)
+    if not first:
+        back_in_ref, out_in_ref = take(2)
+    if job == "far":
+        (slabs_ref,) = take(1)
+    if job == "near":
+        slabs_ref, moved_ref = take(2)
+    if owners:
+        (residual_ref,) = take(1)
+    grad_ref, back_ref, out_ref = take(3)
+    if job == "far":
+        (moved_ref,) = take(1)
+    if job == "near":
+        (total_ref,) = take(1)
+    pair_ref, hidden_ref = take(2)
+    if cores:
+        mine_ref, theirs_ref, core_send, core_recv = take(4)
+    if job:
+        job_recv, job_send_sem, job_recv_sem, load_sem = take(4)
+    if job == "near":
+        (slab_ref,) = take(1)
+    if owners:
+        part_ref, owned_ref, owner_send, owner_recv = take(4)
+
     step = pl.program_id(0)
+    end = steps + slabs - 1
     chunk = hidden_ref.shape[1]
     tile = chunk // steps
-    height = rows_turned_ref.shape[0]
+    height = rows_ref.shape[1] // slabs
+    if cores or job:
+        z, core, peers = line_peers()
+        far = None
+        if job == "far":
+            loads = [
+                pltpu.make_async_copy(slabs_ref.at[1 + at], moved_ref.at[at], load_sem.at[at])
+                for at in range(2)
+            ]
+            far = far_copies(slabs_ref.at[0], job_recv, job_send_sem.at[0], job_recv_sem, z, peers)
+        if job == "near":
+            loads = [pltpu.make_async_copy(slabs_ref.at[3], slab_ref, load_sem.at[0])]
+            near = near_copies(moved_ref, job_recv, job_send_sem, job_recv_sem, peers)
+
+        if owners:
+            fsdp, rank = lax.axis_index("fsdp"), lax.axis_index("tp")
+            beside = rank + 1 - 2 * (rank % 2)
+            row_peers = [(fsdp, beside), (fsdp, (rank + 2) % 4), (fsdp, 3 - rank)]
+
+            def to_owner(piece, columns):
+                return pltpu.make_async_remote_copy(
+                    src_ref=part_ref.at[piece, :, columns],
+                    dst_ref=owned_ref.at[piece - 1, :, columns],
+                    send_sem=owner_send.at[piece - 1],
+                    recv_sem=owner_recv.at[piece - 1],
+                    device_id=row_peers[piece - 1],
+                    device_id_type=MESH,
+                )
+
+        @pl.when(step == 0)
+        def _():
+            greet(peers + (row_peers if owners else []))
+            if job == "far":
+                far.start()
+            if job == "near":
+                for copy in near:
+                    copy.start()
+            if job:
+                for load in loads:
+                    load.start()
 
     for at in range(steps):
 
@@ -368,91 +559,177 @@
             pair_ref[:, cut] = (back * up * sigmoid * (1.0 + gate * (1.0 - sigmoid))).astype(BF)
             pair_ref[:, chunk + at * tile : chunk + (at + 1) * tile] = (back * silu).astype(BF)
 
-    def write(grad_ref):
-        grad = jnp.concatenate(
-            [
-                dot_nn(rows_turned_ref[...], pair_ref[...]).astype(BF),
-                dot_nn(cot_turned_ref[...], hidden_ref[...]).astype(BF),
-            ],
-            axis=1,
-        )
-        grad_ref[...] = grad.reshape(grad_ref.shape)
+    def write(slab, target_ref, added_ref):
+        at = pl.ds(pl.multiple_of(slab * height, height), height)
+        grad = dot_tn(rows_ref[:, at], pair_ref[...])
+        more = dot_tn(cot_ref[:, at], hidden_ref[...])
+        if added_ref is not None:
+            grad = grad.astype(BF).astype(F32) + added_ref[:, : 2 * chunk].astype(F32)
+            more = more.astype(BF).astype(F32) + added_ref[:, 2 * chunk :].astype(F32)
+        target_ref[:, : 2 * chunk] = grad.astype(BF)
+        target_ref[:, 2 * chunk :] = more.astype(BF)
 
     @pl.when(step >= steps)
     def _():
-        slab = pl.ds(pl.multiple_of(order_ref[step - steps] * height, height), height)
+        slab = pl.ds(pl.multiple_of((step - steps) * height, height), height)
         back = dot_nt(pair_ref[...], full_ref[slab, : 2 * chunk])
         out = dot_nt(hidden_ref[...], full_ref[slab, 2 * chunk :])
-        back = back_in_ref[...] + back if added else back
-        out = out_in_ref[...] + out if added else out
+        back = back if first else back_in_ref[...] + back
+        out = out if first else out_in_ref[...] + out
         back_ref[...] = back.astype(back_ref.dtype)
-        out_ref[...] = out.astype(out_ref.dtype)
-        if halves == 1:
-            write(grad_refs[0])
-
-    if halves == 2:
-
-        @pl.when((step >= steps) & (step < steps + slabs // 2))
+        if owners:
+            columns = pl.ds(pl.multiple_of((step - steps) * height, height), height)
+            part_ref[:, :, columns] = out.astype(BF).reshape(4, -1, height)
+            for piece in (3, 1, 2):
+                to_owner(piece, columns).start()
+        else:
+            out_ref[...] = out.astype(out_ref.dtype)
+        if not cores:
+            write(step - steps, grad_ref, None)
+
+    if cores:
+        copies = [
+            pltpu.make_async_remote_copy(
+                src_ref=mine_ref.at[at % 2],
+                dst_ref=theirs_ref.at[at],
+                send_sem=core_send.at[at],
+                recv_sem=core_recv.at[at],
+                device_id=peers[0],
+                device_id_type=MESH,
+            )
+            for at in range(4)
+        ]
+        for at, slot in enumerate(SLOTS):
+            chip = (z + 4 - slot) % 4
+
+            @pl.when(step == steps + at)
+            def _():
+                if at >= 2:
+                    copies[at - 2].wait_send()
+                write(2 * chip + 1 - core, mine_ref.at[at % 2], None)
+                copies[at].start()
+
+            @pl.when(step == steps + 4 + at)
+            def _():
+                copies[at].wait_recv()
+                write(2 * chip + core, grad_ref.at[0], theirs_ref.at[at])
+
+        @pl.when(step == end)
         def _():
-            write(grad_refs[0])
-
-        @pl.when(step >= steps + slabs // 2)
+            copies[2].wait_send()
+            copies[3].wait_send()
+
+    if job == "far":
+
+        @pl.when(step == end)
         def _():
-            write(grad_refs[1])
-
-
-def chunk_pass(order, halves, rows, cot, full, rows_turned, cot_turned, sums, last):
+            for load in loads:
+                load.wait()
+            far.wait_send()
+            far_add(moved_ref, job_recv, job_recv_sem, z, peers)
+
+    if job == "near":
+
+        @pl.when(step == end)
+        def _():
+            loads[0].wait()
+            for copy in near:
+                copy.wait()
+            total_ref[...] = (
+                slab_ref[...].astype(F32) + job_recv[0].astype(F32) + job_recv[1].astype(F32)
+            )
+
+
+    if owners:
+
+        @pl.when(step == end)
+        def _():
+            for piece in (1, 2, 3):
+                to_owner(piece, slice(None)).wait()
+            total = residual_ref[...] + part_ref[0].astype(F32)
+            for piece in range(3):
+                total = total + owned_ref[piece].astype(F32)
+            out_ref[...] = total.astype(BF)
+
+
+def chunk_pass(rows, cot, full, at, width, sums, last, cores=False, job=None, operands=(), number=None, residual=None):
     count, depth = rows.shape
-    width = full.shape[1]
     chunk = width // 3
-    slabs = order.shape[0]
+    slabs = 8
     height = depth // slabs
     steps = max(1, chunk // 256)
-    added = sums is not None
+    first = sums is None
     whole = pl.BlockSpec(memory_space=pltpu.VMEM)
+    anywhere = pl.BlockSpec(memory_space=pl.ANY)
+    weights = pl.BlockSpec((depth, width), lambda i: (0, at), pipeline_mode=pl.Buffered(1))
 
     def place(i):
         return jnp.maximum(i - steps, 0)
 
-    turned = pl.BlockSpec((height, count), lambda i, order: (order[place(i)], 0))
-    column = pl.BlockSpec((count, height), lambda i, order: (0, order[place(i)]))
-    if halves == 2:
-        half = slabs // 2
-        grad_shapes = [jax.ShapeDtypeStruct((half, height, width), BF)] * 2
-        grad_specs = [
-            pl.BlockSpec(
-                (1, height, width), lambda i, order: (jnp.minimum(place(i), half - 1), 0, 0)
-            ),
-            pl.BlockSpec(
-                (1, height, width), lambda i, order: (jnp.maximum(place(i) - half, 0), 0, 0)
-            ),
+    column = pl.BlockSpec((count, height), lambda i: (0, place(i)))
+    total = jax.ShapeDtypeStruct((count, depth), BF if last else F32)
+    if cores:
+        grad_shape = jax.ShapeDtypeStruct((4, height, width), BF)
+        grad_spec = pl.BlockSpec((1, height, width), lambda i: (jnp.maximum(place(i) - 4, 0), 0, 0))
+    else:
+        grad_shape = jax.ShapeDtypeStruct((depth, width), BF)
+        grad_spec = pl.BlockSpec((height, width), lambda i: (place(i), 0))
+    out_shapes, out_specs = [grad_shape, total, total], [grad_spec, column, column]
+    in_specs = [whole, whole, weights] + ([] if first else [column, column])
+    scratch = [pltpu.VMEM((count, 2 * chunk), BF), pltpu.VMEM((count, chunk), BF)]
+    dma = pltpu.SemaphoreType.DMA
+    if cores:
+        scratch += [
+            pltpu.VMEM((2, height, width), BF),
+            pltpu.VMEM((4, height, width), BF),
+            dma((4,)),
+            dma((4,)),
         ]
-    else:
-        grad_shapes = [jax.ShapeDtypeStruct((depth, width), BF)]
-        grad_specs = [pl.BlockSpec((height, width), lambda i, order: (order[place(i)], 0))]
-    total = jax.ShapeDtypeStruct((count, depth), BF if last else F32)
+    if job:
+        job_width = operands[0].shape[-1]
+        scratch += [pltpu.VMEM((2, height, job_width), BF), dma((2,)), dma((2,)), dma((2,))]
+    if job == "far":
+        in_specs += [anywhere]
+        out_shapes += [jax.ShapeDtypeStruct((2, height, job_width), BF)]
+        out_specs += [whole]
+    if job == "near":
+        in_specs += [anywhere, anywhere]
+        out_shapes += [jax.ShapeDtypeStruct((height, job_width), F32)]
+        out_specs += [whole]
+        scratch += [pltpu.VMEM((height, job_width), BF)]
+    if residual is not None:
+        own = residual.shape[0]
+        in_specs += [whole]
+        operands = (*operands, residual)
+        out_shapes[2] = jax.ShapeDtypeStruct((own, depth), BF)
+        out_specs[2] = whole
+        scratch += [
+            pltpu.VMEM((4, own, depth), BF),
+            pltpu.VMEM((3, own, depth), BF),
+            dma((3,)),
+            dma((3,)),
+        ]
+    remote = cores or job
     return pl.pallas_call(
-        functools.partial(chunk_kernel, steps, slabs, halves, added, last),
+        functools.partial(chunk_kernel, (steps, slabs, first, last, cores, job, residual is not None)),
         name="chunk_pass",
-        out_shape=(*grad_shapes, total, total),
-        grid_spec=pltpu.PrefetchScalarGridSpec(
-            num_scalar_prefetch=1,
-            grid=(steps + slabs,),
-            in_specs=[whole, whole, whole, turned, turned] + [column] * (2 if added else 0),
-            out_specs=(*grad_specs, column, column),
-            scratch_shapes=[
-                pltpu.VMEM((count, 2 * chunk), BF),
-                pltpu.VMEM((count, chunk), BF),
-            ],
-        ),
-        input_output_aliases={6: halves, 7: halves + 1} if added and not last else {},
-        compiler_params=pltpu.CompilerParams(vmem_limit_bytes=56 << 20),
+        out_shape=tuple(out_shapes),
+        grid=(steps + slabs,),
+        in_specs=in_specs,
+        out_specs=tuple(out_specs),
+        scratch_shapes=scratch,
+        input_output_aliases={} if first or last else {3: 1, 4: 2},
+        compiler_params=pltpu.CompilerParams(
+            vmem_limit_bytes=60 << 20,
+            collective_id=number if remote else None,
+            has_side_effects=bool(remote),
+        ),
         cost_estimate=pl.CostEstimate(
             flops=6 * count * depth * width,
             bytes_accessed=8 * count * depth + 4 * depth * width + 16 * count * depth,
             transcendentals=count * chunk,
         ),
-    )(order, rows, cot, full, rows_turned, cot_turned, *(sums if added else ()))
+    )(rows, cot, full, *(() if first else sums), *operands)
 
 
 def pair_kernel(left_ref, first_ref, other_ref, second_ref, out_ref):
@@ -475,6 +752,82 @@
         in_specs=[column, whole, column, whole],
         out_specs=pl.BlockSpec((height, width), lambda i: (i, 0)),
         compiler_params=pltpu.CompilerParams(vmem_limit_bytes=32 << 20),
+        cost_estimate=LIGHT,
+    )(left, first, other, second)
+
+
+def pair_hops_kernel(
+    left_ref, first_ref, other_ref, second_ref, out_ref, mine_ref, theirs_ref, core_send, core_recv
+):
+    step = pl.program_id(0)
+    z, core, peers = line_peers()
+    width = first_ref.shape[1]
+    height = out_ref.shape[1]
+
+    def write(slab, target_ref, added_ref):
+        at = pl.ds(pl.multiple_of(slab * height, height), height)
+        grad = dot_tn(left_ref[:, at], first_ref[...])
+        more = dot_tn(other_ref[:, at], second_ref[...])
+        if added_ref is not None:
+            grad = grad.astype(BF).astype(F32) + added_ref[:, :width].astype(F32)
+            more = more.astype(BF).astype(F32) + added_ref[:, width:].astype(F32)
+        target_ref[:, :width] = grad.astype(BF)
+        target_ref[:, width:] = more.astype(BF)
+
+    @pl.when(step == 0)
+    def _():
+        greet(peers[:1])
+
+    copies = [
+        pltpu.make_async_remote_copy(
+            src_ref=mine_ref.at[at],
+            dst_ref=theirs_ref.at[at],
+            send_sem=core_send.at[at],
+            recv_sem=core_recv.at[at],
+            device_id=peers[0],
+            device_id_type=MESH,
+        )
+        for at in range(4)
+    ]
+    for at, slot in enumerate(SLOTS):
+        chip = (z + 4 - slot) % 4
+
+        @pl.when(step == at)
+        def _():
+            write(2 * chip + 1 - core, mine_ref.at[at], None)
+            copies[at].start()
+
+        @pl.when(step == 4 + at)
+        def _():
+            copies[at].wait_recv()
+            write(2 * chip + core, out_ref.at[0], theirs_ref.at[at])
+
+    @pl.when(step == 7)
+    def _():
+        for copy in copies:
+            copy.wait_send()
+
+
+def pair_hops(left, first, other, second):
+    count, depth = left.shape
+    width = first.shape[1] + second.shape[1]
+    height = depth // 8
+    return pl.pallas_call(
+        pair_hops_kernel,
+        name="pair_hops",
+        out_shape=jax.ShapeDtypeStruct((4, height, width), BF),
+        grid=(8,),
+        in_specs=[VMEM] * 4,
+        out_specs=pl.BlockSpec((1, height, width), lambda i: (jnp.maximum(i - 4, 0), 0, 0)),
+        scratch_shapes=[
+            pltpu.VMEM((4, height, width), BF),
+            pltpu.VMEM((4, height, width), BF),
+            pltpu.SemaphoreType.DMA((4,)),
+            pltpu.SemaphoreType.DMA((4,)),
+        ],
+        compiler_params=pltpu.CompilerParams(
+            collective_id=7, has_side_effects=True, vmem_limit_bytes=48 << 20
+        ),
         cost_estimate=pl.CostEstimate(
             flops=2 * count * depth * width,
             bytes_accessed=4 * count * depth + 2 * depth * width,
@@ -483,21 +836,10 @@
     )(left, first, other, second)
 
 
-def on_z(pairs):
-    return [(2 * a + core, 2 * b + core) for a, b in pairs for core in range(2)]
-
-
-UP = [on_z([(z, z + 1) for z in range(count)]) for count in (1, 2, 3)]
-DOWN = [on_z([(3 - z, 2 - z) for z in range(count)]) for count in (1, 2, 3)]
-CORES = [(i, i ^ 1) for i in range(8)]
 X_SWAP = [(i, i ^ 1) for i in range(4)]
 Y_SWAP = [(i, i ^ 2) for i in range(4)]
 
 
-def by_fsdp(value, pairs):
-    return lax.ppermute(value, "fsdp", pairs)
-
-
 def by_tp(value, pairs):
     return lax.ppermute(value, "tp", pairs)
 
@@ -506,17 +848,256 @@
     return lax.optimization_barrier((value, *earlier))[0]
 
 
+def sum_pieces(part_ref, make, half_ref, whole_ref, send_sem, recv_sem, peers, meanwhile):
+    half = part_ref.shape[1] // 2
+    make(3)
+    copies = [
+        send(
+            part_ref.at[3, pl.ds(axis * half, half)],
+            half_ref.at[axis],
+            send_sem.at[axis],
+            recv_sem.at[axis],
+            peers[axis],
+        )
+        for axis in range(2)
+    ]
+    for piece in (1, 2, 0):
+        make(piece)
+    meanwhile(0)
+    for copy in copies:
+        copy.wait()
+    part_ref[2, :half] = (part_ref[2, :half].astype(F32) + half_ref[0].astype(F32)).astype(BF)
+    part_ref[1, half:] = (part_ref[1, half:].astype(F32) + half_ref[1].astype(F32)).astype(BF)
+    copies = [
+        send(
+            part_ref.at[1 + axis],
+            whole_ref.at[axis],
+            send_sem.at[2 + axis],
+            recv_sem.at[2 + axis],
+            peers[axis],
+        )
+        for axis in range(2)
+    ]
+    meanwhile(1)
+    for copy in copies:
+        copy.wait()
+    return part_ref[0].astype(F32) + whole_ref[0].astype(F32) + whole_ref[1].astype(F32)
+
+
+def gather_pieces(all_ref, send_sem, recv_sem, peers, meanwhile):
+    half = all_ref.shape[1] // 2
+    copies = [
+        send(all_ref.at[0], all_ref.at[1 + axis], send_sem.at[axis], recv_sem.at[axis], peers[axis])
+        for axis in range(2)
+    ]
+    meanwhile(2)
+    for copy in copies:
+        copy.wait()
+    copies = []
+    for axis in range(2):
+        rows = pl.ds(axis * half, half)
+        copies.append(
+            send(
+                all_ref.at[1 + axis, rows],
+                all_ref.at[3, rows],
+                send_sem.at[2 + axis],
+                recv_sem.at[2 + axis],
+                peers[1 - axis],
+            )
+        )
+    meanwhile(3)
+    for copy in copies:
+        copy.wait()
+
+
+def idle(stage):
+    return None
+
+
+def row_scale(values):
+    return lax.rsqrt(jnp.mean(values * values, axis=-1, keepdims=True) + EPSILON)
+
+
+def mid_forward_kernel(
+    attended_ref, weight_ref, input_ref, gain_ref,
+    residual_ref, all_ref,
+    part_ref, half_ref, whole_ref, sems,
+):
+    peers = swap_peers()
+    rows = input_ref.shape[0]
+    greet(peers)
+
+    def make(piece):
+        part_ref[piece] = dot_nt(
+            attended_ref[piece * rows : (piece + 1) * rows], weight_ref[...]
+        ).astype(BF)
+
+    summed = sum_pieces(part_ref, make, half_ref, whole_ref, sems.at[0], sems.at[1], peers, idle)
+    residual = input_ref[...].astype(F32) + summed
+    residual_ref[...] = residual
+    all_ref[0] = (residual * row_scale(residual) * gain_ref[...].astype(F32)).astype(BF)
+    gather_pieces(all_ref, sems.at[2], sems.at[3], peers, idle)
+
+
+def mid_forward(attended, weight, inputs, gain):
+    rows, width = inputs.shape
+    return pl.pallas_call(
+        mid_forward_kernel,
+        name="mid_forward",
+        out_shape=(
+            jax.ShapeDtypeStruct((rows, width), F32),
+            jax.ShapeDtypeStruct((4, rows, width), BF),
+        ),
+        in_specs=[VMEM] * 4,
+        out_specs=(VMEM,) * 2,
+        scratch_shapes=[
+            pltpu.VMEM((4, rows, width), BF),
+            pltpu.VMEM((2, rows // 2, width), BF),
+            pltpu.VMEM((2, rows, width), BF),
+            pltpu.SemaphoreType.DMA((4, 4)),
+        ],
+        compiler_params=pltpu.CompilerParams(
+            collective_id=1, has_side_effects=True, vmem_limit_bytes=56 << 20
+        ),
+        cost_estimate=pl.CostEstimate(
+            flops=80_000_000_000, bytes_accessed=20_000_000, transcendentals=0
+        ),
+    )(attended, weight, inputs, gain)
+
+
+def row_grads(values, gain, back):
+    scale = row_scale(values)
+    scaled = back * gain
+    return scale * scaled - values * (scale * scale * scale) * jnp.mean(
+        scaled * values, axis=-1, keepdims=True
+    )
+
+
+def mid_backward_kernel(
+    back_ref, residual_ref, cot_ref, gain_ref, slabs_ref,
+    out_ref, all_ref, total_ref,
+    part_ref, half_ref, whole_ref, sems, load_sem, *hop_refs,
+):
+    peers = swap_peers()
+    hops = Hops(slabs_ref, total_ref, *hop_refs)
+    greet(peers + hops.line[1:])
+    hops.begin()
+
+    def meanwhile(stage):
+        if stage == 1:
+            hops.onward()
+
+    order = (3, 1, 2, 0)
+    loads = [
+        pltpu.make_async_copy(back_ref.at[piece], part_ref.at[piece], load_sem.at[piece])
+        for piece in range(4)
+    ]
+    for piece in order:
+        loads[piece].start()
+    summed = sum_pieces(
+        part_ref, lambda piece: loads[piece].wait(), half_ref, whole_ref,
+        sems.at[0], sems.at[1], peers, meanwhile,
+    )
+    grads = cot_ref[...].astype(F32) + row_grads(
+        residual_ref[...], gain_ref[...].astype(F32), summed
+    )
+    out_ref[...] = grads
+    all_ref[0] = grads.astype(BF)
+    gather_pieces(all_ref, sems.at[2], sems.at[3], peers, idle)
+    hops.finish()
+
+
+def mid_backward(back, residual, cot, gain, slabs):
+    rows, width = residual.shape
+    _, height, job_width = slabs.shape
+    return pl.pallas_call(
+        mid_backward_kernel,
+        name="mid_backward",
+        out_shape=(
+            jax.ShapeDtypeStruct((rows, width), F32),
+            jax.ShapeDtypeStruct((4, rows, width), BF),
+            jax.ShapeDtypeStruct((height, job_width), F32),
+        ),
+        in_specs=[
+            pl.BlockSpec(memory_space=pl.ANY), VMEM, VMEM, VMEM, pl.BlockSpec(memory_space=pl.ANY)
+        ],
+        out_specs=(VMEM,) * 3,
+        scratch_shapes=[
+            pltpu.VMEM((4, rows, width), BF),
+            pltpu.VMEM((2, rows // 2, width), BF),
+            pltpu.VMEM((2, rows, width), BF),
+            pltpu.SemaphoreType.DMA((4, 4)),
+            pltpu.SemaphoreType.DMA((4,)),
+            *hop_scratch(height, job_width),
+        ],
+        compiler_params=pltpu.CompilerParams(
+            collective_id=2, has_side_effects=True, vmem_limit_bytes=48 << 20
+        ),
+        cost_estimate=pl.CostEstimate(
+            flops=80_000_000_000, bytes_accessed=20_000_000, transcendentals=0
+        ),
+    )(back.reshape(4, rows, width), residual, cot, gain, slabs)
+
+
+def end_backward_kernel(
+    grads_ref, weight_ref, input_ref, gain_ref, later_ref, slabs_ref,
+    out_ref, total_ref, part_ref, half_ref, whole_ref, sems, *hop_refs,
+):
+    peers = swap_peers()
+    rows = input_ref.shape[0]
+    hops = Hops(slabs_ref, total_ref, *hop_refs)
+    greet(peers + hops.line[1:])
+    hops.begin()
+
+    def meanwhile(stage):
+        if stage == 1:
+            hops.onward()
+
+    def make(piece):
+        part_ref[piece] = dot_nt(
+            grads_ref[piece * rows : (piece + 1) * rows], weight_ref[...]
+        ).astype(BF)
+
+    summed = sum_pieces(
+        part_ref, make, half_ref, whole_ref, sems.at[0], sems.at[1], peers, meanwhile
+    )
+    out_ref[...] = later_ref[...] + row_grads(
+        input_ref[...].astype(F32), gain_ref[...].astype(F32), summed
+    )
+    hops.finish()
+
+
+def end_backward(grads, weight, inputs, gain, later, slabs):
+    rows, width = inputs.shape
+    _, height, job_width = slabs.shape
+    return pl.pallas_call(
+        end_backward_kernel,
+        name="end_backward",
+        out_shape=(
+            jax.ShapeDtypeStruct((rows, width), F32),
+            jax.ShapeDtypeStruct((height, job_width), F32),
+        ),
+        in_specs=[VMEM] * 5 + [pl.BlockSpec(memory_space=pl.ANY)],
+        out_specs=(VMEM, VMEM),
+        scratch_shapes=[
+            pltpu.VMEM((4, rows, width), BF),
+            pltpu.VMEM((2, rows // 2, width), BF),
+            pltpu.VMEM((2, rows, width), BF),
+            pltpu.SemaphoreType.DMA((2, 4)),
+            *hop_scratch(height, job_width),
+        ],
+        compiler_params=pltpu.CompilerParams(
+            collective_id=3, has_side_effects=True, vmem_limit_bytes=48 << 20
+        ),
+        cost_estimate=pl.CostEstimate(
+            flops=40_000_000_000, bytes_accessed=20_000_000, transcendentals=0
+        ),
+    )(grads, weight, inputs, gain, later, slabs)
+
+
 class Line:
-    by_hops = True
-    slabs = 8
-
     def __init__(self):
-        place = lax.axis_index("fsdp")
-        z, core = place // 2, place % 2
         self.rank = lax.axis_index("tp")
-        self.order = jnp.stack(
-            [((z + 4 - slot) % 4) * 2 + (core ^ other) for other in (1, 0) for slot in range(4)]
-        ).astype(jnp.int32)
 
     def row_order(self, values):
         count = values.shape[0] // 4
@@ -526,23 +1107,6 @@
 
     def trunk_base(self):
         return self.rank * TRUNK
-
-    def sum_slabs(self, away, own):
-        sums = own.astype(F32) + by_fsdp(away, CORES).astype(F32)
-        low = sums.astype(BF)
-        up = by_fsdp(low[1], UP[0])
-        down = by_fsdp(low[3], DOWN[0])
-        middle = (sums[2] + up.astype(F32) + down.astype(F32)).astype(BF)
-        marks = [low, middle]
-        up = by_fsdp(middle, UP[1])
-        down = by_fsdp(middle, DOWN[1])
-        up = (sums[3] + up.astype(F32)).astype(BF)
-        down = (sums[1] + down.astype(F32)).astype(BF)
-        marks.append(up)
-        marks.append(down)
-        up = by_fsdp(up, UP[2])
-        down = by_fsdp(down, DOWN[2])
-        return sums[0] + up.astype(F32) + down.astype(F32), marks
 
     def gather_rows(self, rows):
         half = rows.shape[0] // 2
@@ -552,24 +1116,33 @@
             [rows, beside, above, by_tp(beside[:half], Y_SWAP), by_tp(above[half:], X_SWAP)]
         )
 
-    def scatter_rows(self, partial):
-        count = partial.shape[0] // 4
-        half = count // 2
-        own = partial[:count].astype(F32)
-        beside = partial[count : 2 * count]
-        above = partial[2 * count : 3 * count]
-        far = partial[3 * count :].astype(BF)
-        first = by_tp(far[:half], X_SWAP).astype(F32)
-        second = by_tp(far[half:], Y_SWAP).astype(F32)
-        above = jnp.concatenate([above[:half] + first, above[half:].astype(F32)]).astype(BF)
-        beside = jnp.concatenate([beside[:half].astype(F32), beside[half:] + second]).astype(BF)
-        return own + by_tp(beside, X_SWAP).astype(F32) + by_tp(above, Y_SWAP).astype(F32)
+    def mid_forward(self, attended, weight, inputs, gain):
+        residual, normed = mid_forward(attended, weight, inputs, gain)
+        return residual, normed.reshape(-1, normed.shape[-1])
+
+    def mid_backward(self, back, residual, cot, gain, slabs):
+        grads, gathered, total = mid_backward(back, residual, cot, gain, slabs)
+        return grads, gathered.reshape(-1, gathered.shape[-1]), total
+
+    def chunks(self, rows, cot, blocks, residual):
+        (full, at, width), second, third = blocks
+        slabs, *sums = chunk_pass(rows, cot, full, at, width, None, False, True, None, (), 4)
+        first = slabs
+        full, at, width = second
+        slabs, *sums, moved = chunk_pass(
+            rows, cot, full, at, width, sums, False, True, "far", (first,), 5
+        )
+        full, at, width = third
+        grads, *sums, total = chunk_pass(
+            rows, cot, full, at, width, sums, True, False, "near", (first, moved), 6, residual
+        )
+        return sums, [total, None, grads], slabs
+
+    def end_backward(self, grads, weight, inputs, gain, later, operands):
+        return end_backward(grads, weight, inputs, gain, later, pair_hops(*operands))
 
 
 class Plain:
-    by_hops = False
-    slabs = 8
-
     def row_order(self, values):
         return values
 
@@ -582,6 +1155,31 @@
     def scatter_rows(self, partial):
         return lax.psum_scatter(partial.astype(F32), "tp", scatter_dimension=0, tiled=True)
 
+    def mid_forward(self, attended, weight, inputs, gain):
+        residual = inputs.astype(F32) + self.scatter_rows(dot_nt(attended, weight))
+        normed = residual * row_scale(residual) * gain.astype(F32)
+        normed = self.gather_rows(normed.astype(BF))
+        return residual, normed
+
+    def chunks(self, rows, cot, blocks, residual):
+        sums = None
+        parts = []
+        for full, at, width in blocks:
+            grads, *sums = chunk_pass(rows, cot, full, at, width, sums, len(parts) == len(blocks) - 1)
+            parts.append(scatter_slabs(grads))
+        back, out = sums
+        return (back, (residual + self.scatter_rows(out)).astype(BF)), parts, None
+
+    def mid_backward(self, back, residual, cot, gain, slabs):
+        grads = row_grads(residual, gain.astype(F32), self.scatter_rows(back))
+        grads = cot.astype(F32) + grads
+        return grads, self.gather_rows(grads.astype(BF)), None
+
+    def end_backward(self, grads, weight, inputs, gain, later, operands):
+        sums = scatter_slabs(pair_grads(*operands))
+        back = self.scatter_rows(dot_nt(grads, weight))
+        return later + row_grads(inputs.astype(F32), gain.astype(F32), back), sums
+
 
 def gather_slabs(shard):
     return lax.all_gather(shard, "fsdp", axis=0, tiled=True)
@@ -589,17 +1187,6 @@
 
 def scatter_slabs(grads):
     return lax.psum_scatter(grads, "fsdp", scatter_dimension=0, tiled=True).astype(F32)
-
-
-def rms_scale(row_values):
-    return lax.rsqrt(jnp.mean(row_values * row_values, axis=-1, keepdims=True) + EPSILON)
-
-
-def norm_back(row_values, row_scale, gain_values, grad_out):
-    scaled_grad = grad_out * gain_values
-    return row_scale * scaled_grad - row_values * row_scale**3 * jnp.mean(
-        scaled_grad * row_values, axis=-1, keepdims=True
-    )
 
 
 def body(
@@ -627,20 +1214,19 @@
     units = gate_weight.shape[1]
     edges = [units * sum(PARTS[:i]) // sum(PARTS) for i in range(len(PARTS) + 1)]
 
-    gain_rows = gather_slabs(jnp.stack([attn_gain, mlp_gain], axis=1)).astype(F32)
+    gain_rows = gather_slabs(jnp.stack([attn_gain, mlp_gain], axis=1))
     first_gain, second_gain = gain_rows[:, 0][None, :], gain_rows[:, 1][None, :]
     own_qkv = jnp.concatenate([query_weight, key_weight, value_weight], axis=1)
     attn_full = gather_slabs(jnp.concatenate([own_qkv, out_weight.T], axis=1))
     qkv_full, out_full = attn_full[:, :qkv_width], attn_full[:, qkv_width:]
     own_down = down_weight.T
-    mlp_full = []
-    for first, last in zip(edges[:-1], edges[1:]):
-        cut = slice(first, last)
-        mlp_full.append(
-            gather_slabs(
-                jnp.concatenate([gate_weight[:, cut], up_weight[:, cut], own_down[:, cut]], axis=1)
-            )
-        )
+    own_mlp = [
+        jnp.concatenate([gate_weight[:, cut], up_weight[:, cut], own_down[:, cut]], axis=1)
+        for cut in map(slice, edges[:-1], edges[1:])
+    ]
+    early = gather_slabs(jnp.concatenate(own_mlp[:EARLY], axis=1))
+    mlp_full = [(early, place) for place in range(EARLY)]
+    mlp_full += [(gather_slabs(own), 0) for own in own_mlp[EARLY:]]
 
     positions = links.row_order(path_positions)
     angles = positions.astype(F32)[:, None] * jnp.asarray(inverse_freq(HD))[None, :]
@@ -652,61 +1238,41 @@
     base = jnp.reshape(links.trunk_base(), (1,)).astype(jnp.int32)
 
     inputs = layer_input.astype(F32)
-    first_scale = rms_scale(inputs)
-    first_normed = links.gather_rows((inputs * first_scale * first_gain).astype(BF))
+    cot_all = links.gather_rows(cotangent)
+    first_rows = (inputs * row_scale(inputs) * first_gain.astype(F32)).astype(BF)
+    first_normed = after(links.gather_rows(first_rows), cot_all)
 
     qkv_pre = dot_nn(first_normed, qkv_full)
-    cot_all = links.gather_rows(after(cotangent, qkv_pre))
     attended, queries, keys, vals = attention_forward(
         heads, groups, masks, segs, base, qkv_pre, cosine, sine
     )
-    residual = inputs + links.scatter_rows(dot_nt(attended, out_full))
-    second_scale = rms_scale(residual)
-    cot_turned = cot_all.T
-    second_rows = (residual * second_scale * second_gain).astype(BF)
-    second_normed = links.gather_rows(after(second_rows, cot_turned))
-
-    second_turned = second_normed.T
-    sums = None
-    mlp_sums = []
-    later = []
-    for index, full in enumerate(mlp_full):
-        halves = 2 if index < HOPS and links.by_hops else 1
-        if later:
-            full = after(full, later.pop(0))
-        *grads, back_sum, out_sum = chunk_pass(
-            links.order if halves == 2 else jnp.arange(links.slabs, dtype=jnp.int32),
-            halves,
-            second_normed,
-            cot_all,
-            full,
-            second_turned,
-            cot_turned,
-            sums,
-            index == len(mlp_full) - 1,
-        )
-        sums = (back_sum, out_sum)
-        if halves == 2:
-            part, later = links.sum_slabs(*grads)
-        else:
-            part = scatter_slabs(grads[0])
-        mlp_sums.append(part)
-    if later:
-        back_sum = after(back_sum, *later)
-    second_back = links.scatter_rows(back_sum)
-    cot_float = cotangent.astype(F32)
-    residual_back = cot_float + norm_back(residual, second_scale, second_gain, second_back)
-    branch_back = links.gather_rows(residual_back.astype(BF))
+    residual, second_normed = links.mid_forward(attended, out_full, layer_input, second_gain)
+
+    widths = [own.shape[1] for own in own_mlp]
+    (back_sum, output), mlp_sums, slabs = links.chunks(
+        second_normed,
+        cot_all,
+        [(*pair, width) for pair, width in zip(mlp_full, widths)],
+        residual,
+    )
+    residual_back, branch_back, total = links.mid_backward(
+        back_sum, residual, cotangent, second_gain, slabs
+    )
+    if total is not None:
+        mlp_sums = [mlp_sums[0], total, scatter_slabs(after(mlp_sums[2], branch_back))]
     attended_back = dot_nn(branch_back, out_full).astype(BF)
-    output = (residual + links.scatter_rows(out_sum)).astype(BF)
     qkv_back = attention_backward(
         heads, groups, masks, segs, base, queries, keys, vals, attended_back, cosine, sine
     )
-    first_back = links.scatter_rows(dot_nt(qkv_back, qkv_full))
-    attn_grads = pair_grads(first_normed, after(qkv_back, *mlp_sums), branch_back, attended)
-    attn_sum = scatter_slabs(attn_grads)
+    input_grad, attn_sum = links.end_backward(
+        qkv_back,
+        qkv_full,
+        layer_input,
+        first_gain,
+        residual_back,
+        (first_normed, qkv_back, branch_back, attended),
+    )
     qkv_sum = attn_sum[:, :qkv_width]
-    input_grad = residual_back + norm_back(inputs, first_scale, first_gain, first_back)
 
     thirds = [
         [part[:, at * part.shape[1] // 3 : (at + 1) * part.shape[1] // 3] for part in mlp_sums]

time: 700 us -> 657 us (0.939)
  Pallas kernels: 182 us -> 477 us
  waiting for transfers between devices: 266 us -> 43.4 us
  starting transfers between devices: 58 us -> 10.3 us
  other arithmetic: 49.6 us -> 19.2 us
  local copies, waits for them, and re-layouts: 73.2 us -> 53.3 us
  matrix products: 26.1 us -> 10.9 us
    pallas_call x4 -> x7, Pallas kernels: 129 us -> 424 us  [the longest x3 191 us: chunk_pass(): pl.pallas_call(functools.partial(chunk_kernel, (steps, slabs, first, last...]
    ppermute x32 -> x8, waiting for transfers between devices: 191 us -> 43.2 us  [by_tp(): return lax.ppermute(value, 'tp', pairs)]
    ppermute x7 -> x0, waiting for transfers between devices: 49.5 us -> none  [by_fsdp(): return lax.ppermute(value, 'fsdp', pairs)]
    ppermute x32 -> x8, starting transfers between devices: 39.3 us -> 10.1 us  [by_tp(): return lax.ppermute(value, 'tp', pairs)]
    reduce_scatter x3 -> x1, waiting for transfers between devices: 24.5 us -> 0.01 us  [scatter_slabs(): lax.psum_scatter(grads, 'fsdp', scatter_dimension=0, tiled=True).astype(F32)]
    ppermute x7 -> x0, starting transfers between devices: 18.4 us -> none  [by_fsdp(): return lax.ppermute(value, 'fsdp', pairs)]
    convert_element_type x5 -> x0, other arithmetic: 15.7 us -> none  [the longest x1 8.61 us: sum_slabs(): low = sums.astype(BF)]
    dot_general x2 -> x0, matrix products: 13.7 us -> none  [dot_nt(): lax.dot_general(left, right, (((1,), (1,)), ((), ())), preferred_element_...]
  transfers between devices with their start and end apart: 46 -> 13, of which waited for: 26 -> 4; matrix products, arithmetic and copies ran while one was open for 18% -> 8% of each run, Pallas kernels for 20% -> 49%
where the time goes in v2:
time: 657 us; the launch traced here: 652 us
  Pallas kernels  477 us (73%)
  local copies, waits for them, and re-layouts  53.3 us (8%)
  waiting for transfers between devices  43.4 us (7%)
  blocking collectives  23.6 us (4%)
  other arithmetic  19.2 us (3%)
  between operations  14.5 us (2%)
  matrix products  10.9 us (2%)
  starting transfers between devices  10.3 us (2%)
    pallas_call x3, Pallas kernels, chunk_pass(): pl.pallas_call(functools.partial(chunk_kernel, (steps, slabs, first, last...  191 us
    pallas_call x1, Pallas kernels, mid_backward(): pl.pallas_call(mid_backward_kernel, name='mid_backward', out_shape=(jax.S...  83.7 us
    pallas_call x1, Pallas kernels, mid_forward(): pl.pallas_call(mid_forward_kernel, name='mid_forward', out_shape=(jax.Sha...  76.4 us
    pallas_call x1, Pallas kernels, end_backward(): pl.pallas_call(end_backward_kernel, name='end_backward', out_shape=(jax.S...  60.3 us
    ppermute x8, waiting for transfers between devices, by_tp(): return lax.ppermute(value, 'tp', pairs)  43.2 us
    unnamed x81, local copies, waits for them, and re-layouts  30.8 us
    pallas_call x1, Pallas kernels, attention_backward(): pl.pallas_call(functools.partial(attn_bwd_kernel, heads, groups), name='a...  29.2 us
    pallas_call x1, Pallas kernels, attention_forward(): pl.pallas_call(functools.partial(attn_fwd_kernel, heads, groups), name='a...  23.8 us
  transfers between devices with their start and end apart: 13, of which 4 were waited for; matrix products, arithmetic and copies ran while one was open for 8% of the time, Pallas kernels for 49%

profile of v2, /device:TPU:0, one launch (start us, length us, event | category | flops | bytes accessed | tf_op | source)
XLA Modules:
  0.0 651.7 jit_solution(5848482212515303404)
XLA Ops:
  7.2 1.1 copy.36
  8.3 1.9 pad_maximum_fusion.5
  10.3 1.6 copy.38
  15.1 1.1 pad_maximum_fusion.2
  16.3 13.8 %all_gather.15 = bf16[2048,2]{0,1:T(2,128)(2,1)S(1)} all-gather(bf16[256,2]{0,1:T(2,128)(2,1)S(1)} %pad_maximum_fusion.8), channel_id=1, replica_groups=mesh['fsdp'=8,'tp'=4] {'fsdp'}, dimensions={0}, use_global_device_ids=true | all-gather | bytes 9216 | tf_op jit(solution)/shard_map/all_gather | solution.py:1185
  31.0 1.7 constant_dynamic-update-slice_fusion.4
  32.7 1.5 collective-permute-start
  34.2 1.4 collective-permute-start.1
  38.3 1.9 fusion.3
  42.2 16.8 %collective-permute-done = bf16[256,2048]{1,0:T(8,128)(2,1)S(1)} collective-permute-done((bf16[256,2048]{1,0:T(8,128)(2,1)}, bf16[256,2048]{1,0:T(8,128)(2,1)S(1)}, u32[]{:S(2)}, u32[]{:S(2)}) %collective-permute-start) | collective-permute-done | bytes 1048608 | tf_op jit(solution)/shard_map/ppermute | solution.py:844
  59.0 1.5 collective-permute-start.2
  61.6 1.5 collective-permute-start.3
  63.1 18.4 %collective-permute-done.4 = bf16[256,2048]{1,0:T(8,128)(2,1)} collective-permute-done((bf16[256,2048]{1,0:T(8,128)(2,1)S(1)}, bf16[256,2048]{1,0:T(8,128)(2,1)}, u32[]{:S(2)}, u32[]{:S(2)}) %collective-permute-start.4) | collective-permute-done | bytes 1048608 | tf_op jit(solution)/shard_map/ppermute | solution.py:844
  82.6 1.5 collective-permute-start.6
  85.2 1.5 collective-permute-start.7
  87.8 2.4 constant_dynamic-update-slice_fusion.2
  90.2 2.4 constant_dynamic-update-slice_fusion.8
  92.5 2.3 constant_dynamic-update-slice_fusion.7
  96.5 7.9 %collective-permute-done.6 = bf16[128,2048]{1,0:T(8,128)(2,1)S(1)} collective-permute-done((bf16[128,2048]{1,0:T(8,128)(2,1)S(1)}, bf16[128,2048]{1,0:T(8,128)(2,1)S(1)}, u32[]{:S(2)}, u32[]{:S(2)}) %collective-permute-start.6) | collective-permute-done | bytes 524320 | tf_op jit(solution)/shard_map/ppermute | solution.py:844
  106.2 6.6 %fusion.5.pre_ref = f32[1024,768]{1,0:T(8,128)S(1)} fusion(bf16[1024,2048]{1,0:T(8,128)(2,1)} %constant_dynamic-update-slice_fusion.left_ref, bf16[2048,1280]{1,0:T(8,128)(2,1)} %all-gather.5.cloned.1.call-done), kind=kOutput, calls=%fused_computation.41 | convolution fusion | flops 3221225472 | bytes 10485760 | tf_op jit(solution)/shard_map/dot_general | solution.py:37
  112.8 23.8 %attn_fwd.1 = (bf16[1024,512]{1,0:T(8,128)(2,1)S(1)}, bf16[2,16,256,64]{3,2,1,0:T(8,128)(2,1)S(1)}, bf16[2,1024,64]{2,1,0:T(8,128)(2,1)S(1)}, bf16[2,1024,64]{2,1,0:T(8,128)(2,1)S(1)}) custom-call(s32[169]{0:T(256)S(1)} %reshape.84.mask_ref, s32[16]{0:T(128)S(1)} %slice.99.seg_ref, s32[1]{0:T(128)} %bitcast.base_ref, f32[1024,768]{1,0:T(8,128)S(1)} %fusion.5.pre_ref, ...), custom_call_target="tpu_custom_call" | custom-call | flops 1000 | bytes 1000 | tf_op jit(solution)/shard_map/attn_fwd/pallas_call | solution.py:303
  139.2 3.0 slice.137.weight_ref
  142.2 76.4 %mid_forward.1 = (f32[256,2048]{1,0:T(8,128)}, bf16[4,256,2048]{2,1,0:T(8,128)(2,1)}) custom-call(bf16[1024,512]{1,0:T(8,128)(2,1)} %copy-done.11, bf16[2048,512]{1,0:T(8,128)(2,1)} %slice.137.weight_ref, bf16[256,2048]{1,0:T(8,128)(2,1)} %input_ref.3, bf16[1,2048]{1,0:T(2,128)(2,1)} %get-tuple-element.119.gain_ref), custom_call_target="tpu_custom_call" | custom-call | flops 80000000000 | bytes 20000000 | tf_op jit(solution)/shard_map/mid_forward/pallas_call | solution.py:944
  218.7 43.2 %chunk_pass.3 = (bf16[4,256,2304]{2,1,0:T(8,128)(2,1)}, f32[1024,2048]{1,0:T(8,128)}, f32[1024,2048]{1,0:T(8,128)}) custom-call(bf16[1024,2048]{1,0:T(8,128)(2,1)} %bitcast.21, bf16[1024,2048]{1,0:T(8,128)(2,1)} %constant_dynamic-update-slice_fusion.5.refs_1_, bf16[2048,2304]{1,0:T(8,128)(2,1)} %all-gather.11.cloned.1.call-done.refs_2_), custom_call_target="tpu_custom_call" | custom-call | flops 28991029248 | bytes 69206016 | tf_op jit(solution)/shard_map/chunk_pass/pallas_call | solution.py:713
  261.9 77.5 %chunk_pass.4 = (bf16[4,256,2304]{2,1,0:T(8,128)(2,1)}, f32[1024,2048]{1,0:T(8,128)}, f32[1024,2048]{1,0:T(8,128)}, bf16[2,256,2304]{2,1,0:T(8,128)(2,1)}) custom-call(bf16[1024,2048]{1,0:T(8,128)(2,1)} %bitcast.22, bf16[1024,2048]{1,0:T(8,128)(2,1)} %constant_dynamic-update-slice_fusion.5.refs_1_, ...), custom_call_target="tpu_custom_call", output_to_operand_aliasing={{1}: (3, {}), {2}: (4, {})} | custom-call | flops 28991029248 | bytes 69206016 | tf_op jit(solution)/shard_map/chunk_pass/pallas_call | solution.py:713
  339.5 70.5 %chunk_pass.5 = (bf16[2048,1536]{1,0:T(8,128)(2,1)}, bf16[1024,2048]{1,0:T(8,128)(2,1)}, bf16[256,2048]{1,0:T(8,128)(2,1)}, f32[256,2304]{1,0:T(8,128)}) custom-call(bf16[1024,2048]{1,0:T(8,128)(2,1)} %bitcast.23, bf16[1024,2048]{1,0:T(8,128)(2,1)} %constant_dynamic-update-slice_fusion.5.refs_1_, bf16[2048,1536]{1,0:T(8,128)(2,1)} %all-gather.7.cloned.1.call-done.refs_2_, ...), custom_call_target="tpu_custom_call" | custom-call | flops 19327352832 | bytes 62914560 | tf_op jit(solution)/shard_map/chunk_pass/pallas_call | solution.py:713
  410.0 1.2 copy-done.3
  411.3 1.6 copy-done.14
  412.8 83.7 %mid_backward.1 = (f32[256,2048]{1,0:T(8,128)S(1)}, bf16[4,256,2048]{2,1,0:T(8,128)(2,1)}, f32[256,2304]{1,0:T(8,128)}) custom-call(bf16[4,256,2048]{2,1,0:T(8,128)(2,1)} %bitcast.26, f32[256,2048]{1,0:T(8,128)S(1)} %copy-done.14, bf16[256,2048]{1,0:T(8,128)(2,1)S(1)} %copy-done.3, bf16[1,2048]{1,0:T(2,128)(2,1)S(1)} %copy-done.8, ...), custom_call_target="tpu_custom_call" | custom-call | flops 80000000000 | bytes 20000000 | tf_op jit(solution)/shard_map/mid_backward/pallas_call | solution.py:1013
  496.6 1.3 copy-done.15
  497.9 3.9 slice.136.weight_ref
  501.8 4.3 convolution_convert_fusion.grad_ref
  506.1 29.2 %attn_bwd.1.first_ref.grads_ref = bf16[1024,768]{1,0:T(8,128)(2,1)S(1)} custom-call(s32[169]{0:T(256)S(1)} %reshape.84.mask_ref, s32[16]{0:T(128)S(1)} %copy-done.10, s32[1]{0:T(128)} %bitcast.base_ref, bf16[2,16,256,64]{3,2,1,0:T(8,128)(2,1)S(1)} %get-tuple-element.46.q_ref, bf16[2,1024,64]{2,1,0:T(8,128)(2,1)S(1)} %copy-done.5, ...), custom_call_target="tpu_custom_call" | custom-call | flops 1000 | bytes 1000 | tf_op jit(solution)/shard_map/attn_bwd/pallas_call | solution.py:323
  535.3 11.9 %pair_hops.1.slabs_ref = bf16[4,256,1280]{2,1,0:T(8,128)(2,1)S(1)} custom-call(bf16[1024,2048]{1,0:T(8,128)(2,1)} %constant_dynamic-update-slice_fusion.left_ref, bf16[1024,768]{1,0:T(8,128)(2,1)S(1)} %attn_bwd.1.first_ref.grads_ref, bf16[1024,2048]{1,0:T(8,128)(2,1)} %bitcast.24, bf16[1024,512]{1,0:T(8,128)(2,1)S(1)} %copy-done.12), custom_call_target="tpu_custom_call" | custom-call | flops 5368709120 | bytes 13631488 | tf_op jit(solution)/shard_map/pair_hops/pallas_call | solution.py:815
  547.2 1.5 copy-done.13
  548.7 60.3 %end_backward.1 = (f32[256,2048]{1,0:T(8,128)S(1)}, f32[256,1280]{1,0:T(8,128)S(1)}) custom-call(bf16[1024,768]{1,0:T(8,128)(2,1)S(1)} %attn_bwd.1.first_ref.grads_ref, bf16[2048,768]{1,0:T(8,128)(2,1)} %slice.136.weight_ref, bf16[256,2048]{1,0:T(8,128)(2,1)S(1)} %copy-done.1, bf16[1,2048]{1,0:T(2,128)(2,1)S(1)} %get-tuple-element.118.gain_ref, ...), custom_call_target="tpu_custom_call" | custom-call | flops 40000000000 | bytes 20000000 | tf_op jit(solution)/shard_map/end_backward/pallas_call | solution.py:1073
  609.0 1.1 slice_bitcast_fusion
  610.1 2.0 copy.39
  612.2 1.1 multiply_reduce_fusion
  614.0 3.0 fusion.9
  617.0 1.5 fusion.8
  618.5 2.4 fusion.14
  620.9 1.6 maximum_bitcast_fusion
  622.5 3.0 copy.40
  625.4 4.9 add_reduce_fusion
  630.4 9.8 %all-reduce = (f32[256]{0:T(256)S(1)}, f32[256]{0:T(256)S(1)}) all-reduce(f32[256]{0:T(256)S(1)} %multiply_reduce_fusion, f32[256]{0:T(256)S(1)} %get-tuple-element.94), channel_id=1, replica_groups=mesh['fsdp'=8,'tp'=4] {'tp'}, use_global_device_ids=true, to_apply=%region_2.0 | all-reduce | flops 512 | bytes 4096 | tf_op jit(solution)/shard_map/psum | solution.py:1287
  641.3 2.3 copy.53
  643.6 1.3 copy.54
  (122 shorter events, 21.1 us)
Async XLA Ops:
  7.2 99.0 %all-gather.5.cloned.1.call-start = ((), (), s32[]{:S(2)}) async-start(), calls=%async_computation.1 | async-start | bytes 5898240 | tf_op jit(solution)/shard_map/all_gather | solution.py:1185
  10.2 2.5 copy-start.16
  10.2 2.5 copy-start.18
  10.3 208.4 %all-gather.11.cloned.1.call-start = ((), (), s32[]{:S(2)}) async-start(), calls=%async_computation.4 | async-start | bytes 10616832 | tf_op jit(solution)/shard_map/all_gather | solution.py:1185
  13.6 1.2 copy-start.21
  13.6 1.5 copy-start.22
  14.7 1.6 copy-start.29
  14.7 1.6 copy-start.31
  14.7 15.4 %copy-start = (bf16[256,2048]{1,0:T(8,128)(2,1)S(1)}, bf16[256,2048]{1,0:T(8,128)(2,1)}, u32[]{:S(2)}) copy-start(bf16[256,2048]{1,0:T(8,128)(2,1)} %input_ref.3) | copy-start | bytes 3145732
  14.8 247.2 %all-gather.9.cloned.1.call-start = ((), (), s32[]{:S(2)}) async-start(), calls=%async_computation.3 | async-start | bytes 10616832 | tf_op jit(solution)/shard_map/all_gather | solution.py:1185
  16.2 19.4 %copy-start.2 = (bf16[256,2048]{1,0:T(8,128)(2,1)S(1)}, bf16[256,2048]{1,0:T(8,128)(2,1)}, u32[]{:S(2)}) copy-start(bf16[256,2048]{1,0:T(8,128)(2,1)} %cot_ref.1) | copy-start | bytes 3145732
  16.2 323.3 %all-gather.7.cloned.1.call-start = ((), (), s32[]{:S(2)}) async-start(), calls=%async_computation.2 | async-start | bytes 7077888 | tf_op jit(solution)/shard_map/all_gather | solution.py:1185
  31.0 5.8 slice-start
  31.0 5.8 slice-start.1
  32.7 5.2 copy-start.26
  32.7 5.2 copy-start.27
  32.7 5.4 copy-start.25
  32.7 5.6 copy-start.28
  32.7 26.3 %collective-permute-start = (bf16[256,2048]{1,0:T(8,128)(2,1)}, bf16[256,2048]{1,0:T(8,128)(2,1)S(1)}, u32[]{:S(2)}, u32[]{:S(2)}) collective-permute-start(bf16[256,2048]{1,0:T(8,128)(2,1)} %get-tuple-element.98), channel_id=1, source_target_pairs={{0,1},{1,0},{2,3},{3,2},{4,5},{5,4},{6,7},{7,6},{8,9},{9,8},{10,11... | collective-permute-start | bytes 3145736 | tf_op jit(solution)/shard_map/ppermute | solution.py:844
  34.2 26.3 %collective-permute-start.1 = (bf16[256,2048]{1,0:T(8,128)(2,1)}, bf16[256,2048]{1,0:T(8,128)(2,1)}, u32[]{:S(2)}, u32[]{:S(2)}) collective-permute-start(bf16[256,2048]{1,0:T(8,128)(2,1)} %get-tuple-element.98), channel_id=1, source_target_pairs={{0,2},{1,3},{2,0},{3,1},{4,6},{5,7},{6,4},{7,5},{8,10},{9,11},{10,... | collective-permute-start | bytes 3145736 | tf_op jit(solution)/shard_map/ppermute | solution.py:844
  35.6 45.9 %collective-permute-start.4 = (bf16[256,2048]{1,0:T(8,128)(2,1)S(1)}, bf16[256,2048]{1,0:T(8,128)(2,1)}, u32[]{:S(2)}, u32[]{:S(2)}) collective-permute-start(bf16[256,2048]{1,0:T(8,128)(2,1)S(1)} %copy-done.2), channel_id=1, source_target_pairs={{0,1},{1,0},{2,3},{3,2},{4,5},{5,4},{6,7},{7,6},{8,9},{9,8},{10,11... | collective-permute-start | bytes 3145736 | tf_op jit(solution)/shard_map/ppermute | solution.py:844
  36.2 47.9 %collective-permute-start.5 = (bf16[256,2048]{1,0:T(8,128)(2,1)S(1)}, bf16[256,2048]{1,0:T(8,128)(2,1)}, u32[]{:S(2)}, u32[]{:S(2)}) collective-permute-start(bf16[256,2048]{1,0:T(8,128)(2,1)S(1)} %copy-done.2), channel_id=1, source_target_pairs={{0,2},{1,3},{2,0},{3,1},{4,6},{5,7},{6,4},{7,5},{8,10},{9,11},{10,... | collective-permute-start | bytes 3145736 | tf_op jit(solution)/shard_map/ppermute | solution.py:844
  37.8 580.7 %reduce-scatter.2.cloned.1.call-start = ((), (), s32[]{:S(2)}) async-start(), calls=%async_computation.5 | async-start | bytes 7077888 | tf_op jit(solution)/shard_map/reduce_scatter | solution.py:1189
  38.1 74.7 %copy-start.9 = (s32[16]{0:T(128)}, s32[16]{0:T(128)S(1)}, u32[]{:S(2)}) copy-start(s32[16]{0:T(128)S(1)} %slice.99.seg_ref) | copy-start | bytes 196
  59.0 35.9 %collective-permute-start.2 = (bf16[128,2048]{1,0:T(8,128)(2,1)S(1)}, bf16[128,2048]{1,0:T(8,128)(2,1)S(1)}, u32[]{:S(2)}, u32[]{:S(2)}) collective-permute-start(bf16[128,2048]{1,0:T(8,128)(2,1)S(1)} %slice.132), channel_id=1, source_target_pairs={{0,2},{1,3},{2,0},{3,1},{4,6},{5,7},{6,4},{7,5},{8,10},{9,11},{10,... | collective-permute-start | bytes 1572872 | tf_op jit(solution)/shard_map/ppermute | solution.py:844
  61.6 34.1 %collective-permute-start.3 = (bf16[128,2048]{1,0:T(8,128)(2,1)S(1)}, bf16[128,2048]{1,0:T(8,128)(2,1)S(1)}, u32[]{:S(2)}, u32[]{:S(2)}) collective-permute-start(bf16[128,2048]{1,0:T(8,128)(2,1)S(1)} %slice.133), channel_id=1, source_target_pairs={{0,1},{1,0},{2,3},{3,2},{4,5},{5,4},{6,7},{7,6},{8,9},{9,8},{10,11... | collective-permute-start | bytes 1572872 | tf_op jit(solution)/shard_map/ppermute | solution.py:844
  82.6 21.9 %collective-permute-start.6 = (bf16[128,2048]{1,0:T(8,128)(2,1)S(1)}, bf16[128,2048]{1,0:T(8,128)(2,1)S(1)}, u32[]{:S(2)}, u32[]{:S(2)}) collective-permute-start(bf16[128,2048]{1,0:T(8,128)(2,1)S(1)} %slice.134), channel_id=1, source_target_pairs={{0,2},{1,3},{2,0},{3,1},{4,6},{5,7},{6,4},{7,5},{8,10},{9,11},{10,... | collective-permute-start | bytes 1572872 | tf_op jit(solution)/shard_map/ppermute | solution.py:844
  85.2 20.1 %collective-permute-start.7 = (bf16[128,2048]{1,0:T(8,128)(2,1)S(1)}, bf16[128,2048]{1,0:T(8,128)(2,1)S(1)}, u32[]{:S(2)}, u32[]{:S(2)}) collective-permute-start(bf16[128,2048]{1,0:T(8,128)(2,1)S(1)} %slice.135), channel_id=1, source_target_pairs={{0,1},{1,0},{2,3},{3,2},{4,5},{5,4},{6,7},{7,6},{8,9},{9,8},{10,11... | collective-permute-start | bytes 1572872 | tf_op jit(solution)/shard_map/ppermute | solution.py:844
  136.6 0.8 copy-start.4
  138.2 1.0 copy-start.11
  339.5 70.5 %copy-start.8 = (bf16[1,2048]{1,0:T(2,128)(2,1)S(1)}, bf16[1,2048]{1,0:T(2,128)(2,1)}, u32[]{:S(2)}) copy-start(bf16[1,2048]{1,0:T(2,128)(2,1)} %get-tuple-element.119.gain_ref) | copy-start | bytes 12292
  410.0 1.2 copy-start.3
  411.3 1.6 copy-start.14
  496.6 1.3 copy-start.15
  497.9 3.9 copy-start.33
  501.8 4.3 copy-start.5
  501.8 4.3 copy-start.7
  501.8 4.3 copy-start.10
  506.1 29.2 %copy-start.12 = (bf16[1024,512]{1,0:T(8,128)(2,1)S(1)}, bf16[1024,512]{1,0:T(8,128)(2,1)}, u32[]{:S(2)}) copy-start(bf16[1024,512]{1,0:T(8,128)(2,1)} %copy-done.11) | copy-start | bytes 3145732
  535.3 13.4 %copy-start.1 = (bf16[256,2048]{1,0:T(8,128)(2,1)S(1)}, bf16[256,2048]{1,0:T(8,128)(2,1)}, u32[]{:S(2)}) copy-start(bf16[256,2048]{1,0:T(8,128)(2,1)} %input_ref.3) | copy-start | bytes 3145732
  547.2 1.5 copy-start.13
  609.0 3.2 copy-start.23
  609.0 3.2 copy-start.24
  614.0 3.1 copy-start.20
  618.5 2.4 copy-start.19
  622.5 3.0 copy-start.17
  625.4 14.8 %copy-start.30 = (bf16[256]{0:T(256)(128)(2,1)S(1)}, bf16[256]{0:T(256)(128)(2,1)}, u32[]{:S(2)}) copy-start(bf16[256]{0:T(256)(128)(2,1)} %param.25) | copy-start | bytes 1540
  625.4 15.3 %copy-start.32 = (bf16[256]{0:T(256)(128)(2,1)S(1)}, bf16[256]{0:T(256)(128)(2,1)}, u32[]{:S(2)}) copy-start(bf16[256]{0:T(256)(128)(2,1)} %param.20) | copy-start | bytes 1540
  (1 other events, 0.8 us)
Sparse Core Ops, SparseCore 0:
  10.4 58.7 all-gather.4
  71.4 89.4 all-gather.10
  163.1 89.1 all-gather.8
  254.4 83.7 all-gather.6
  498.0 76.4 reduce-scatter.1

commit v3 on v2

--- a/solution.py
+++ b/solution.py
@@ -15,8 +15,7 @@
 TRUNK = 256
 BRANCHES = 4
 EPSILON = 1e-05
-PARTS = (3, 3, 2)
-EARLY = 1
+PARTS = (2, 3, 3)
 NEG = -1e30
 BF = jnp.bfloat16
 F32 = jnp.float32
@@ -471,38 +470,52 @@
 
 
 def chunk_kernel(cfg, *refs):
-    steps, slabs, first, last, cores, job, owners = cfg
+    steps, slabs, first, last, cores, job, offset = cfg
     refs = list(refs)
     take = lambda count: [refs.pop(0) for _ in range(count)]
-    rows_ref, cot_ref, full_ref = take(3)
+    rows_ref, cot_ref, source_ref = take(3)
     if not first:
         back_in_ref, out_in_ref = take(2)
     if job == "far":
         (slabs_ref,) = take(1)
     if job == "near":
         slabs_ref, moved_ref = take(2)
-    if owners:
-        (residual_ref,) = take(1)
     grad_ref, back_ref, out_ref = take(3)
     if job == "far":
         (moved_ref,) = take(1)
     if job == "near":
         (total_ref,) = take(1)
-    pair_ref, hidden_ref = take(2)
+    pair_ref, hidden_ref, full_ref, full_sem = take(4)
     if cores:
         mine_ref, theirs_ref, core_send, core_recv = take(4)
     if job:
         job_recv, job_send_sem, job_recv_sem, load_sem = take(4)
     if job == "near":
         (slab_ref,) = take(1)
-    if owners:
-        part_ref, owned_ref, owner_send, owner_recv = take(4)
 
     step = pl.program_id(0)
     end = steps + slabs - 1
     chunk = hidden_ref.shape[1]
     tile = chunk // steps
     height = rows_ref.shape[1] // slabs
+    fetches = [
+        pltpu.make_async_copy(
+            source_ref.at[:, pl.ds(offset + third * chunk, chunk)],
+            full_ref.at[:, pl.ds(third * chunk, chunk)],
+            full_sem.at[third],
+        )
+        for third in range(3)
+    ]
+
+    @pl.when(step == 0)
+    def _():
+        for fetch in fetches:
+            fetch.start()
+
+    def fetched(at, third):
+        if at == 0:
+            fetches[third].wait()
+
     if cores or job:
         z, core, peers = line_peers()
         far = None
@@ -516,24 +529,9 @@
             loads = [pltpu.make_async_copy(slabs_ref.at[3], slab_ref, load_sem.at[0])]
             near = near_copies(moved_ref, job_recv, job_send_sem, job_recv_sem, peers)
 
-        if owners:
-            fsdp, rank = lax.axis_index("fsdp"), lax.axis_index("tp")
-            beside = rank + 1 - 2 * (rank % 2)
-            row_peers = [(fsdp, beside), (fsdp, (rank + 2) % 4), (fsdp, 3 - rank)]
-
-            def to_owner(piece, columns):
-                return pltpu.make_async_remote_copy(
-                    src_ref=part_ref.at[piece, :, columns],
-                    dst_ref=owned_ref.at[piece - 1, :, columns],
-                    send_sem=owner_send.at[piece - 1],
-                    recv_sem=owner_recv.at[piece - 1],
-                    device_id=row_peers[piece - 1],
-                    device_id_type=MESH,
-                )
-
         @pl.when(step == 0)
         def _():
-            greet(peers + (row_peers if owners else []))
+            greet(peers)
             if job == "far":
                 far.start()
             if job == "near":
@@ -548,8 +546,11 @@
         @pl.when(step == at)
         def _():
             cut = slice(at * tile, (at + 1) * tile)
+            fetched(at, 0)
             gate = dot_nn(rows_ref[...], full_ref[:, cut])
+            fetched(at, 1)
             up = dot_nn(rows_ref[...], full_ref[:, chunk + at * tile : chunk + (at + 1) * tile])
+            fetched(at, 2)
             back = dot_nn(
                 cot_ref[...], full_ref[:, 2 * chunk + at * tile : 2 * chunk + (at + 1) * tile]
             )
@@ -577,13 +578,7 @@
         back = back if first else back_in_ref[...] + back
         out = out if first else out_in_ref[...] + out
         back_ref[...] = back.astype(back_ref.dtype)
-        if owners:
-            columns = pl.ds(pl.multiple_of((step - steps) * height, height), height)
-            part_ref[:, :, columns] = out.astype(BF).reshape(4, -1, height)
-            for piece in (3, 1, 2):
-                to_owner(piece, columns).start()
-        else:
-            out_ref[...] = out.astype(out_ref.dtype)
+        out_ref[...] = out.astype(out_ref.dtype)
         if not cores:
             write(step - steps, grad_ref, None)
 
@@ -640,19 +635,7 @@
             )
 
 
-    if owners:
-
-        @pl.when(step == end)
-        def _():
-            for piece in (1, 2, 3):
-                to_owner(piece, slice(None)).wait()
-            total = residual_ref[...] + part_ref[0].astype(F32)
-            for piece in range(3):
-                total = total + owned_ref[piece].astype(F32)
-            out_ref[...] = total.astype(BF)
-
-
-def chunk_pass(rows, cot, full, at, width, sums, last, cores=False, job=None, operands=(), number=None, residual=None):
+def chunk_pass(rows, cot, full, at, width, sums, last, cores=False, job=None, operands=(), number=None):
     count, depth = rows.shape
     chunk = width // 3
     slabs = 8
@@ -661,7 +644,6 @@
     first = sums is None
     whole = pl.BlockSpec(memory_space=pltpu.VMEM)
     anywhere = pl.BlockSpec(memory_space=pl.ANY)
-    weights = pl.BlockSpec((depth, width), lambda i: (0, at), pipeline_mode=pl.Buffered(1))
 
     def place(i):
         return jnp.maximum(i - steps, 0)
@@ -675,9 +657,14 @@
         grad_shape = jax.ShapeDtypeStruct((depth, width), BF)
         grad_spec = pl.BlockSpec((height, width), lambda i: (place(i), 0))
     out_shapes, out_specs = [grad_shape, total, total], [grad_spec, column, column]
-    in_specs = [whole, whole, weights] + ([] if first else [column, column])
-    scratch = [pltpu.VMEM((count, 2 * chunk), BF), pltpu.VMEM((count, chunk), BF)]
+    in_specs = [whole, whole, anywhere] + ([] if first else [column, column])
     dma = pltpu.SemaphoreType.DMA
+    scratch = [
+        pltpu.VMEM((count, 2 * chunk), BF),
+        pltpu.VMEM((count, chunk), BF),
+        pltpu.VMEM((depth, width), BF),
+        dma((3,)),
+    ]
     if cores:
         scratch += [
             pltpu.VMEM((2, height, width), BF),
@@ -697,21 +684,9 @@
         out_shapes += [jax.ShapeDtypeStruct((height, job_width), F32)]
         out_specs += [whole]
         scratch += [pltpu.VMEM((height, job_width), BF)]
-    if residual is not None:
-        own = residual.shape[0]
-        in_specs += [whole]
-        operands = (*operands, residual)
-        out_shapes[2] = jax.ShapeDtypeStruct((own, depth), BF)
-        out_specs[2] = whole
-        scratch += [
-            pltpu.VMEM((4, own, depth), BF),
-            pltpu.VMEM((3, own, depth), BF),
-            dma((3,)),
-            dma((3,)),
-        ]
     remote = cores or job
     return pl.pallas_call(
-        functools.partial(chunk_kernel, (steps, slabs, first, last, cores, job, residual is not None)),
+        functools.partial(chunk_kernel, (steps, slabs, first, last, cores, job, at)),
         name="chunk_pass",
         out_shape=tuple(out_shapes),
         grid=(steps + slabs,),
@@ -1040,9 +1015,15 @@
 
 
 def end_backward_kernel(
-    grads_ref, weight_ref, input_ref, gain_ref, later_ref, slabs_ref,
-    out_ref, total_ref, part_ref, half_ref, whole_ref, sems, *hop_refs,
+    grads_ref, weight_ref, input_ref, gain_ref, later_ref, residual_ref, rows_ref, slabs_ref,
+    out_ref, sum_ref, total_ref,
+    part_ref, half_ref, whole_ref, sems, rows_part_ref, rows_half_ref, rows_whole_ref, rows_sems,
+    load_sem, *hop_refs,
 ):
+    loads = [
+        pltpu.make_async_copy(rows_ref.at[piece], rows_part_ref.at[piece], load_sem.at[piece])
+        for piece in range(4)
+    ]
     peers = swap_peers()
     rows = input_ref.shape[0]
     hops = Hops(slabs_ref, total_ref, *hop_refs)
@@ -1050,6 +1031,9 @@
     hops.begin()
 
     def meanwhile(stage):
+        if stage == 0:
+            for load in loads:
+                load.start()
         if stage == 1:
             hops.onward()
 
@@ -1061,13 +1045,22 @@
     summed = sum_pieces(
         part_ref, make, half_ref, whole_ref, sems.at[0], sems.at[1], peers, meanwhile
     )
-    out_ref[...] = later_ref[...] + row_grads(
-        input_ref[...].astype(F32), gain_ref[...].astype(F32), summed
-    )
+
+    def finish(stage):
+        if stage == 0:
+            out_ref[...] = later_ref[...] + row_grads(
+                input_ref[...].astype(F32), gain_ref[...].astype(F32), summed
+            )
+
+    summed_rows = sum_pieces(
+        rows_part_ref, lambda piece: loads[piece].wait(), rows_half_ref, rows_whole_ref,
+        rows_sems.at[0], rows_sems.at[1], peers, finish,
+    )
+    sum_ref[...] = (residual_ref[...] + summed_rows).astype(BF)
     hops.finish()
 
 
-def end_backward(grads, weight, inputs, gain, later, slabs):
+def end_backward(grads, weight, inputs, gain, later, residual, out_part, slabs):
     rows, width = inputs.shape
     _, height, job_width = slabs.shape
     return pl.pallas_call(
@@ -1075,15 +1068,21 @@
         name="end_backward",
         out_shape=(
             jax.ShapeDtypeStruct((rows, width), F32),
+            jax.ShapeDtypeStruct((rows, width), BF),
             jax.ShapeDtypeStruct((height, job_width), F32),
         ),
-        in_specs=[VMEM] * 5 + [pl.BlockSpec(memory_space=pl.ANY)],
-        out_specs=(VMEM, VMEM),
+        in_specs=[VMEM] * 6 + [pl.BlockSpec(memory_space=pl.ANY)] * 2,
+        out_specs=(VMEM,) * 3,
         scratch_shapes=[
             pltpu.VMEM((4, rows, width), BF),
             pltpu.VMEM((2, rows // 2, width), BF),
             pltpu.VMEM((2, rows, width), BF),
             pltpu.SemaphoreType.DMA((2, 4)),
+            pltpu.VMEM((4, rows, width), BF),
+            pltpu.VMEM((2, rows // 2, width), BF),
+            pltpu.VMEM((2, rows, width), BF),
+            pltpu.SemaphoreType.DMA((2, 4)),
+            pltpu.SemaphoreType.DMA((4,)),
             *hop_scratch(height, job_width),
         ],
         compiler_params=pltpu.CompilerParams(
@@ -1092,7 +1091,9 @@
         cost_estimate=pl.CostEstimate(
             flops=40_000_000_000, bytes_accessed=20_000_000, transcendentals=0
         ),
-    )(grads, weight, inputs, gain, later, slabs)
+    )(
+        grads, weight, inputs, gain, later, residual, out_part.reshape(4, rows, width), slabs
+    )
 
 
 class Line:
@@ -1124,7 +1125,7 @@
         grads, gathered, total = mid_backward(back, residual, cot, gain, slabs)
         return grads, gathered.reshape(-1, gathered.shape[-1]), total
 
-    def chunks(self, rows, cot, blocks, residual):
+    def chunks(self, rows, cot, blocks):
         (full, at, width), second, third = blocks
         slabs, *sums = chunk_pass(rows, cot, full, at, width, None, False, True, None, (), 4)
         first = slabs
@@ -1134,12 +1135,13 @@
         )
         full, at, width = third
         grads, *sums, total = chunk_pass(
-            rows, cot, full, at, width, sums, True, False, "near", (first, moved), 6, residual
+            rows, cot, full, at, width, sums, True, False, "near", (first, moved), 6
         )
         return sums, [total, None, grads], slabs
 
-    def end_backward(self, grads, weight, inputs, gain, later, operands):
-        return end_backward(grads, weight, inputs, gain, later, pair_hops(*operands))
+    def end_backward(self, grads, weight, inputs, gain, later, residual, out_part, operands):
+        slabs = pair_hops(*operands)
+        return end_backward(grads, weight, inputs, gain, later, residual, out_part, slabs)
 
 
 class Plain:
@@ -1161,24 +1163,24 @@
         normed = self.gather_rows(normed.astype(BF))
         return residual, normed
 
-    def chunks(self, rows, cot, blocks, residual):
+    def chunks(self, rows, cot, blocks):
         sums = None
         parts = []
         for full, at, width in blocks:
             grads, *sums = chunk_pass(rows, cot, full, at, width, sums, len(parts) == len(blocks) - 1)
             parts.append(scatter_slabs(grads))
-        back, out = sums
-        return (back, (residual + self.scatter_rows(out)).astype(BF)), parts, None
+        return sums, parts, None
 
     def mid_backward(self, back, residual, cot, gain, slabs):
         grads = row_grads(residual, gain.astype(F32), self.scatter_rows(back))
         grads = cot.astype(F32) + grads
         return grads, self.gather_rows(grads.astype(BF)), None
 
-    def end_backward(self, grads, weight, inputs, gain, later, operands):
+    def end_backward(self, grads, weight, inputs, gain, later, residual, out_part, operands):
+        output = (residual + self.scatter_rows(out_part)).astype(BF)
         sums = scatter_slabs(pair_grads(*operands))
         back = self.scatter_rows(dot_nt(grads, weight))
-        return later + row_grads(inputs.astype(F32), gain.astype(F32), back), sums
+        return later + row_grads(inputs.astype(F32), gain.astype(F32), back), output, sums
 
 
 def gather_slabs(shard):
@@ -1218,15 +1220,15 @@
     first_gain, second_gain = gain_rows[:, 0][None, :], gain_rows[:, 1][None, :]
     own_qkv = jnp.concatenate([query_weight, key_weight, value_weight], axis=1)
     attn_full = gather_slabs(jnp.concatenate([own_qkv, out_weight.T], axis=1))
-    qkv_full, out_full = attn_full[:, :qkv_width], attn_full[:, qkv_width:]
+    out_full = attn_full[:, qkv_width:]
+    qkv_full = lax.optimization_barrier(attn_full[:, :qkv_width])
     own_down = down_weight.T
     own_mlp = [
         jnp.concatenate([gate_weight[:, cut], up_weight[:, cut], own_down[:, cut]], axis=1)
         for cut in map(slice, edges[:-1], edges[1:])
     ]
-    early = gather_slabs(jnp.concatenate(own_mlp[:EARLY], axis=1))
-    mlp_full = [(early, place) for place in range(EARLY)]
-    mlp_full += [(gather_slabs(own), 0) for own in own_mlp[EARLY:]]
+    early = gather_slabs(jnp.concatenate(own_mlp[:2], axis=1))
+    mlp_full = [(early, 0), (early, own_mlp[0].shape[1]), (gather_slabs(own_mlp[2]), 0)]
 
     positions = links.row_order(path_positions)
     angles = positions.astype(F32)[:, None] * jnp.asarray(inverse_freq(HD))[None, :]
@@ -1246,14 +1248,15 @@
     attended, queries, keys, vals = attention_forward(
         heads, groups, masks, segs, base, qkv_pre, cosine, sine
     )
-    residual, second_normed = links.mid_forward(attended, out_full, layer_input, second_gain)
+    residual, second_normed = links.mid_forward(
+        after(attended, qkv_full), out_full, layer_input, second_gain
+    )
 
     widths = [own.shape[1] for own in own_mlp]
-    (back_sum, output), mlp_sums, slabs = links.chunks(
+    (back_sum, out_part), mlp_sums, slabs = links.chunks(
         second_normed,
         cot_all,
         [(*pair, width) for pair, width in zip(mlp_full, widths)],
-        residual,
     )
     residual_back, branch_back, total = links.mid_backward(
         back_sum, residual, cotangent, second_gain, slabs
@@ -1264,26 +1267,42 @@
     qkv_back = attention_backward(
         heads, groups, masks, segs, base, queries, keys, vals, attended_back, cosine, sine
     )
-    input_grad, attn_sum = links.end_backward(
+    thirds = [
+        [part[:, at * part.shape[1] // 3 : (at + 1) * part.shape[1] // 3] for part in mlp_sums]
+        for at in range(3)
+    ]
+    room = jnp.zeros_like(thirds[0][2])
+    gate_sum, up_sum, down_sum = (
+        jnp.concatenate([parts[0], parts[1], room], axis=1) for parts in thirds
+    )
+    down_sum = down_sum.T
+    mlp_parts = [
+        jnp.sum(
+            (own * part)[:, : 2 * own.shape[1] // 3].astype(F32), axis=1
+        )
+        for own, part in zip([own.astype(F32) for own in own_mlp], mlp_sums)
+    ]
+    early_part = mlp_parts[0] + mlp_parts[1]
+    residual_back, gate_sum, up_sum, down_sum, early_part = lax.optimization_barrier(
+        (residual_back, gate_sum, up_sum, down_sum, early_part)
+    )
+    input_grad, output, attn_sum = links.end_backward(
         qkv_back,
         qkv_full,
         layer_input,
         first_gain,
         residual_back,
+        residual,
+        out_part,
         (first_normed, qkv_back, branch_back, attended),
     )
     qkv_sum = attn_sum[:, :qkv_width]
 
-    thirds = [
-        [part[:, at * part.shape[1] // 3 : (at + 1) * part.shape[1] // 3] for part in mlp_sums]
-        for at in range(3)
-    ]
-    gate_sum, up_sum = jnp.concatenate(thirds[0], axis=1), jnp.concatenate(thirds[1], axis=1)
-    down_sum = jnp.concatenate(thirds[2], axis=1).T
+    gate_sum = lax.dynamic_update_slice(gate_sum, thirds[0][2], (0, edges[2]))
+    up_sum = lax.dynamic_update_slice(up_sum, thirds[1][2], (0, edges[2]))
+    down_sum = lax.dynamic_update_slice(down_sum, thirds[2][2].T, (edges[2], 0))
     attn_part = jnp.sum(own_qkv.astype(F32) * qkv_sum, axis=1)
-    mlp_part = jnp.sum(
-        gate_weight.astype(F32) * gate_sum + up_weight.astype(F32) * up_sum, axis=1
-    )
+    mlp_part = early_part + mlp_parts[2]
     attn_total, mlp_total = lax.psum((attn_part, mlp_part), "tp")
     return (
         output,

time: 657 us -> 633 us (0.963)
  Pallas kernels: 477 us -> 439 us
  waiting for transfers between devices: 43.4 us -> 59.4 us
    pallas_call x3, Pallas kernels: 191 us -> 126 us  [chunk_pass(): pl.pallas_call(functools.partial(chunk_kernel, (steps, slabs, first, last...]
    pallas_call x1, Pallas kernels: 60.3 us -> 88.2 us  [end_backward(): pl.pallas_call(end_backward_kernel, name='end_backward', out_shape=(jax.S...]
    all_gather x4 -> x3, waiting for transfers between devices: 0.06 us -> 15.3 us  [gather_slabs(): return lax.all_gather(shard, 'fsdp', axis=0, tiled=True)]
    unnamed x81 -> x95, local copies, waits for them, and re-layouts: 30.8 us -> 28.1 us
  transfers between devices with their start and end apart: 13 -> 12, of which waited for: 4 -> 4; matrix products, arithmetic and copies ran while one was open for 8% -> 8% of each run, Pallas kernels for 49% -> 50%
where the time goes in v3:
time: 633 us; the launch traced here: 624 us
  Pallas kernels  439 us (69%)
  waiting for transfers between devices  59.4 us (9%)
  local copies, waits for them, and re-layouts  51.6 us (8%)
  blocking collectives  23.5 us (4%)
  other arithmetic  16.2 us (3%)
  between operations  14.6 us (2%)
  starting transfers between devices  10.5 us (2%)
  matrix products  8.68 us (1%)
    pallas_call x3, Pallas kernels, chunk_pass(): pl.pallas_call(functools.partial(chunk_kernel, (steps, slabs, first, last...  126 us
    pallas_call x1, Pallas kernels, end_backward(): pl.pallas_call(end_backward_kernel, name='end_backward', out_shape=(jax.S...  88.2 us
    pallas_call x1, Pallas kernels, mid_backward(): pl.pallas_call(mid_backward_kernel, name='mid_backward', out_shape=(jax.S...  83 us
    pallas_call x1, Pallas kernels, mid_forward(): pl.pallas_call(mid_forward_kernel, name='mid_forward', out_shape=(jax.Sha...  77.1 us
    ppermute x8, waiting for transfers between devices, by_tp(): return lax.ppermute(value, 'tp', pairs)  44.1 us
    pallas_call x1, Pallas kernels, attention_backward(): pl.pallas_call(functools.partial(attn_bwd_kernel, heads, groups), name='a...  28.9 us
    unnamed x95, local copies, waits for them, and re-layouts  28.1 us
    pallas_call x1, Pallas kernels, attention_forward(): pl.pallas_call(functools.partial(attn_fwd_kernel, heads, groups), name='a...  23.8 us
  transfers between devices with their start and end apart: 12, of which 4 were waited for; matrix products, arithmetic and copies ran while one was open for 8% of the time, Pallas kernels for 50%

profile of v3, /device:TPU:0, one launch (start us, length us, event | category | flops | bytes accessed | tf_op | source)
XLA Modules:
  0.0 623.7 jit_solution(8917171296175807555)
XLA Ops:
  7.2 1.2 copy.36
  8.4 1.9 pad_maximum_fusion.3
  11.1 1.8 fusion.16
  12.8 1.7 fusion.17
  15.3 1.9 fusion.13
  19.2 1.3 copy-done.17
  20.9 1.2 pad_maximum_fusion
  22.2 13.6 %all_gather.12 = bf16[2048,2]{0,1:T(2,128)(2,1)S(1)} all-gather(bf16[256,2]{0,1:T(2,128)(2,1)S(1)} %pad_maximum_fusion.8), channel_id=1, replica_groups=mesh['fsdp'=8,'tp'=4] {'fsdp'}, dimensions={0}, use_global_device_ids=true | all-gather | bytes 9216 | tf_op jit(solution)/shard_map/all_gather | solution.py:1187
  36.8 1.6 constant_dynamic-update-slice_fusion.4
  38.4 1.5 collective-permute-start
  39.9 1.5 collective-permute-start.1
  42.8 1.9 fusion.7
  46.7 17.8 %collective-permute-done = bf16[256,2048]{1,0:T(8,128)(2,1)S(1)} collective-permute-done((bf16[256,2048]{1,0:T(8,128)(2,1)}, bf16[256,2048]{1,0:T(8,128)(2,1)S(1)}, u32[]{:S(2)}, u32[]{:S(2)}) %collective-permute-start) | collective-permute-done | bytes 1048608 | tf_op jit(solution)/shard_map/ppermute | solution.py:819
  64.6 1.6 collective-permute-start.2
  67.3 1.5 collective-permute-start.3
  68.9 18.3 %collective-permute-done.4 = bf16[256,2048]{1,0:T(8,128)(2,1)} collective-permute-done((bf16[256,2048]{1,0:T(8,128)(2,1)S(1)}, bf16[256,2048]{1,0:T(8,128)(2,1)}, u32[]{:S(2)}, u32[]{:S(2)}) %collective-permute-start.4) | collective-permute-done | bytes 1048608 | tf_op jit(solution)/shard_map/ppermute | solution.py:819
  88.2 1.6 collective-permute-start.6
  89.9 1.1 slice.147
  91.0 1.6 collective-permute-start.7
  93.6 2.3 constant_dynamic-update-slice_fusion.2
  95.9 2.3 constant_dynamic-update-slice_fusion.8
  98.2 2.3 constant_dynamic-update-slice_fusion.7
  102.3 7.9 %collective-permute-done.6 = bf16[128,2048]{1,0:T(8,128)(2,1)S(1)} collective-permute-done((bf16[128,2048]{1,0:T(8,128)(2,1)S(1)}, bf16[128,2048]{1,0:T(8,128)(2,1)S(1)}, u32[]{:S(2)}, u32[]{:S(2)}) %collective-permute-start.6) | collective-permute-done | bytes 524320 | tf_op jit(solution)/shard_map/ppermute | solution.py:819
  111.9 2.2 slice.148.weight_ref
  115.0 3.4 fusion.21.pre_ref
  118.5 23.8 %attn_fwd.1 = (bf16[1024,512]{1,0:T(8,128)(2,1)S(1)}, bf16[2,16,256,64]{3,2,1,0:T(8,128)(2,1)S(1)}, bf16[2,1024,64]{2,1,0:T(8,128)(2,1)S(1)}, bf16[2,1024,64]{2,1,0:T(8,128)(2,1)S(1)}) custom-call(s32[169]{0:T(256)S(1)} %reshape.87.mask_ref, s32[16]{0:T(128)S(1)} %slice.108.seg_ref, s32[1]{0:T(128)} %bitcast.base_ref, f32[1024,768]{1,0:T(8,128)S(1)} %fusion.21.pre_ref, ...), custom_call_target="tpu_custom_call" | custom-call | flops 1000 | bytes 1000 | tf_op jit(solution)/shard_map/attn_fwd/pallas_call | solution.py:302
  142.3 3.8 slice.149.weight_ref
  146.1 77.1 %mid_forward.1 = (f32[256,2048]{1,0:T(8,128)}, bf16[4,256,2048]{2,1,0:T(8,128)(2,1)}) custom-call(bf16[1024,512]{1,0:T(8,128)(2,1)} %copy-done.9, bf16[2048,512]{1,0:T(8,128)(2,1)} %slice.149.weight_ref, bf16[256,2048]{1,0:T(8,128)(2,1)} %input_ref.3, bf16[1,2048]{1,0:T(2,128)(2,1)} %get-tuple-element.141.gain_ref), custom_call_target="tpu_custom_call" | custom-call | flops 80000000000 | bytes 20000000 | tf_op jit(solution)/shard_map/mid_forward/pallas_call | solution.py:919
  223.2 34.5 %chunk_pass.3 = (bf16[4,256,1536]{2,1,0:T(8,128)(2,1)}, f32[1024,2048]{1,0:T(8,128)}, f32[1024,2048]{1,0:T(8,128)}) custom-call(bf16[1024,2048]{1,0:T(8,128)(2,1)} %bitcast.30, bf16[1024,2048]{1,0:T(8,128)(2,1)} %constant_dynamic-update-slice_fusion.5.refs_1_, bf16[2048,3840]{1,0:T(8,128)(2,1)} %all-gather.8.cloned.1.call-done.refs_2_), custom_call_target="tpu_custom_call" | custom-call | flops 19327352832 | bytes 62914560 | tf_op jit(solution)/shard_map/chunk_pass/pallas_call | solution.py:688
  257.7 47.1 %chunk_pass.4 = (bf16[4,256,2304]{2,1,0:T(8,128)(2,1)}, f32[1024,2048]{1,0:T(8,128)}, f32[1024,2048]{1,0:T(8,128)}, bf16[2,256,1536]{2,1,0:T(8,128)(2,1)}) custom-call(bf16[1024,2048]{1,0:T(8,128)(2,1)} %bitcast.31, bf16[1024,2048]{1,0:T(8,128)(2,1)} %constant_dynamic-update-slice_fusion.5.refs_1_, ...), custom_call_target="tpu_custom_call", output_to_operand_aliasing={{1}: (3, {}), {2}: (4, {})} | custom-call | flops 28991029248 | bytes 69206016 | tf_op jit(solution)/shard_map/chunk_pass/pallas_call | solution.py:688
  304.8 15.3 %all-gather.6.cloned.1.call-done.refs_2_ = bf16[2048,2304]{1,0:T(8,128)(2,1)} async-done(((bf16[256,2304]{1,0:T(8,128)(2,1)}), bf16[2048,2304]{1,0:T(8,128)(2,1)}) %all-gather.6.cloned.1.call-update) | async-done | bytes 9437200 | tf_op jit(solution)/shard_map/all_gather | solution.py:1187
  320.1 44.9 %chunk_pass.5 = (bf16[2048,2304]{1,0:T(8,128)(2,1)}, bf16[1024,2048]{1,0:T(8,128)(2,1)}, bf16[1024,2048]{1,0:T(8,128)(2,1)}, f32[256,1536]{1,0:T(8,128)}) custom-call(bf16[1024,2048]{1,0:T(8,128)(2,1)} %bitcast.32, bf16[1024,2048]{1,0:T(8,128)(2,1)} %constant_dynamic-update-slice_fusion.5.refs_1_, bf16[2048,2304]{1,0:T(8,128)(2,1)} %all-gather.6.cloned.1.call-done.refs_2_, ...), custom_call_target="tpu_custom_call" | custom-call | flops 28991029248 | bytes 69206016 | tf_op jit(solution)/shard_map/chunk_pass/pallas_call | solution.py:688
  365.0 1.2 copy-done.3
  366.2 1.6 copy-done.12
  367.8 83.0 %mid_backward.1 = (f32[256,2048]{1,0:T(8,128)S(1)}, bf16[4,256,2048]{2,1,0:T(8,128)(2,1)}, f32[256,2304]{1,0:T(8,128)}) custom-call(bf16[4,256,2048]{2,1,0:T(8,128)(2,1)} %bitcast.33, f32[256,2048]{1,0:T(8,128)S(1)} %copy-done.12, bf16[256,2048]{1,0:T(8,128)(2,1)S(1)} %copy-done.3, bf16[1,2048]{1,0:T(2,128)(2,1)S(1)} %copy-done.8, ...), custom_call_target="tpu_custom_call" | custom-call | flops 80000000000 | bytes 20000000 | tf_op jit(solution)/shard_map/mid_backward/pallas_call | solution.py:988
  450.8 1.3 copy-done.13
  452.2 5.3 convolution_convert_fusion.grad_ref
  457.5 28.9 %attn_bwd.1.first_ref.grads_ref = bf16[1024,768]{1,0:T(8,128)(2,1)S(1)} custom-call(s32[169]{0:T(256)S(1)} %reshape.87.mask_ref, s32[16]{0:T(128)S(1)} %slice.108.seg_ref, s32[1]{0:T(128)} %bitcast.base_ref, bf16[2,16,256,64]{3,2,1,0:T(8,128)(2,1)S(1)} %get-tuple-element.43.q_ref, bf16[2,1024,64]{2,1,0:T(8,128)(2,1)S(1)} %copy-done.5, ...), custom_call_target="tpu_custom_call" | custom-call | flops 1000 | bytes 1000 | tf_op jit(solution)/shard_map/attn_bwd/pallas_call | solution.py:322
  488.3 3.1 maximum_bitcast_fusion
  491.5 11.8 %pair_hops.1.slabs_ref = bf16[4,256,1280]{2,1,0:T(8,128)(2,1)S(1)} custom-call(bf16[1024,2048]{1,0:T(8,128)(2,1)} %constant_dynamic-update-slice_fusion.left_ref, bf16[1024,768]{1,0:T(8,128)(2,1)S(1)} %attn_bwd.1.first_ref.grads_ref, bf16[1024,2048]{1,0:T(8,128)(2,1)} %bitcast.29, bf16[1024,512]{1,0:T(8,128)(2,1)S(1)} %copy-done.10), custom_call_target="tpu_custom_call" | custom-call | flops 5368709120 | bytes 13631488 | tf_op jit(solution)/shard_map/pair_hops/pallas_call | solution.py:790
  503.3 1.5 copy-done.11
  504.8 88.2 %end_backward.1 = (f32[256,2048]{1,0:T(8,128)}, bf16[256,2048]{1,0:T(8,128)(2,1)S(1)}, f32[256,1280]{1,0:T(8,128)S(1)}) custom-call(bf16[1024,768]{1,0:T(8,128)(2,1)S(1)} %attn_bwd.1.first_ref.grads_ref, bf16[2048,768]{1,0:T(8,128)(2,1)} %copy-done.16, bf16[256,2048]{1,0:T(8,128)(2,1)S(1)} %copy-done.1, bf16[1,2048]{1,0:T(2,128)(2,1)S(1)} %get-tuple-element.140.gain_ref, ...), custom_call_target="tpu_custom_call" | custom-call | flops 40000000000 | bytes 20000000 | tf_op jit(solution)/shard_map/end_backward/pallas_call | solution.py:1066
  595.8 1.4 convert_element_type.59
  597.2 1.4 fusion.3
  599.5 2.9 copy.40
  602.4 9.8 %all-reduce = (f32[256]{0:T(256)S(1)}, f32[256]{0:T(256)S(1)}) all-reduce(f32[256]{0:T(256)S(1)} %multiply_reduce_fusion, f32[256]{0:T(256)S(1)} %add.46), channel_id=1, replica_groups=mesh['fsdp'=8,'tp'=4] {'tp'}, use_global_device_ids=true, to_apply=%region_4.0 | all-reduce | flops 512 | bytes 4096 | tf_op jit(solution)/shard_map/psum | solution.py:1306
  613.4 1.2 slice_dynamic-update-slice_fusion
  615.6 1.3 copy.62
  (138 shorter events, 23.5 us)
Async XLA Ops:
  7.2 3.2 copy-start.27
  7.2 104.7 %all-gather.4.cloned.1.call-start = ((), (), s32[]{:S(2)}) async-start(), calls=%async_computation.1 | async-start | bytes 5898240 | tf_op jit(solution)/shard_map/all_gather | solution.py:1187
  10.3 212.9 %all-gather.8.cloned.1.call-start = ((), (), s32[]{:S(2)}) async-start(), calls=%async_computation.3 | async-start | bytes 17694720 | tf_op jit(solution)/shard_map/all_gather | solution.py:1187
  11.1 6.2 copy-start.28
  19.2 1.4 copy-start.22
  19.2 1.7 copy-start.23
  20.4 1.7 copy-start.37
  20.5 1.7 copy-start.39
  20.5 16.0 %copy-start = (bf16[256,2048]{1,0:T(8,128)(2,1)S(1)}, bf16[256,2048]{1,0:T(8,128)(2,1)}, u32[]{:S(2)}) copy-start(bf16[256,2048]{1,0:T(8,128)(2,1)} %input_ref.3) | copy-start | bytes 3145732
  20.5 299.6 %all-gather.6.cloned.1.call-start = ((), (), s32[]{:S(2)}) async-start(), calls=%async_computation.2 | async-start | bytes 10616832 | tf_op jit(solution)/shard_map/all_gather | solution.py:1187
  22.1 573.7 %reduce-scatter.2.cloned.1.call-start = ((), (), s32[]{:S(2)}) async-start(), calls=%async_computation.4 | async-start | bytes 10616832 | tf_op jit(solution)/shard_map/reduce_scatter | solution.py:1191
  36.4 5.0 copy-start.2
  36.4 6.0 copy-start.34
  36.4 6.0 copy-start.35
  36.4 6.2 copy-start.33
  36.5 6.3 %copy-start.36 = (f32[32]{0:T(128)S(1)}, f32[32]{0:T(128)}, u32[]{:S(2)}) copy-start(f32[32]{0:T(128)} %constant.28.clone) | copy-start | bytes 388
  38.4 26.2 %collective-permute-start = (bf16[256,2048]{1,0:T(8,128)(2,1)}, bf16[256,2048]{1,0:T(8,128)(2,1)S(1)}, u32[]{:S(2)}, u32[]{:S(2)}) collective-permute-start(bf16[256,2048]{1,0:T(8,128)(2,1)} %get-tuple-element.109), channel_id=1, source_target_pairs={{0,1},{1,0},{2,3},{3,2},{4,5},{5,4},{6,7},{7,6},{8,9},{9,8},{10,11... | collective-permute-start | bytes 3145736 | tf_op jit(solution)/shard_map/ppermute | solution.py:819
  39.9 26.3 %collective-permute-start.1 = (bf16[256,2048]{1,0:T(8,128)(2,1)}, bf16[256,2048]{1,0:T(8,128)(2,1)}, u32[]{:S(2)}, u32[]{:S(2)}) collective-permute-start(bf16[256,2048]{1,0:T(8,128)(2,1)} %get-tuple-element.109), channel_id=1, source_target_pairs={{0,2},{1,3},{2,0},{3,1},{4,6},{5,7},{6,4},{7,5},{8,10},{9,11},{10,... | collective-permute-start | bytes 3145736 | tf_op jit(solution)/shard_map/ppermute | solution.py:819
  41.4 45.7 %collective-permute-start.4 = (bf16[256,2048]{1,0:T(8,128)(2,1)S(1)}, bf16[256,2048]{1,0:T(8,128)(2,1)}, u32[]{:S(2)}, u32[]{:S(2)}) collective-permute-start(bf16[256,2048]{1,0:T(8,128)(2,1)S(1)} %copy-done.2), channel_id=1, source_target_pairs={{0,1},{1,0},{2,3},{3,2},{4,5},{5,4},{6,7},{7,6},{8,9},{9,8},{10,11... | collective-permute-start | bytes 3145736 | tf_op jit(solution)/shard_map/ppermute | solution.py:819
  42.0 47.9 %collective-permute-start.5 = (bf16[256,2048]{1,0:T(8,128)(2,1)S(1)}, bf16[256,2048]{1,0:T(8,128)(2,1)}, u32[]{:S(2)}, u32[]{:S(2)}) collective-permute-start(bf16[256,2048]{1,0:T(8,128)(2,1)S(1)} %copy-done.2), channel_id=1, source_target_pairs={{0,2},{1,3},{2,0},{3,1},{4,6},{5,7},{6,4},{7,5},{8,10},{9,11},{10,... | collective-permute-start | bytes 3145736 | tf_op jit(solution)/shard_map/ppermute | solution.py:819
  64.6 35.9 %collective-permute-start.2 = (bf16[128,2048]{1,0:T(8,128)(2,1)S(1)}, bf16[128,2048]{1,0:T(8,128)(2,1)S(1)}, u32[]{:S(2)}, u32[]{:S(2)}) collective-permute-start(bf16[128,2048]{1,0:T(8,128)(2,1)S(1)} %slice.144), channel_id=1, source_target_pairs={{0,2},{1,3},{2,0},{3,1},{4,6},{5,7},{6,4},{7,5},{8,10},{9,11},{10,... | collective-permute-start | bytes 1572872 | tf_op jit(solution)/shard_map/ppermute | solution.py:819
  67.3 34.1 %collective-permute-start.3 = (bf16[128,2048]{1,0:T(8,128)(2,1)S(1)}, bf16[128,2048]{1,0:T(8,128)(2,1)S(1)}, u32[]{:S(2)}, u32[]{:S(2)}) collective-permute-start(bf16[128,2048]{1,0:T(8,128)(2,1)S(1)} %slice.145), channel_id=1, source_target_pairs={{0,1},{1,0},{2,3},{3,2},{4,5},{5,4},{6,7},{7,6},{8,9},{9,8},{10,11... | collective-permute-start | bytes 1572872 | tf_op jit(solution)/shard_map/ppermute | solution.py:819
  88.2 21.9 %collective-permute-start.6 = (bf16[128,2048]{1,0:T(8,128)(2,1)S(1)}, bf16[128,2048]{1,0:T(8,128)(2,1)S(1)}, u32[]{:S(2)}, u32[]{:S(2)}) collective-permute-start(bf16[128,2048]{1,0:T(8,128)(2,1)S(1)} %slice.146), channel_id=1, source_target_pairs={{0,2},{1,3},{2,0},{3,1},{4,6},{5,7},{6,4},{7,5},{8,10},{9,11},{10,... | collective-permute-start | bytes 1572872 | tf_op jit(solution)/shard_map/ppermute | solution.py:819
  91.0 20.1 %collective-permute-start.7 = (bf16[128,2048]{1,0:T(8,128)(2,1)S(1)}, bf16[128,2048]{1,0:T(8,128)(2,1)S(1)}, u32[]{:S(2)}, u32[]{:S(2)}) collective-permute-start(bf16[128,2048]{1,0:T(8,128)(2,1)S(1)} %slice.147), channel_id=1, source_target_pairs={{0,1},{1,0},{2,3},{3,2},{4,5},{5,4},{6,7},{7,6},{8,9},{9,8},{10,11... | collective-permute-start | bytes 1572872 | tf_op jit(solution)/shard_map/ppermute | solution.py:819
  111.9 3.1 copy-start.30
  115.0 3.4 copy-start.16
  142.3 3.8 copy-start.4
  142.3 3.8 copy-start.6
  142.3 3.8 copy-start.9
  320.1 44.9 %copy-start.8 = (bf16[1,2048]{1,0:T(2,128)(2,1)S(1)}, bf16[1,2048]{1,0:T(2,128)(2,1)}, u32[]{:S(2)}) copy-start(bf16[1,2048]{1,0:T(2,128)(2,1)} %get-tuple-element.141.gain_ref) | copy-start | bytes 12292
  366.2 1.6 copy-start.12
  450.8 1.3 copy-start.13
  452.1 5.3 copy-start.5
  452.2 5.3 copy-start.7
  457.5 29.0 %copy-start.15 = (f32[256,1536]{1,0:T(8,128)S(1)}, f32[256,1536]{1,0:T(8,128)}, u32[]{:S(2)}) copy-start(f32[256,1536]{1,0:T(8,128)} %get-tuple-element.60) | copy-start | bytes 4718596
  457.5 29.0 %copy-start.24 = (bf16[256,512]{1,0:T(8,128)(2,1)S(1)}, bf16[256,512]{1,0:T(8,128)(2,1)}, u32[]{:S(2)}) copy-start(bf16[256,512]{1,0:T(8,128)(2,1)} %get-tuple-element.131) | copy-start | bytes 786436
  457.5 29.0 %copy-start.25 = (bf16[256,512]{1,0:T(8,128)(2,1)S(1)}, bf16[256,512]{1,0:T(8,128)(2,1)}, u32[]{:S(2)}) copy-start(bf16[256,512]{1,0:T(8,128)(2,1)} %get-tuple-element.133) | copy-start | bytes 786436
  457.5 29.0 %copy-start.26 = (bf16[256,512]{1,0:T(8,128)(2,1)S(1)}, bf16[256,512]{1,0:T(8,128)(2,1)}, u32[]{:S(2)}) copy-start(bf16[256,512]{1,0:T(8,128)(2,1)} %get-tuple-element.135) | copy-start | bytes 786436
  457.5 29.2 %copy-start.14 = (f32[256,2304]{1,0:T(8,128)S(1)}, f32[256,2304]{1,0:T(8,128)}, u32[]{:S(2)}) copy-start(f32[256,2304]{1,0:T(8,128)} %get-tuple-element.61) | copy-start | bytes 7077892
  488.3 3.1 copy-start.10
  491.5 13.3 %copy-start.1 = (bf16[256,2048]{1,0:T(8,128)(2,1)S(1)}, bf16[256,2048]{1,0:T(8,128)(2,1)}, u32[]{:S(2)}) copy-start(bf16[256,2048]{1,0:T(8,128)(2,1)} %input_ref.3) | copy-start | bytes 3145732
  503.3 1.5 copy-start.11
  593.0 1.9 copy-start.29
  593.0 1.9 copy-start.31
  593.0 1.9 copy-start.32
  599.5 12.7 %copy-start.38 = (bf16[256]{0:T(256)(128)(2,1)S(1)}, bf16[256]{0:T(256)(128)(2,1)}, u32[]{:S(2)}) copy-start(bf16[256]{0:T(256)(128)(2,1)} %param.25) | copy-start | bytes 1540
  599.5 13.3 %copy-start.40 = (bf16[256]{0:T(256)(128)(2,1)S(1)}, bf16[256]{0:T(256)(128)(2,1)}, u32[]{:S(2)}) copy-start(bf16[256]{0:T(256)(128)(2,1)} %param.20) | copy-start | bytes 1540
  613.4 2.2 copy-start.18
  (5 other events, 5.9 us)
Sparse Core Ops, SparseCore 0:
  10.5 58.7 all-gather.3
  71.5 141.2 all-gather.7
  214.4 105.5 all-gather.5
  452.2 132.9 reduce-scatter.1

commit v4 on v3

--- a/solution.py
+++ b/solution.py
@@ -295,6 +295,12 @@
 VMEM = pl.BlockSpec(memory_space=pltpu.VMEM)
 
 
+def loaded(value):
+    return pl.BlockSpec(
+        value.shape, lambda i: (0,) * value.ndim, pipeline_mode=pl.Buffered(1)
+    )
+
+
 def attention_forward(heads, groups, masks, segs, base, pre, cosine, sine):
     rows = pre.shape[0]
     members = heads // groups
@@ -323,7 +329,9 @@
         functools.partial(attn_bwd_kernel, heads, groups),
         name="attn_bwd",
         out_shape=jax.ShapeDtypeStruct((rows, (heads + 2 * groups) * HD), BF),
-        in_specs=[SMEM, SMEM, SMEM, VMEM, VMEM, VMEM, VMEM, VMEM, VMEM],
+        grid=(1,),
+        in_specs=[SMEM, SMEM, SMEM]
+        + [loaded(value) for value in (queries, keys, vals, grads, cosine, sine)],
         out_specs=VMEM,
         scratch_shapes=[
             pltpu.VMEM((groups, blocks, members * SEG, HD), BF),
@@ -476,22 +484,16 @@
     rows_ref, cot_ref, source_ref = take(3)
     if not first:
         back_in_ref, out_in_ref = take(2)
-    if job == "far":
+    if job:
         (slabs_ref,) = take(1)
-    if job == "near":
-        slabs_ref, moved_ref = take(2)
     grad_ref, back_ref, out_ref = take(3)
-    if job == "far":
-        (moved_ref,) = take(1)
-    if job == "near":
+    if job:
         (total_ref,) = take(1)
     pair_ref, hidden_ref, full_ref, full_sem = take(4)
     if cores:
         mine_ref, theirs_ref, core_send, core_recv = take(4)
     if job:
-        job_recv, job_send_sem, job_recv_sem, load_sem = take(4)
-    if job == "near":
-        (slab_ref,) = take(1)
+        hops = Hops(slabs_ref, total_ref, *take(7))
 
     step = pl.program_id(0)
     end = steps + slabs - 1
@@ -518,28 +520,18 @@
 
     if cores or job:
         z, core, peers = line_peers()
-        far = None
-        if job == "far":
-            loads = [
-                pltpu.make_async_copy(slabs_ref.at[1 + at], moved_ref.at[at], load_sem.at[at])
-                for at in range(2)
-            ]
-            far = far_copies(slabs_ref.at[0], job_recv, job_send_sem.at[0], job_recv_sem, z, peers)
-        if job == "near":
-            loads = [pltpu.make_async_copy(slabs_ref.at[3], slab_ref, load_sem.at[0])]
-            near = near_copies(moved_ref, job_recv, job_send_sem, job_recv_sem, peers)
 
         @pl.when(step == 0)
         def _():
             greet(peers)
-            if job == "far":
-                far.start()
-            if job == "near":
-                for copy in near:
-                    copy.start()
             if job:
-                for load in loads:
-                    load.start()
+                hops.begin()
+
+    if job:
+
+        @pl.when(step == steps + 1)
+        def _():
+            hops.onward()
 
     for at in range(steps):
 
@@ -614,28 +606,14 @@
             copies[2].wait_send()
             copies[3].wait_send()
 
-    if job == "far":
+    if job:
 
         @pl.when(step == end)
         def _():
-            for load in loads:
-                load.wait()
-            far.wait_send()
-            far_add(moved_ref, job_recv, job_recv_sem, z, peers)
-
-    if job == "near":
-
-        @pl.when(step == end)
-        def _():
-            loads[0].wait()
-            for copy in near:
-                copy.wait()
-            total_ref[...] = (
-                slab_ref[...].astype(F32) + job_recv[0].astype(F32) + job_recv[1].astype(F32)
-            )
-
-
-def chunk_pass(rows, cot, full, at, width, sums, last, cores=False, job=None, operands=(), number=None):
+            hops.finish()
+
+
+def chunk_pass(rows, cot, full, at, width, sums, last, cores=False, job=False, operands=(), number=None):
     count, depth = rows.shape
     chunk = width // 3
     slabs = 8
@@ -674,16 +652,10 @@
         ]
     if job:
         job_width = operands[0].shape[-1]
-        scratch += [pltpu.VMEM((2, height, job_width), BF), dma((2,)), dma((2,)), dma((2,))]
-    if job == "far":
         in_specs += [anywhere]
-        out_shapes += [jax.ShapeDtypeStruct((2, height, job_width), BF)]
-        out_specs += [whole]
-    if job == "near":
-        in_specs += [anywhere, anywhere]
         out_shapes += [jax.ShapeDtypeStruct((height, job_width), F32)]
         out_specs += [whole]
-        scratch += [pltpu.VMEM((height, job_width), BF)]
+        scratch += hop_scratch(height, job_width)
     remote = cores or job
     return pl.pallas_call(
         functools.partial(chunk_kernel, (steps, slabs, first, last, cores, job, at)),
@@ -949,8 +921,8 @@
 
 
 def mid_backward_kernel(
-    back_ref, residual_ref, cot_ref, gain_ref, slabs_ref,
-    out_ref, all_ref, total_ref,
+    back_ref, residual_ref, cot_ref, gain_ref, weight_ref, slabs_ref,
+    out_ref, all_ref, attended_ref, total_ref,
     part_ref, half_ref, whole_ref, sems, load_sem, *hop_refs,
 ):
     peers = swap_peers()
@@ -958,9 +930,21 @@
     greet(peers + hops.line[1:])
     hops.begin()
 
+    rows = residual_ref.shape[0]
+
+    def project(piece):
+        attended_ref[piece * rows : (piece + 1) * rows] = dot_nn(
+            all_ref[piece], weight_ref[...]
+        ).astype(BF)
+
     def meanwhile(stage):
         if stage == 1:
             hops.onward()
+        if stage == 2:
+            project(0)
+        if stage == 3:
+            project(1)
+            project(2)
 
     order = (3, 1, 2, 0)
     loads = [
@@ -978,11 +962,12 @@
     )
     out_ref[...] = grads
     all_ref[0] = grads.astype(BF)
-    gather_pieces(all_ref, sems.at[2], sems.at[3], peers, idle)
+    gather_pieces(all_ref, sems.at[2], sems.at[3], peers, meanwhile)
+    project(3)
     hops.finish()
 
 
-def mid_backward(back, residual, cot, gain, slabs):
+def mid_backward(back, residual, cot, gain, weight, slabs):
     rows, width = residual.shape
     _, height, job_width = slabs.shape
     return pl.pallas_call(
@@ -991,12 +976,18 @@
         out_shape=(
             jax.ShapeDtypeStruct((rows, width), F32),
             jax.ShapeDtypeStruct((4, rows, width), BF),
+            jax.ShapeDtypeStruct((4 * rows, weight.shape[1]), BF),
             jax.ShapeDtypeStruct((height, job_width), F32),
         ),
         in_specs=[
-            pl.BlockSpec(memory_space=pl.ANY), VMEM, VMEM, VMEM, pl.BlockSpec(memory_space=pl.ANY)
+            pl.BlockSpec(memory_space=pl.ANY),
+            VMEM,
+            VMEM,
+            VMEM,
+            VMEM,
+            pl.BlockSpec(memory_space=pl.ANY),
         ],
-        out_specs=(VMEM,) * 3,
+        out_specs=(VMEM,) * 4,
         scratch_shapes=[
             pltpu.VMEM((4, rows, width), BF),
             pltpu.VMEM((2, rows // 2, width), BF),
@@ -1006,12 +997,12 @@
             *hop_scratch(height, job_width),
         ],
         compiler_params=pltpu.CompilerParams(
-            collective_id=2, has_side_effects=True, vmem_limit_bytes=48 << 20
+            collective_id=2, has_side_effects=True, vmem_limit_bytes=36 << 20
         ),
         cost_estimate=pl.CostEstimate(
             flops=80_000_000_000, bytes_accessed=20_000_000, transcendentals=0
         ),
-    )(back.reshape(4, rows, width), residual, cot, gain, slabs)
+    )(back.reshape(4, rows, width), residual, cot, gain, weight, slabs)
 
 
 def end_backward_kernel(
@@ -1109,6 +1100,16 @@
     def trunk_base(self):
         return self.rank * TRUNK
 
+    def gather_begin(self, rows):
+        return rows, by_tp(rows, X_SWAP), by_tp(rows, Y_SWAP)
+
+    def gather_end(self, pieces, hold):
+        rows, beside, above, _ = lax.optimization_barrier((*pieces, hold))
+        half = rows.shape[0] // 2
+        return jnp.concatenate(
+            [rows, beside, above, by_tp(beside[:half], Y_SWAP), by_tp(above[half:], X_SWAP)]
+        )
+
     def gather_rows(self, rows):
         half = rows.shape[0] // 2
         beside = by_tp(rows, X_SWAP)
@@ -1117,25 +1118,27 @@
             [rows, beside, above, by_tp(beside[:half], Y_SWAP), by_tp(above[half:], X_SWAP)]
         )
 
+    def sum_rows(self, values):
+        values = values + by_tp(values, X_SWAP)
+        return values + by_tp(values, Y_SWAP)
+
     def mid_forward(self, attended, weight, inputs, gain):
         residual, normed = mid_forward(attended, weight, inputs, gain)
         return residual, normed.reshape(-1, normed.shape[-1])
 
-    def mid_backward(self, back, residual, cot, gain, slabs):
-        grads, gathered, total = mid_backward(back, residual, cot, gain, slabs)
-        return grads, gathered.reshape(-1, gathered.shape[-1]), total
+    def mid_backward(self, back, residual, cot, gain, weight, slabs):
+        grads, gathered, attended, total = mid_backward(back, residual, cot, gain, weight, slabs)
+        return grads, gathered.reshape(-1, gathered.shape[-1]), attended, total
 
     def chunks(self, rows, cot, blocks):
         (full, at, width), second, third = blocks
-        slabs, *sums = chunk_pass(rows, cot, full, at, width, None, False, True, None, (), 4)
+        slabs, *sums = chunk_pass(rows, cot, full, at, width, None, False, True, False, (), 4)
         first = slabs
         full, at, width = second
-        slabs, *sums, moved = chunk_pass(
-            rows, cot, full, at, width, sums, False, True, "far", (first,), 5
-        )
+        slabs, *sums = chunk_pass(rows, cot, full, at, width, sums, False, True, False, (), 5)
         full, at, width = third
         grads, *sums, total = chunk_pass(
-            rows, cot, full, at, width, sums, True, False, "near", (first, moved), 6
+            rows, cot, full, at, width, sums, True, False, True, (first,), 6
         )
         return sums, [total, None, grads], slabs
 
@@ -1151,11 +1154,20 @@
     def trunk_base(self):
         return jnp.int32(0)
 
+    def gather_begin(self, rows):
+        return rows
+
+    def gather_end(self, rows, hold):
+        return self.gather_rows(rows)
+
     def gather_rows(self, rows):
         return lax.all_gather(rows, "tp", axis=0, tiled=True)
 
     def scatter_rows(self, partial):
         return lax.psum_scatter(partial.astype(F32), "tp", scatter_dimension=0, tiled=True)
+
+    def sum_rows(self, values):
+        return lax.psum(values, "tp")
 
     def mid_forward(self, attended, weight, inputs, gain):
         residual = inputs.astype(F32) + self.scatter_rows(dot_nt(attended, weight))
@@ -1171,10 +1183,11 @@
             parts.append(scatter_slabs(grads))
         return sums, parts, None
 
-    def mid_backward(self, back, residual, cot, gain, slabs):
+    def mid_backward(self, back, residual, cot, gain, weight, slabs):
         grads = row_grads(residual, gain.astype(F32), self.scatter_rows(back))
         grads = cot.astype(F32) + grads
-        return grads, self.gather_rows(grads.astype(BF)), None
+        gathered = self.gather_rows(grads.astype(BF))
+        return grads, gathered, dot_nn(gathered, weight).astype(BF), None
 
     def end_backward(self, grads, weight, inputs, gain, later, residual, out_part, operands):
         output = (residual + self.scatter_rows(out_part)).astype(BF)
@@ -1240,14 +1253,15 @@
     base = jnp.reshape(links.trunk_base(), (1,)).astype(jnp.int32)
 
     inputs = layer_input.astype(F32)
-    cot_all = links.gather_rows(cotangent)
     first_rows = (inputs * row_scale(inputs) * first_gain.astype(F32)).astype(BF)
-    first_normed = after(links.gather_rows(first_rows), cot_all)
+    first_normed = links.gather_rows(first_rows)
 
     qkv_pre = dot_nn(first_normed, qkv_full)
+    cot_pieces = links.gather_begin(after(cotangent, qkv_pre))
     attended, queries, keys, vals = attention_forward(
         heads, groups, masks, segs, base, qkv_pre, cosine, sine
     )
+    cot_all = links.gather_end(cot_pieces, attended)
     residual, second_normed = links.mid_forward(
         after(attended, qkv_full), out_full, layer_input, second_gain
     )
@@ -1258,12 +1272,11 @@
         cot_all,
         [(*pair, width) for pair, width in zip(mlp_full, widths)],
     )
-    residual_back, branch_back, total = links.mid_backward(
-        back_sum, residual, cotangent, second_gain, slabs
+    residual_back, branch_back, attended_back, total = links.mid_backward(
+        back_sum, residual, cotangent, second_gain, out_full, slabs
     )
     if total is not None:
         mlp_sums = [mlp_sums[0], total, scatter_slabs(after(mlp_sums[2], branch_back))]
-    attended_back = dot_nn(branch_back, out_full).astype(BF)
     qkv_back = attention_backward(
         heads, groups, masks, segs, base, queries, keys, vals, attended_back, cosine, sine
     )
@@ -1303,7 +1316,7 @@
     down_sum = lax.dynamic_update_slice(down_sum, thirds[2][2].T, (edges[2], 0))
     attn_part = jnp.sum(own_qkv.astype(F32) * qkv_sum, axis=1)
     mlp_part = early_part + mlp_parts[2]
-    attn_total, mlp_total = lax.psum((attn_part, mlp_part), "tp")
+    attn_total, mlp_total = links.sum_rows(jnp.stack([attn_part, mlp_part]))
     return (
         output,
         input_grad,

time: 633 us -> 626 us (0.989)
  Pallas kernels: 439 us -> 450 us
  waiting for transfers between devices: 59.4 us -> 49.3 us
  blocking collectives: 23.5 us -> 13.6 us
    pallas_call x3, Pallas kernels: 126 us -> 143 us  [chunk_pass(): pl.pallas_call(functools.partial(chunk_kernel, (steps, slabs, first, last...]
    psum x1 -> x0, blocking collectives: 9.82 us -> none  [body(): attn_total, mlp_total = lax.psum((attn_part, mlp_part), 'tp')]
    ppermute x8 -> x10, waiting for transfers between devices: 44.1 us -> 36 us  [by_tp(): return lax.ppermute(value, 'tp', pairs)]
    unnamed x95 -> x121, local copies, waits for them, and re-layouts: 28.1 us -> 35.1 us
    ppermute x8 -> x10, starting transfers between devices: 10.4 us -> 14.4 us  [by_tp(): return lax.ppermute(value, 'tp', pairs)]
  transfers between devices with their start and end apart: 12 -> 14, of which waited for: 4 -> 7; matrix products, arithmetic and copies ran while one was open for 8% -> 8% of each run, Pallas kernels for 50% -> 50%
where the time goes in v4:
time: 626 us; the launch traced here: 618 us
  Pallas kernels  450 us (72%)
  local copies, waits for them, and re-layouts  57.5 us (9%)
  waiting for transfers between devices  49.3 us (8%)
  other arithmetic  15 us (2%)
  starting transfers between devices  14.6 us (2%)
  between operations  14.6 us (2%)
  blocking collectives  13.6 us (2%)
    pallas_call x3, Pallas kernels, chunk_pass(): pl.pallas_call(functools.partial(chunk_kernel, (steps, slabs, first, last...  143 us
    pallas_call x1, Pallas kernels, end_backward(): pl.pallas_call(end_backward_kernel, name='end_backward', out_shape=(jax.S...  86.6 us
    pallas_call x1, Pallas kernels, mid_backward(): pl.pallas_call(mid_backward_kernel, name='mid_backward', out_shape=(jax.S...  80.5 us
    pallas_call x1, Pallas kernels, mid_forward(): pl.pallas_call(mid_forward_kernel, name='mid_forward', out_shape=(jax.Sha...  74.8 us
    ppermute x10, waiting for transfers between devices, by_tp(): return lax.ppermute(value, 'tp', pairs)  36 us
    unnamed x121, local copies, waits for them, and re-layouts  35.1 us
    pallas_call x1, Pallas kernels, attention_backward(): pl.pallas_call(functools.partial(attn_bwd_kernel, heads, groups), name='a...  29.3 us
    pallas_call x1, Pallas kernels, attention_forward(): pl.pallas_call(functools.partial(attn_fwd_kernel, heads, groups), name='a...  24 us
  transfers between devices with their start and end apart: 14, of which 7 were waited for; matrix products, arithmetic and copies ran while one was open for 8% of the time, Pallas kernels for 50%

profile of v4, /device:TPU:0, one launch (start us, length us, event | category | flops | bytes accessed | tf_op | source)
XLA Modules:
  0.0 617.8 jit_solution(5043541629175247582)
XLA Ops:
  8.4 1.9 pad_maximum_fusion.3
  11.1 1.8 fusion.16
  12.8 1.7 fusion.17
  15.3 1.9 fusion.13
  19.1 1.3 copy-done.30
  22.1 13.6 %all_gather.12 = bf16[2048,2]{0,1:T(2,128)(2,1)S(1)} all-gather(bf16[256,2]{0,1:T(2,128)(2,1)S(1)} %pad_maximum_fusion.9), channel_id=1, replica_groups=mesh['fsdp'=8,'tp'=4] {'fsdp'}, dimensions={0}, use_global_device_ids=true | all-gather | bytes 9216 | tf_op jit(solution)/shard_map/all_gather | solution.py:1200
  36.6 1.6 constant_dynamic-update-slice_fusion.4
  38.3 1.5 collective-permute-start
  39.8 1.4 collective-permute-start.1
  41.3 1.9 fusion.7
  44.2 19.7 %collective-permute-done = bf16[256,2048]{1,0:T(8,128)(2,1)S(1)} collective-permute-done((bf16[256,2048]{1,0:T(8,128)(2,1)}, bf16[256,2048]{1,0:T(8,128)(2,1)S(1)}, u32[]{:S(2)}, u32[]{:S(2)}) %collective-permute-start) | collective-permute-done | bytes 1048608 | tf_op jit(solution)/shard_map/ppermute | solution.py:791
  64.7 1.5 collective-permute-start.2
  66.6 1.5 collective-permute-start.3
  70.2 8.3 %collective-permute-done.2 = bf16[128,2048]{1,0:T(8,128)(2,1)} collective-permute-done((bf16[128,2048]{1,0:T(8,128)(2,1)}, bf16[128,2048]{1,0:T(8,128)(2,1)}, u32[]{:S(2)}, u32[]{:S(2)}) %collective-permute-start.2) | collective-permute-done | bytes 524320 | tf_op jit(solution)/shard_map/ppermute | solution.py:791
  78.5 2.0 constant_dynamic-update-slice_fusion.1
  81.3 2.6 slice.146.weight_ref
  85.0 3.4 fusion.22.pre_ref
  88.4 1.8 collective-permute-start.4
  90.2 1.5 collective-permute-start.5
  91.7 24.0 %attn_fwd.1 = (bf16[1024,512]{1,0:T(8,128)(2,1)S(1)}, bf16[2,16,256,64]{3,2,1,0:T(8,128)(2,1)S(1)}, bf16[2,1024,64]{2,1,0:T(8,128)(2,1)S(1)}, bf16[2,1024,64]{2,1,0:T(8,128)(2,1)S(1)}) custom-call(s32[169]{0:T(256)S(1)} %reshape.87.mask_ref, s32[16]{0:T(128)S(1)} %slice.108.seg_ref, s32[1]{0:T(128)} %bitcast.base_ref, f32[1024,768]{1,0:T(8,128)S(1)} %fusion.22.pre_ref, ...), custom_call_target="tpu_custom_call" | custom-call | flops 1000 | bytes 1000 | tf_op jit(solution)/shard_map/attn_fwd/pallas_call | solution.py:308
  115.7 4.6 slice.147.weight_ref
  120.3 74.8 %mid_forward.1 = (f32[256,2048]{1,0:T(8,128)}, bf16[4,256,2048]{2,1,0:T(8,128)(2,1)}) custom-call(bf16[1024,512]{1,0:T(8,128)(2,1)} %copy-done.21, bf16[2048,512]{1,0:T(8,128)(2,1)} %slice.147.weight_ref, bf16[256,2048]{1,0:T(8,128)(2,1)} %input_ref.3, bf16[1,2048]{1,0:T(2,128)(2,1)} %get-tuple-element.145.gain_ref), custom_call_target="tpu_custom_call" | custom-call | flops 80000000000 | bytes 20000000 | tf_op jit(solution)/shard_map/mid_forward/pallas_call | solution.py:891
  195.2 1.6 collective-permute-start.6
  200.5 5.4 collective-permute-done.6
  206.8 1.7 collective-permute-done.7
  209.4 3.4 all-gather.8.cloned.1.call-done.refs_2_
  212.8 34.3 %chunk_pass.3 = (bf16[4,256,1536]{2,1,0:T(8,128)(2,1)}, f32[1024,2048]{1,0:T(8,128)}, f32[1024,2048]{1,0:T(8,128)}) custom-call(bf16[1024,2048]{1,0:T(8,128)(2,1)} %bitcast.40, bf16[1024,2048]{1,0:T(8,128)(2,1)} %constant_dynamic-update-slice_fusion.5.refs_1_, bf16[2048,3840]{1,0:T(8,128)(2,1)} %all-gather.8.cloned.1.call-done.refs_2_), custom_call_target="tpu_custom_call" | custom-call | flops 19327352832 | bytes 62914560 | tf_op jit(solution)/shard_map/chunk_pass/pallas_call | solution.py:660
  247.1 46.5 %chunk_pass.4 = (bf16[4,256,2304]{2,1,0:T(8,128)(2,1)}, f32[1024,2048]{1,0:T(8,128)}, f32[1024,2048]{1,0:T(8,128)}) custom-call(bf16[1024,2048]{1,0:T(8,128)(2,1)} %bitcast.41, bf16[1024,2048]{1,0:T(8,128)(2,1)} %constant_dynamic-update-slice_fusion.5.refs_1_, ...), custom_call_target="tpu_custom_call", output_to_operand_aliasing={{1}: (3, {}), {2}: (4, {})} | custom-call | flops 28991029248 | bytes 69206016 | tf_op jit(solution)/shard_map/chunk_pass/pallas_call | solution.py:660
  293.6 9.8 %all-gather.6.cloned.1.call-done.refs_2_ = bf16[2048,2304]{1,0:T(8,128)(2,1)} async-done(((bf16[256,2304]{1,0:T(8,128)(2,1)}), bf16[2048,2304]{1,0:T(8,128)(2,1)}) %all-gather.6.cloned.1.call-update) | async-done | bytes 9437200 | tf_op jit(solution)/shard_map/all_gather | solution.py:1200
  303.4 61.9 %chunk_pass.5 = (bf16[2048,2304]{1,0:T(8,128)(2,1)}, bf16[1024,2048]{1,0:T(8,128)(2,1)}, bf16[1024,2048]{1,0:T(8,128)(2,1)}, f32[256,1536]{1,0:T(8,128)}) custom-call(bf16[1024,2048]{1,0:T(8,128)(2,1)} %bitcast.42, bf16[1024,2048]{1,0:T(8,128)(2,1)} %constant_dynamic-update-slice_fusion.5.refs_1_, bf16[2048,2304]{1,0:T(8,128)(2,1)} %all-gather.6.cloned.1.call-done.refs_2_, ...), custom_call_target="tpu_custom_call" | custom-call | flops 28991029248 | bytes 69206016 | tf_op jit(solution)/shard_map/chunk_pass/pallas_call | solution.py:660
  365.3 1.6 copy-done.8
  366.9 1.6 copy-done.25
  368.5 80.5 %mid_backward.1 = (f32[256,2048]{1,0:T(8,128)S(1)}, bf16[4,256,2048]{2,1,0:T(8,128)(2,1)S(1)}, bf16[1024,512]{1,0:T(8,128)(2,1)S(1)}, f32[256,2304]{1,0:T(8,128)S(1)}) custom-call(bf16[4,256,2048]{2,1,0:T(8,128)(2,1)} %bitcast.43, f32[256,2048]{1,0:T(8,128)S(1)} %copy-done.25, bf16[256,2048]{1,0:T(8,128)(2,1)S(1)} %copy-done.11, ...), custom_call_target="tpu_custom_call" | custom-call | flops 80000000000 | bytes 20000000 | tf_op jit(solution)/shard_map/mid_backward/pallas_call | solution.py:973
  450.0 2.0 copy-done.23
  452.0 1.3 copy-done.26
  454.5 1.6 copy-done.7
  456.1 1.2 copy-done.10
  459.5 29.3 %attn_bwd.1.first_ref.grads_ref = bf16[1024,768]{1,0:T(8,128)(2,1)S(1)} custom-call(s32[169]{0:T(256)S(1)} %copy-done.17, s32[16]{0:T(128)S(1)} %copy-done.20, s32[1]{0:T(128)} %bitcast.base_ref, bf16[2,16,256,64]{3,2,1,0:T(8,128)(2,1)S(1)} %copy-done.7, bf16[2,1024,64]{2,1,0:T(8,128)(2,1)S(1)} %copy-done.13, bf16[2,1024,64]{2,1,0:T(8,128)(2,1)S(1)} %copy-done.15, ...), custom_call_target="tpu_custom_call" | custom-call | flops 1000 | bytes 1000 | tf_op jit(solution)/shard_map/attn_bwd/pallas_call | solution.py:328
  490.7 3.1 maximum_bitcast_fusion
  493.8 11.9 %pair_hops.1.slabs_ref = bf16[4,256,1280]{2,1,0:T(8,128)(2,1)S(1)} custom-call(bf16[1024,2048]{1,0:T(8,128)(2,1)} %constant_dynamic-update-slice_fusion.left_ref, bf16[1024,768]{1,0:T(8,128)(2,1)S(1)} %attn_bwd.1.first_ref.grads_ref, bf16[1024,2048]{1,0:T(8,128)(2,1)} %bitcast.26, bf16[1024,512]{1,0:T(8,128)(2,1)S(1)} %copy-done.22), custom_call_target="tpu_custom_call" | custom-call | flops 5368709120 | bytes 13631488 | tf_op jit(solution)/shard_map/pair_hops/pallas_call | solution.py:762
  505.7 1.5 copy-done.24
  507.2 86.6 %end_backward.1 = (f32[256,2048]{1,0:T(8,128)}, bf16[256,2048]{1,0:T(8,128)(2,1)S(1)}, f32[256,1280]{1,0:T(8,128)S(1)}) custom-call(bf16[1024,768]{1,0:T(8,128)(2,1)S(1)} %attn_bwd.1.first_ref.grads_ref, bf16[2048,768]{1,0:T(8,128)(2,1)} %copy-done.29, bf16[256,2048]{1,0:T(8,128)(2,1)S(1)} %copy-done.5, bf16[1,2048]{1,0:T(2,128)(2,1)S(1)} %get-tuple-element.144.gain_ref, ...), custom_call_target="tpu_custom_call" | custom-call | flops 40000000000 | bytes 20000000 | tf_op jit(solution)/shard_map/end_backward/pallas_call | solution.py:1057
  596.7 1.4 convert_element_type.54
  598.5 1.5 collective-permute-start.8
  600.0 1.2 slice_dynamic-update-slice_fusion
  602.1 1.5 collective-permute-start.9
  604.6 2.9 copy.40
  609.7 1.3 copy.62
  (170 shorter events, 32.1 us)
Async XLA Ops:
  7.2 3.2 copy-start.40
  7.2 74.1 %all-gather.4.cloned.1.call-start = ((), (), s32[]{:S(2)}) async-start(), calls=%async_computation.1 | async-start | bytes 5898240 | tf_op jit(solution)/shard_map/all_gather | solution.py:1200
  10.3 202.4 %all-gather.8.cloned.1.call-start = ((), (), s32[]{:S(2)}) async-start(), calls=%async_computation.3 | async-start | bytes 17694720 | tf_op jit(solution)/shard_map/all_gather | solution.py:1200
  11.1 6.1 copy-start.41
  19.1 1.7 copy-start.36
  20.4 15.9 %copy-start.4 = (bf16[256,2048]{1,0:T(8,128)(2,1)S(1)}, bf16[256,2048]{1,0:T(8,128)(2,1)}, u32[]{:S(2)}) copy-start(bf16[256,2048]{1,0:T(8,128)(2,1)} %input_ref.3) | copy-start | bytes 3145732
  20.5 283.0 %all-gather.6.cloned.1.call-start = ((), (), s32[]{:S(2)}) async-start(), calls=%async_computation.2 | async-start | bytes 10616832 | tf_op jit(solution)/shard_map/all_gather | solution.py:1200
  22.0 574.7 %reduce-scatter.2.cloned.1.call-start = ((), (), s32[]{:S(2)}) async-start(), calls=%async_computation.4 | async-start | bytes 10616832 | tf_op jit(solution)/shard_map/reduce_scatter | solution.py:1204
  36.3 4.9 copy-start.47
  36.3 4.9 copy-start.48
  36.3 5.0 copy-start.49
  38.3 25.6 %collective-permute-start = (bf16[256,2048]{1,0:T(8,128)(2,1)}, bf16[256,2048]{1,0:T(8,128)(2,1)S(1)}, u32[]{:S(2)}, u32[]{:S(2)}) collective-permute-start(bf16[256,2048]{1,0:T(8,128)(2,1)} %get-tuple-element.113), channel_id=1, source_target_pairs={{0,1},{1,0},{2,3},{3,2},{4,5},{5,4},{6,7},{7,6},{8,9},{9,8},{10,11... | collective-permute-start | bytes 3145736 | tf_op jit(solution)/shard_map/ppermute | solution.py:791
  39.8 26.7 %collective-permute-start.1 = (bf16[256,2048]{1,0:T(8,128)(2,1)}, bf16[256,2048]{1,0:T(8,128)(2,1)S(1)}, u32[]{:S(2)}, u32[]{:S(2)}) collective-permute-start(bf16[256,2048]{1,0:T(8,128)(2,1)} %get-tuple-element.113), channel_id=1, source_target_pairs={{0,2},{1,3},{2,0},{3,1},{4,6},{5,7},{6,4},{7,5},{8,10},{9,11},{10,... | collective-permute-start | bytes 3145736 | tf_op jit(solution)/shard_map/ppermute | solution.py:791
  43.2 23.1 %copy-start.46 = (s32[1,13,13]{2,0,1:T(1,128)S(1)}, s32[1,13,13]{2,0,1:T(1,128)}, u32[]{:S(2)}) copy-start(s32[1,13,13]{2,0,1:T(1,128)} %param.19) | copy-start | bytes 2032
  43.7 48.0 %copy-start.2 = (f32[1024,128]{1,0:T(8,128)}, f32[1024,128]{1,0:T(8,128)S(1)}, u32[]{:S(2)}) copy-start(f32[1024,128]{1,0:T(8,128)S(1)} %pad_maximum_fusion.6.cos_ref) | copy-start | bytes 1572868
  44.2 47.5 %copy-start = (f32[1024,128]{1,0:T(8,128)}, f32[1024,128]{1,0:T(8,128)S(1)}, u32[]{:S(2)}) copy-start(f32[1024,128]{1,0:T(8,128)S(1)} %pad_maximum_fusion.7.sin_ref) | copy-start | bytes 1572868
  64.7 13.8 %collective-permute-start.2 = (bf16[128,2048]{1,0:T(8,128)(2,1)}, bf16[128,2048]{1,0:T(8,128)(2,1)}, u32[]{:S(2)}, u32[]{:S(2)}) collective-permute-start(bf16[128,2048]{1,0:T(8,128)(2,1)} %slice.144), channel_id=1, source_target_pairs={{0,2},{1,3},{2,0},{3,1},{4,6},{5,7},{6,4},{7,5},{8,10},{9,11},{10,... | collective-permute-start | bytes 1572872 | tf_op jit(solution)/shard_map/ppermute | solution.py:791
  66.4 25.4 %copy-start.19 = (s32[16]{0:T(128)}, s32[16]{0:T(128)S(1)}, u32[]{:S(2)}) copy-start(s32[16]{0:T(128)S(1)} %slice.108.seg_ref) | copy-start | bytes 196
  66.5 25.2 %copy-start.16 = (s32[169]{0:T(256)}, s32[169]{0:T(256)S(1)}, u32[]{:S(2)}) copy-start(s32[169]{0:T(256)S(1)} %reshape.87.mask_ref) | copy-start | bytes 2032
  66.6 13.9 %collective-permute-start.3 = (bf16[128,2048]{1,0:T(8,128)(2,1)S(1)}, bf16[128,2048]{1,0:T(8,128)(2,1)S(1)}, u32[]{:S(2)}, u32[]{:S(2)}) collective-permute-start(bf16[128,2048]{1,0:T(8,128)(2,1)S(1)} %slice.145), channel_id=1, source_target_pairs={{0,1},{1,0},{2,3},{3,2},{4,5},{5,4},{6,7},{7,6},{8,9},{9,8},{10,11... | collective-permute-start | bytes 1572872 | tf_op jit(solution)/shard_map/ppermute | solution.py:791
  81.3 3.7 copy-start.43
  85.0 3.4 copy-start.29
  85.0 3.4 copy-start.11
  88.4 106.7 %collective-permute-start.4 = (bf16[256,2048]{1,0:T(8,128)(2,1)S(1)}, bf16[256,2048]{1,0:T(8,128)(2,1)S(1)}, u32[]{:S(2)}, u32[]{:S(2)}) collective-permute-start(bf16[256,2048]{1,0:T(8,128)(2,1)S(1)} %copy-done.11), channel_id=1, source_target_pairs={{0,1},{1,0},{2,3},{3,2},{4,5},{5,4},{6,7},{7,6},{8,9},{9,8},{10,11... | collective-permute-start | bytes 3145736 | tf_op jit(solution)/shard_map/ppermute | solution.py:791
  90.2 104.9 %collective-permute-start.5 = (bf16[256,2048]{1,0:T(8,128)(2,1)S(1)}, bf16[256,2048]{1,0:T(8,128)(2,1)S(1)}, u32[]{:S(2)}, u32[]{:S(2)}) collective-permute-start(bf16[256,2048]{1,0:T(8,128)(2,1)S(1)} %copy-done.11), channel_id=1, source_target_pairs={{0,2},{1,3},{2,0},{3,1},{4,6},{5,7},{6,4},{7,5},{8,10},{9,11},{10,... | collective-permute-start | bytes 3145736 | tf_op jit(solution)/shard_map/ppermute | solution.py:791
  115.7 4.6 copy-start.6
  115.7 4.6 copy-start.12
  115.7 4.6 copy-start.14
  115.7 4.6 copy-start.21
  195.2 10.8 %collective-permute-start.6 = (bf16[128,2048]{1,0:T(8,128)(2,1)S(1)}, bf16[128,2048]{1,0:T(8,128)(2,1)S(1)}, u32[]{:S(2)}, u32[]{:S(2)}) collective-permute-start(bf16[128,2048]{1,0:T(8,128)(2,1)S(1)} %slice.115), channel_id=1, source_target_pairs={{0,2},{1,3},{2,0},{3,1},{4,6},{5,7},{6,4},{7,5},{8,10},{9,11},{10,... | collective-permute-start | bytes 1572872 | tf_op jit(solution)/shard_map/ppermute | solution.py:791
  197.9 10.7 %collective-permute-start.7 = (bf16[128,2048]{1,0:T(8,128)(2,1)S(1)}, bf16[128,2048]{1,0:T(8,128)(2,1)S(1)}, u32[]{:S(2)}, u32[]{:S(2)}) collective-permute-start(bf16[128,2048]{1,0:T(8,128)(2,1)S(1)} %slice.116), channel_id=1, source_target_pairs={{0,1},{1,0},{2,3},{3,2},{4,5},{5,4},{6,7},{7,6},{8,9},{9,8},{10,11... | collective-permute-start | bytes 1572872 | tf_op jit(solution)/shard_map/ppermute | solution.py:791
  303.4 61.9 %copy-start.18 = (bf16[1,2048]{1,0:T(2,128)(2,1)S(1)}, bf16[1,2048]{1,0:T(2,128)(2,1)}, u32[]{:S(2)}) copy-start(bf16[1,2048]{1,0:T(2,128)(2,1)} %get-tuple-element.145.gain_ref) | copy-start | bytes 12292
  449.9 2.0 copy-start.23
  459.5 29.3 %copy-start.28 = (f32[256,1536]{1,0:T(8,128)S(1)}, f32[256,1536]{1,0:T(8,128)}, u32[]{:S(2)}) copy-start(f32[256,1536]{1,0:T(8,128)} %get-tuple-element.65) | copy-start | bytes 4718596
  459.5 29.3 %copy-start.37 = (bf16[256,512]{1,0:T(8,128)(2,1)S(1)}, bf16[256,512]{1,0:T(8,128)(2,1)}, u32[]{:S(2)}) copy-start(bf16[256,512]{1,0:T(8,128)(2,1)} %get-tuple-element.135) | copy-start | bytes 786436
  459.5 29.3 %copy-start.38 = (bf16[256,512]{1,0:T(8,128)(2,1)S(1)}, bf16[256,512]{1,0:T(8,128)(2,1)}, u32[]{:S(2)}) copy-start(bf16[256,512]{1,0:T(8,128)(2,1)} %get-tuple-element.137) | copy-start | bytes 786436
  459.5 29.4 %copy-start.39 = (bf16[256,512]{1,0:T(8,128)(2,1)S(1)}, bf16[256,512]{1,0:T(8,128)(2,1)}, u32[]{:S(2)}) copy-start(bf16[256,512]{1,0:T(8,128)(2,1)} %get-tuple-element.139) | copy-start | bytes 786436
  490.7 3.1 copy-start.22
  493.8 13.4 %copy-start.5 = (bf16[256,2048]{1,0:T(8,128)(2,1)S(1)}, bf16[256,2048]{1,0:T(8,128)(2,1)}, u32[]{:S(2)}) copy-start(bf16[256,2048]{1,0:T(8,128)(2,1)} %input_ref.3) | copy-start | bytes 3145732
  593.9 2.0 copy-start.42
  593.9 2.0 copy-start.44
  593.9 2.0 copy-start.45
  596.0 2.2 copy-start.27
  598.5 3.7 collective-permute-start.8
  602.1 5.4 collective-permute-start.9
  604.6 2.9 copy-start.51
  604.6 3.5 copy-start.53
  607.5 2.2 copy-start.31
  (20 other events, 25.9 us)
Sparse Core Ops, SparseCore 0:
  10.5 58.7 all-gather.3
  71.5 141.1 all-gather.7
  214.4 88.9 all-gather.5
  453.4 131.0 reduce-scatter.1

commit v5 on v4

--- a/solution.py
+++ b/solution.py
@@ -997,7 +997,7 @@
             *hop_scratch(height, job_width),
         ],
         compiler_params=pltpu.CompilerParams(
-            collective_id=2, has_side_effects=True, vmem_limit_bytes=36 << 20
+            collective_id=2, has_side_effects=True, vmem_limit_bytes=48 << 20
         ),
         cost_estimate=pl.CostEstimate(
             flops=80_000_000_000, bytes_accessed=20_000_000, transcendentals=0

time: 626 us -> 627 us (level)
  Pallas kernels: 450 us -> 457 us
    unnamed x121 -> x99, local copies, waits for them, and re-layouts: 35.1 us -> 30.7 us
  transfers between devices with their start and end apart: 14 -> 14, of which waited for: 7 -> 7; matrix products, arithmetic and copies ran while one was open for 8% -> 9% of each run, Pallas kernels for 50% -> 50%
where the time goes in v5:
time: 627 us; the launch traced here: 618 us
  Pallas kernels  457 us (73%)
  local copies, waits for them, and re-layouts  54.4 us (9%)
  waiting for transfers between devices  45.5 us (7%)
  other arithmetic  15 us (2%)
  starting transfers between devices  14.6 us (2%)
  between operations  14.6 us (2%)
  blocking collectives  13.6 us (2%)
    pallas_call x3, Pallas kernels, chunk_pass(): pl.pallas_call(functools.partial(chunk_kernel, (steps, slabs, first, last...  143 us
    pallas_call x1, Pallas kernels, end_backward(): pl.pallas_call(end_backward_kernel, name='end_backward', out_shape=(jax.S...  89.8 us
    pallas_call x1, Pallas kernels, mid_backward(): pl.pallas_call(mid_backward_kernel, name='mid_backward', out_shape=(jax.S...  85 us
    pallas_call x1, Pallas kernels, mid_forward(): pl.pallas_call(mid_forward_kernel, name='mid_forward', out_shape=(jax.Sha...  74.5 us
    ppermute x10, waiting for transfers between devices, by_tp(): return lax.ppermute(value, 'tp', pairs)  33.7 us
    unnamed x99, local copies, waits for them, and re-layouts  30.7 us
    pallas_call x1, Pallas kernels, attention_backward(): pl.pallas_call(functools.partial(attn_bwd_kernel, heads, groups), name='a...  29.2 us
    pallas_call x1, Pallas kernels, attention_forward(): pl.pallas_call(functools.partial(attn_fwd_kernel, heads, groups), name='a...  24 us
  transfers between devices with their start and end apart: 14, of which 7 were waited for; matrix products, arithmetic and copies ran while one was open for 9% of the time, Pallas kernels for 50%

profile of v5, /device:TPU:0, one launch (start us, length us, event | category | flops | bytes accessed | tf_op | source)
XLA Modules:
  0.0 618.4 jit_solution(6808507662111978536)
XLA Ops:
  7.2 1.2 copy.36
  8.4 1.9 pad_maximum_fusion.3
  11.1 1.8 fusion.16
  12.8 1.7 fusion.17
  15.3 1.9 fusion.13
  19.1 1.3 copy-done.19
  22.1 13.6 %all_gather.12 = bf16[2048,2]{0,1:T(2,128)(2,1)S(1)} all-gather(bf16[256,2]{0,1:T(2,128)(2,1)S(1)} %pad_maximum_fusion.9), channel_id=1, replica_groups=mesh['fsdp'=8,'tp'=4] {'fsdp'}, dimensions={0}, use_global_device_ids=true | all-gather | bytes 9216 | tf_op jit(solution)/shard_map/all_gather | solution.py:1200
  36.6 1.7 constant_dynamic-update-slice_fusion.4
  38.3 1.4 collective-permute-start
  39.7 1.5 collective-permute-start.1
  41.3 1.9 fusion.7
  44.2 19.7 %collective-permute-done = bf16[256,2048]{1,0:T(8,128)(2,1)S(1)} collective-permute-done((bf16[256,2048]{1,0:T(8,128)(2,1)}, bf16[256,2048]{1,0:T(8,128)(2,1)S(1)}, u32[]{:S(2)}, u32[]{:S(2)}) %collective-permute-start) | collective-permute-done | bytes 1048608 | tf_op jit(solution)/shard_map/ppermute | solution.py:791
  64.7 1.4 collective-permute-start.2
  66.5 1.6 collective-permute-start.3
  70.1 8.3 %collective-permute-done.2 = bf16[128,2048]{1,0:T(8,128)(2,1)} collective-permute-done((bf16[128,2048]{1,0:T(8,128)(2,1)}, bf16[128,2048]{1,0:T(8,128)(2,1)}, u32[]{:S(2)}, u32[]{:S(2)}) %collective-permute-start.2) | collective-permute-done | bytes 524320 | tf_op jit(solution)/shard_map/ppermute | solution.py:791
  78.5 2.0 constant_dynamic-update-slice_fusion.1
  81.3 2.6 slice.146.weight_ref
  85.0 3.4 fusion.22.pre_ref
  88.5 1.8 collective-permute-start.4
  90.2 1.5 collective-permute-start.5
  91.7 24.0 %attn_fwd.1 = (bf16[1024,512]{1,0:T(8,128)(2,1)S(1)}, bf16[2,16,256,64]{3,2,1,0:T(8,128)(2,1)S(1)}, bf16[2,1024,64]{2,1,0:T(8,128)(2,1)S(1)}, bf16[2,1024,64]{2,1,0:T(8,128)(2,1)S(1)}) custom-call(s32[169]{0:T(256)S(1)} %reshape.87.mask_ref, s32[16]{0:T(128)S(1)} %slice.108.seg_ref, s32[1]{0:T(128)} %bitcast.base_ref, f32[1024,768]{1,0:T(8,128)S(1)} %fusion.22.pre_ref, ...), custom_call_target="tpu_custom_call" | custom-call | flops 1000 | bytes 1000 | tf_op jit(solution)/shard_map/attn_fwd/pallas_call | solution.py:308
  115.7 3.8 slice.147.weight_ref
  119.6 74.5 %mid_forward.1 = (f32[256,2048]{1,0:T(8,128)}, bf16[4,256,2048]{2,1,0:T(8,128)(2,1)}) custom-call(bf16[1024,512]{1,0:T(8,128)(2,1)} %copy-done.11, bf16[2048,512]{1,0:T(8,128)(2,1)} %slice.147.weight_ref, bf16[256,2048]{1,0:T(8,128)(2,1)} %input_ref.3, bf16[1,2048]{1,0:T(2,128)(2,1)} %get-tuple-element.145.gain_ref), custom_call_target="tpu_custom_call" | custom-call | flops 80000000000 | bytes 20000000 | tf_op jit(solution)/shard_map/mid_forward/pallas_call | solution.py:891
  195.2 1.8 collective-permute-start.6
  199.5 2.3 constant_dynamic-update-slice_fusion.8
  201.8 2.3 constant_dynamic-update-slice_fusion.7
  204.1 1.9 collective-permute-done.6
  206.9 2.8 collective-permute-done.7
  210.6 2.2 all-gather.8.cloned.1.call-done.refs_2_
  212.8 34.5 %chunk_pass.3 = (bf16[4,256,1536]{2,1,0:T(8,128)(2,1)}, f32[1024,2048]{1,0:T(8,128)}, f32[1024,2048]{1,0:T(8,128)}) custom-call(bf16[1024,2048]{1,0:T(8,128)(2,1)} %bitcast.40, bf16[1024,2048]{1,0:T(8,128)(2,1)} %constant_dynamic-update-slice_fusion.5.refs_1_, bf16[2048,3840]{1,0:T(8,128)(2,1)} %all-gather.8.cloned.1.call-done.refs_2_), custom_call_target="tpu_custom_call" | custom-call | flops 19327352832 | bytes 62914560 | tf_op jit(solution)/shard_map/chunk_pass/pallas_call | solution.py:660
  247.3 46.5 %chunk_pass.4 = (bf16[4,256,2304]{2,1,0:T(8,128)(2,1)}, f32[1024,2048]{1,0:T(8,128)}, f32[1024,2048]{1,0:T(8,128)}) custom-call(bf16[1024,2048]{1,0:T(8,128)(2,1)} %bitcast.41, bf16[1024,2048]{1,0:T(8,128)(2,1)} %constant_dynamic-update-slice_fusion.5.refs_1_, ...), custom_call_target="tpu_custom_call", output_to_operand_aliasing={{1}: (3, {}), {2}: (4, {})} | custom-call | flops 28991029248 | bytes 69206016 | tf_op jit(solution)/shard_map/chunk_pass/pallas_call | solution.py:660
  293.8 9.6 %all-gather.6.cloned.1.call-done.refs_2_ = bf16[2048,2304]{1,0:T(8,128)(2,1)} async-done(((bf16[256,2304]{1,0:T(8,128)(2,1)}), bf16[2048,2304]{1,0:T(8,128)(2,1)}) %all-gather.6.cloned.1.call-update) | async-done | bytes 9437200 | tf_op jit(solution)/shard_map/all_gather | solution.py:1200
  303.4 61.9 %chunk_pass.5 = (bf16[2048,2304]{1,0:T(8,128)(2,1)}, bf16[1024,2048]{1,0:T(8,128)(2,1)}, bf16[1024,2048]{1,0:T(8,128)(2,1)}, f32[256,1536]{1,0:T(8,128)}) custom-call(bf16[1024,2048]{1,0:T(8,128)(2,1)} %bitcast.42, bf16[1024,2048]{1,0:T(8,128)(2,1)} %constant_dynamic-update-slice_fusion.5.refs_1_, bf16[2048,2304]{1,0:T(8,128)(2,1)} %all-gather.6.cloned.1.call-done.refs_2_, ...), custom_call_target="tpu_custom_call" | custom-call | flops 28991029248 | bytes 69206016 | tf_op jit(solution)/shard_map/chunk_pass/pallas_call | solution.py:660
  365.4 1.2 copy-done.5
  366.6 85.0 %mid_backward.1 = (f32[256,2048]{1,0:T(8,128)S(1)}, bf16[4,256,2048]{2,1,0:T(8,128)(2,1)}, bf16[1024,512]{1,0:T(8,128)(2,1)S(1)}, f32[256,2304]{1,0:T(8,128)}) custom-call(bf16[4,256,2048]{2,1,0:T(8,128)(2,1)} %bitcast.43, f32[256,2048]{1,0:T(8,128)} %get-tuple-element.61.residual_ref, bf16[256,2048]{1,0:T(8,128)(2,1)S(1)} %copy-done.5, ...), custom_call_target="tpu_custom_call" | custom-call | flops 80000000000 | bytes 20000000 | tf_op jit(solution)/shard_map/mid_backward/pallas_call | solution.py:973
  452.5 1.3 copy-done.14
  453.9 1.2 copy-done.3
  457.2 29.2 %attn_bwd.1.first_ref.grads_ref = bf16[1024,768]{1,0:T(8,128)(2,1)S(1)} custom-call(s32[169]{0:T(256)S(1)} %reshape.87.mask_ref, s32[16]{0:T(128)S(1)} %slice.108.seg_ref, s32[1]{0:T(128)} %bitcast.base_ref, bf16[2,16,256,64]{3,2,1,0:T(8,128)(2,1)S(1)} %get-tuple-element.45.q_ref, bf16[2,1024,64]{2,1,0:T(8,128)(2,1)S(1)} %copy-done.7, ...), custom_call_target="tpu_custom_call" | custom-call | flops 1000 | bytes 1000 | tf_op jit(solution)/shard_map/attn_bwd/pallas_call | solution.py:328
  488.3 3.1 maximum_bitcast_fusion
  491.4 11.9 %pair_hops.1.slabs_ref = bf16[4,256,1280]{2,1,0:T(8,128)(2,1)S(1)} custom-call(bf16[1024,2048]{1,0:T(8,128)(2,1)} %constant_dynamic-update-slice_fusion.left_ref, bf16[1024,768]{1,0:T(8,128)(2,1)S(1)} %attn_bwd.1.first_ref.grads_ref, bf16[1024,2048]{1,0:T(8,128)(2,1)} %bitcast.39, bf16[1024,512]{1,0:T(8,128)(2,1)S(1)} %copy-done.12), custom_call_target="tpu_custom_call" | custom-call | flops 5368709120 | bytes 13631488 | tf_op jit(solution)/shard_map/pair_hops/pallas_call | solution.py:762
  503.3 1.5 copy-done.13
  504.7 89.8 %end_backward.1 = (f32[256,2048]{1,0:T(8,128)}, bf16[256,2048]{1,0:T(8,128)(2,1)S(1)}, f32[256,1280]{1,0:T(8,128)S(1)}) custom-call(bf16[1024,768]{1,0:T(8,128)(2,1)S(1)} %attn_bwd.1.first_ref.grads_ref, bf16[2048,768]{1,0:T(8,128)(2,1)} %copy-done.18, bf16[256,2048]{1,0:T(8,128)(2,1)S(1)} %copy-done.1, bf16[1,2048]{1,0:T(2,128)(2,1)S(1)} %get-tuple-element.144.gain_ref, ...), custom_call_target="tpu_custom_call" | custom-call | flops 40000000000 | bytes 20000000 | tf_op jit(solution)/shard_map/end_backward/pallas_call | solution.py:1057
  597.4 1.4 convert_element_type.54
  599.1 1.5 collective-permute-start.8
  600.7 1.2 slice_dynamic-update-slice_fusion
  602.8 1.5 collective-permute-start.9
  605.3 2.9 copy.40
  610.3 1.3 copy.62
  (148 shorter events, 29.4 us)
Async XLA Ops:
  7.2 3.2 copy-start.29
  7.2 74.1 %all-gather.4.cloned.1.call-start = ((), (), s32[]{:S(2)}) async-start(), calls=%async_computation.1 | async-start | bytes 5898240 | tf_op jit(solution)/shard_map/all_gather | solution.py:1200
  10.3 202.4 %all-gather.8.cloned.1.call-start = ((), (), s32[]{:S(2)}) async-start(), calls=%async_computation.3 | async-start | bytes 17694720 | tf_op jit(solution)/shard_map/all_gather | solution.py:1200
  11.1 6.1 copy-start.30
  19.1 1.4 copy-start.24
  19.1 1.7 copy-start.25
  20.4 1.6 copy-start.41
  20.4 1.6 copy-start.39
  20.4 15.9 %copy-start = (bf16[256,2048]{1,0:T(8,128)(2,1)S(1)}, bf16[256,2048]{1,0:T(8,128)(2,1)}, u32[]{:S(2)}) copy-start(bf16[256,2048]{1,0:T(8,128)(2,1)} %input_ref.3) | copy-start | bytes 3145732
  20.5 283.0 %all-gather.6.cloned.1.call-start = ((), (), s32[]{:S(2)}) async-start(), calls=%async_computation.2 | async-start | bytes 10616832 | tf_op jit(solution)/shard_map/all_gather | solution.py:1200
  22.0 575.4 %reduce-scatter.2.cloned.1.call-start = ((), (), s32[]{:S(2)}) async-start(), calls=%async_computation.4 | async-start | bytes 10616832 | tf_op jit(solution)/shard_map/reduce_scatter | solution.py:1204
  36.3 4.9 copy-start.36
  36.3 4.9 copy-start.37
  36.3 5.0 copy-start.38
  38.3 25.6 %collective-permute-start = (bf16[256,2048]{1,0:T(8,128)(2,1)}, bf16[256,2048]{1,0:T(8,128)(2,1)S(1)}, u32[]{:S(2)}, u32[]{:S(2)}) collective-permute-start(bf16[256,2048]{1,0:T(8,128)(2,1)} %get-tuple-element.113), channel_id=1, source_target_pairs={{0,1},{1,0},{2,3},{3,2},{4,5},{5,4},{6,7},{7,6},{8,9},{9,8},{10,11... | collective-permute-start | bytes 3145736 | tf_op jit(solution)/shard_map/ppermute | solution.py:791
  39.7 26.7 %collective-permute-start.1 = (bf16[256,2048]{1,0:T(8,128)(2,1)}, bf16[256,2048]{1,0:T(8,128)(2,1)S(1)}, u32[]{:S(2)}, u32[]{:S(2)}) collective-permute-start(bf16[256,2048]{1,0:T(8,128)(2,1)} %get-tuple-element.113), channel_id=1, source_target_pairs={{0,2},{1,3},{2,0},{3,1},{4,6},{5,7},{6,4},{7,5},{8,10},{9,11},{10,... | collective-permute-start | bytes 3145736 | tf_op jit(solution)/shard_map/ppermute | solution.py:791
  43.2 23.0 %copy-start.35 = (s32[1,13,13]{2,0,1:T(1,128)S(1)}, s32[1,13,13]{2,0,1:T(1,128)}, u32[]{:S(2)}) copy-start(s32[1,13,13]{2,0,1:T(1,128)} %param.19) | copy-start | bytes 2032
  64.7 13.8 %collective-permute-start.2 = (bf16[128,2048]{1,0:T(8,128)(2,1)}, bf16[128,2048]{1,0:T(8,128)(2,1)}, u32[]{:S(2)}, u32[]{:S(2)}) collective-permute-start(bf16[128,2048]{1,0:T(8,128)(2,1)} %slice.144), channel_id=1, source_target_pairs={{0,2},{1,3},{2,0},{3,1},{4,6},{5,7},{6,4},{7,5},{8,10},{9,11},{10,... | collective-permute-start | bytes 1572872 | tf_op jit(solution)/shard_map/ppermute | solution.py:791
  66.5 14.0 %collective-permute-start.3 = (bf16[128,2048]{1,0:T(8,128)(2,1)S(1)}, bf16[128,2048]{1,0:T(8,128)(2,1)S(1)}, u32[]{:S(2)}, u32[]{:S(2)}) collective-permute-start(bf16[128,2048]{1,0:T(8,128)(2,1)S(1)} %slice.145), channel_id=1, source_target_pairs={{0,1},{1,0},{2,3},{3,2},{4,5},{5,4},{6,7},{7,6},{8,9},{9,8},{10,11... | collective-permute-start | bytes 1572872 | tf_op jit(solution)/shard_map/ppermute | solution.py:791
  81.3 3.7 copy-start.32
  85.0 3.4 copy-start.18
  85.0 3.4 copy-start.4
  88.5 105.6 %collective-permute-start.4 = (bf16[256,2048]{1,0:T(8,128)(2,1)S(1)}, bf16[256,2048]{1,0:T(8,128)(2,1)}, u32[]{:S(2)}, u32[]{:S(2)}) collective-permute-start(bf16[256,2048]{1,0:T(8,128)(2,1)S(1)} %copy-done.4), channel_id=1, source_target_pairs={{0,1},{1,0},{2,3},{3,2},{4,5},{5,4},{6,7},{7,6},{8,9},{9,8},{10,11... | collective-permute-start | bytes 3145736 | tf_op jit(solution)/shard_map/ppermute | solution.py:791
  90.2 103.8 %collective-permute-start.5 = (bf16[256,2048]{1,0:T(8,128)(2,1)S(1)}, bf16[256,2048]{1,0:T(8,128)(2,1)}, u32[]{:S(2)}, u32[]{:S(2)}) collective-permute-start(bf16[256,2048]{1,0:T(8,128)(2,1)S(1)} %copy-done.4), channel_id=1, source_target_pairs={{0,2},{1,3},{2,0},{3,1},{4,6},{5,7},{6,4},{7,5},{8,10},{9,11},{10,... | collective-permute-start | bytes 3145736 | tf_op jit(solution)/shard_map/ppermute | solution.py:791
  115.7 3.9 copy-start.6
  115.7 3.9 copy-start.8
  115.7 3.9 copy-start.11
  195.2 10.9 %collective-permute-start.6 = (bf16[128,2048]{1,0:T(8,128)(2,1)S(1)}, bf16[128,2048]{1,0:T(8,128)(2,1)S(1)}, u32[]{:S(2)}, u32[]{:S(2)}) collective-permute-start(bf16[128,2048]{1,0:T(8,128)(2,1)S(1)} %slice.115), channel_id=1, source_target_pairs={{0,2},{1,3},{2,0},{3,1},{4,6},{5,7},{6,4},{7,5},{8,10},{9,11},{10,... | collective-permute-start | bytes 1572872 | tf_op jit(solution)/shard_map/ppermute | solution.py:791
  199.1 10.6 %collective-permute-start.7 = (bf16[128,2048]{1,0:T(8,128)(2,1)S(1)}, bf16[128,2048]{1,0:T(8,128)(2,1)S(1)}, u32[]{:S(2)}, u32[]{:S(2)}) collective-permute-start(bf16[128,2048]{1,0:T(8,128)(2,1)S(1)} %slice.116), channel_id=1, source_target_pairs={{0,1},{1,0},{2,3},{3,2},{4,5},{5,4},{6,7},{7,6},{8,9},{9,8},{10,11... | collective-permute-start | bytes 1572872 | tf_op jit(solution)/shard_map/ppermute | solution.py:791
  303.4 61.9 %copy-start.10 = (bf16[1,2048]{1,0:T(2,128)(2,1)S(1)}, bf16[1,2048]{1,0:T(2,128)(2,1)}, u32[]{:S(2)}) copy-start(bf16[1,2048]{1,0:T(2,128)(2,1)} %get-tuple-element.145.gain_ref) | copy-start | bytes 12292
  452.5 1.3 copy-start.14
  457.2 29.3 %copy-start.17 = (f32[256,1536]{1,0:T(8,128)S(1)}, f32[256,1536]{1,0:T(8,128)}, u32[]{:S(2)}) copy-start(f32[256,1536]{1,0:T(8,128)} %get-tuple-element.65) | copy-start | bytes 4718596
  457.2 29.3 %copy-start.26 = (bf16[256,512]{1,0:T(8,128)(2,1)S(1)}, bf16[256,512]{1,0:T(8,128)(2,1)}, u32[]{:S(2)}) copy-start(bf16[256,512]{1,0:T(8,128)(2,1)} %get-tuple-element.135) | copy-start | bytes 786436
  457.2 29.3 %copy-start.27 = (bf16[256,512]{1,0:T(8,128)(2,1)S(1)}, bf16[256,512]{1,0:T(8,128)(2,1)}, u32[]{:S(2)}) copy-start(bf16[256,512]{1,0:T(8,128)(2,1)} %get-tuple-element.137) | copy-start | bytes 786436
  457.2 29.3 %copy-start.28 = (bf16[256,512]{1,0:T(8,128)(2,1)S(1)}, bf16[256,512]{1,0:T(8,128)(2,1)}, u32[]{:S(2)}) copy-start(bf16[256,512]{1,0:T(8,128)(2,1)} %get-tuple-element.139) | copy-start | bytes 786436
  457.2 29.5 %copy-start.16 = (f32[256,2304]{1,0:T(8,128)S(1)}, f32[256,2304]{1,0:T(8,128)}, u32[]{:S(2)}) copy-start(f32[256,2304]{1,0:T(8,128)} %get-tuple-element.66) | copy-start | bytes 7077892
  488.3 3.1 copy-start.12
  491.4 13.3 %copy-start.1 = (bf16[256,2048]{1,0:T(8,128)(2,1)S(1)}, bf16[256,2048]{1,0:T(8,128)(2,1)}, u32[]{:S(2)}) copy-start(bf16[256,2048]{1,0:T(8,128)(2,1)} %input_ref.3) | copy-start | bytes 3145732
  503.3 1.5 copy-start.13
  594.5 2.0 copy-start.31
  594.5 2.0 copy-start.33
  594.6 2.0 copy-start.34
  596.7 2.2 copy-start.15
  599.1 3.7 collective-permute-start.8
  602.8 5.4 collective-permute-start.9
  605.3 2.9 copy-start.40
  605.3 3.5 copy-start.42
  608.2 2.2 copy-start.20
  (9 other events, 10.1 us)
Sparse Core Ops, SparseCore 0:
  10.5 58.7 all-gather.3
  71.5 141.2 all-gather.7
  214.4 88.9 all-gather.5
  454.0 134.1 reduce-scatter.1
